TPU v7x, 128 devices: a whole 4x4x4 slice. The times are simulated.
128 devices in a mesh: group: 8 (over y, core), member: 16 (over z, x).
Axes of the slice: x: 4, y: 4, z: 4, core: 2. Of those that a mesh axis runs over, the one named last changes fastest.
Arguments:
- feats: bfloat16 [96, 524288], P(None, ('group', 'member')), may hold values from -6 to 6
- kmap: int32 [27, 524288], P(None, ('group', 'member')), may hold values from 0 to 5888, as said below
- send_rows: int32 [128, 7, 256], P(('group', 'member')), may hold values from 0 to 4095
- w_sub: bfloat16 [27, 96, 96], replicated, may hold values from -0.125 to 0.125
- owner: int32 [524288, 1], P(('group', 'member')), may hold values from 0 to 127, as said below
- coarse_id: int32 [524288], P(('group', 'member')), may hold values from 0 to 511
- octant: int32 [524288], P(('group', 'member')), may hold values from 0 to 7
- w_down: bfloat16 [8, 192, 96], replicated, may hold values from -0.21875 to 0.21875
- grad_coarse: bfloat16 [192, 65536], P(None, ('group', 'member')), may hold values from -6 to 6
Outputs:
- coarse_out: bfloat16 [192, 65536], P(None, ('group', 'member'))
- grad_feats: float32 [96, 524288], P(None, ('group', 'member'))
- grad_w_sub: float32 [27, 96, 96], replicated
- grad_w_down: float32 [8, 192, 96], replicated
Inputs may be any that keep to these rules, and one draw needn't show every extreme that they name: kmap[k, v] indexes the table of v's device: below 4096 a voxel of that device, then 256 received voxels for each of the 7 levels in order, and 5888 for a missing neighbour; kmap[13, v] is v's own column. owner[v, 0] is v's own device or its partner at one of the 7 levels; among the voxels of one device at most 128 name its partner of any one level, and on every device some level's partner is named by exactly 128.
All inputs are finite; a program needn't handle non-finite values.
Results may differ from a plain program's by a relative error of at most 0.0056.
Values may be sent and summed in bfloat16 or wider, within the bound.
No kernel may reach another device: no remote copies, remote signals or barrier semaphores. Data moves between devices by JAX's collectives and lax.ppermute only.
A program may use at most 128 MiB of HBM per device.

v0:
```python
import jax
import jax.numpy as jnp
from jax import lax
from jax.sharding import PartitionSpec as P


def from_partner(value, axis, stride):
    mask = 2**stride
    pairs = [(source, source ^ mask) for source in range(lax.axis_size(axis))]
    return lax.ppermute(value, axis, pairs)


def shards(feats, kmap, send_rows, w_sub, owner, coarse_id, octant, w_down, grad_coarse):
    chans, vdev = feats.shape
    levels = send_rows.shape[1]
    hcap = send_rows.shape[2]
    n_member = lax.axis_size("member")
    bits_member = n_member.bit_length() - 1
    myself = lax.axis_index(("group", "member"))
    outgoing = send_rows[0]
    rows_in = feats.T
    pieces = [jnp.take(rows_in, outgoing[level], axis=0) for level in range(levels)]
    received = []
    for level in range(levels):
        if level < bits_member:
            received.append(from_partner(pieces[level], "member", level))
        else:
            received.append(from_partner(pieces[level], "group", level - bits_member))
    table = jnp.concatenate([rows_in] + received + [jnp.zeros((1, chans), jnp.bfloat16)], axis=0)

    def forward_step(total, inputs):
        weight, cols = inputs
        taken = jnp.take(table, cols, axis=0)
        return (total + jnp.dot(taken, weight.T, preferred_element_type=jnp.float32), None)

    pre, _ = lax.scan(forward_step, jnp.zeros((vdev, chans), jnp.float32), (w_sub, kmap))
    y1 = jax.nn.silu(pre).astype(jnp.bfloat16)
    noct = w_down.shape[0]
    coarse_dev = grad_coarse.shape[1]
    sentinel = noct * coarse_dev
    slots = vdev // 32
    differ = jnp.bitwise_xor(owner[:, 0], myself)
    code = jnp.full((vdev,), levels, jnp.int32)
    for level in range(levels):
        code = jnp.where(differ == 1 << level, level, code)
    classes = (code[None, :] == jnp.arange(levels + 1, dtype=jnp.int32)[:, None]).astype(jnp.int32)
    rank = jnp.sum(classes * (jnp.cumsum(classes, axis=1) - 1), axis=0)
    is_self = code == levels
    position = jnp.where(is_self, levels * slots, code * slots + rank)
    local_keys = octant * coarse_dev + coarse_id
    send_feat = jnp.zeros((levels * slots + 1, chans), jnp.bfloat16).at[position].set(y1)
    send_key = jnp.full((levels * slots + 1,), sentinel, jnp.int32).at[position].set(local_keys)
    got_feats = []
    got_keys = []
    for level in range(levels):
        part_feat = send_feat[level * slots : (level + 1) * slots]
        part_key = send_key[level * slots : (level + 1) * slots]
        if level < bits_member:
            came_feat, came_key = from_partner((part_feat, part_key), "member", level)
        else:
            came_feat, came_key = from_partner((part_feat, part_key), "group", level - bits_member)
        got_feats.append(came_feat)
        got_keys.append(came_key)
    self_keys = jnp.where(is_self, local_keys, sentinel)
    all_keys = jnp.concatenate([self_keys] + got_keys, axis=0)
    all_feats = jnp.concatenate([y1] + got_feats, axis=0)
    pooled = (
        jnp.zeros((sentinel + 1, chans), jnp.float32)
        .at[all_keys]
        .add(all_feats.astype(jnp.float32))
    )
    pooled = pooled[:sentinel].astype(jnp.bfloat16).reshape(noct, coarse_dev, chans)
    coarse_out = jnp.einsum(
        "oci,oni->cn", w_down, pooled, preferred_element_type=jnp.float32
    ).astype(jnp.bfloat16)
    grad_down = jnp.einsum("cn,oni->oci", grad_coarse, pooled, preferred_element_type=jnp.float32)
    coarse_rows = grad_coarse.T
    padded_grad = jnp.concatenate(
        [coarse_rows, jnp.zeros((1, coarse_rows.shape[1]), jnp.bfloat16)], axis=0
    )
    returned = []
    for level in range(levels):
        coarse_index = jnp.where(
            got_keys[level] < sentinel, got_keys[level] % coarse_dev, coarse_dev
        )
        outbound = jnp.take(padded_grad, coarse_index, axis=0)
        if level < bits_member:
            returned.append(from_partner(outbound, "member", level))
        else:
            returned.append(from_partner(outbound, "group", level - bits_member))
    parent_table = jnp.concatenate([coarse_rows] + returned, axis=0)
    parent_index = jnp.where(is_self, coarse_id, coarse_dev + position)
    parents = jnp.take(parent_table, parent_index, axis=0)
    every = jnp.einsum("oci,vc->voi", w_down, parents, preferred_element_type=jnp.float32)
    chosen = (octant[:, None] == jnp.arange(noct, dtype=jnp.int32)[None, :]).astype(jnp.float32)
    grad_y1 = jnp.sum(every * chosen[:, :, None], axis=1).astype(jnp.bfloat16)
    sig = jax.nn.sigmoid(pre)
    grad_pre = (grad_y1.astype(jnp.float32) * (sig * (1.0 + pre * (1.0 - sig)))).astype(
        jnp.bfloat16
    )

    def backward_step(grad_table, inputs):
        weight, cols = inputs
        taken = jnp.take(table, cols, axis=0)
        dweight = lax.dot_general(
            grad_pre, taken, (((0,), (0,)), ((), ())), preferred_element_type=jnp.float32
        )
        contrib = jnp.dot(grad_pre, weight, preferred_element_type=jnp.float32)
        return (grad_table.at[cols].add(contrib), dweight)

    grad_table, grad_sub = lax.scan(
        backward_step, jnp.zeros((table.shape[0], chans), jnp.float32), (w_sub, kmap)
    )
    backs = [grad_table[vdev + level * hcap : vdev + (level + 1) * hcap] for level in range(levels)]
    incoming = []
    for level in range(levels):
        if level < bits_member:
            incoming.append(
                from_partner(backs[level].astype(jnp.bfloat16), "member", level).astype(jnp.float32)
            )
        else:
            incoming.append(
                from_partner(
                    backs[level].astype(jnp.bfloat16), "group", level - bits_member
                ).astype(jnp.float32)
            )
    grad_local = grad_table[:vdev]
    for level in range(levels):
        grad_local = grad_local.at[outgoing[level]].add(incoming[level])
    sub_total, down_total = lax.psum((grad_sub, grad_down), ("group", "member"))
    return (coarse_out, grad_local.T, sub_total, down_total)


def solution(mesh):
    in_specs = (
        P(None, ("group", "member")),
        P(None, ("group", "member")),
        P(("group", "member"), None, None),
        P(),
        P(("group", "member"), None),
        P(("group", "member")),
        P(("group", "member")),
        P(),
        P(None, ("group", "member")),
    )
    out_specs = (P(None, ("group", "member")), P(None, ("group", "member")), P(), P())
    return jax.shard_map(shards, mesh=mesh, in_specs=in_specs, out_specs=out_specs, check_vma=False)
```

profile of v0, /device:TPU:0, one launch (start us, length us, event | category | flops | bytes accessed | tf_op | source)
XLA Modules:
  0.0 2139.7 jit_solution(16183327324175720473)
XLA Ops:
  138.6 437.4 %while.24 = (s32[]{:T(128)}, f32[4096,96]{0,1:T(8,128)}, s32[27,4096]{1,0:T(8,128)}, bf16[5889,96]{1,0:T(8,128)(2,1)S(1)}, bf16[27,96,96]{2,1,0:T(8,128)(2,1)}, /*index=5*/s32[]{:T(128)}, s32[]{:T(128)}) while((s32[]{:T(128)}, f32[4096,96]{0,1:T(8,128)}, s32[27,4096]{1,0:T(8,128)}, bf16[5889,96]{1,0:T(8,128)(2,1)S(1)}, ...), condition=%wide.region_5.8_spmd.clone, body=%wide.region_4.7_spmd.clone.sunk | while | flops 76718080 | bytes 5636699 | solution.py:36
  586.1 17.1 gather_fusion.2
  635.3 1296.5 %while.23 = (s32[]{:T(128)}, f32[5889,96]{1,0:T(8,128)}, f32[27,96,96]{2,1,0:T(8,128)}, s32[27,4096]{1,0:T(8,128)}, bf16[27,96,96]{2,1,0:T(8,128)(2,1)}, /*index...) while((s32[]{:T(128)}, f32[5889,96]{1,0:T(8,128)}, f32[27,96,96]{2,1,0:T(8,128)}, ...), condition=%wide.region_11.15_spmd, body=%wide.region_9.14_spmd.sunk | while | flops 151834624 | bytes 20284560 | solution.py:111
  659.4 23.9 %scatter_fusion = f32[5889,96]{1,0:T(8,128)} fusion(f32[5889,96]{1,0:T(8,128)} %get-tuple-element.322, s32[4096]{0:T(1024)S(1)} %bitcast.141, f32[4096,96]{1,0:T(8,128)} %copy.63), kind=kCustom, calls=%fused_computation.17.clone.1 | custom fusion | flops 393216 | bytes 4734976 | tf_op jit(solution)/shard_map/while/body/eval_jaxpr/scatter-add | solution.py:109
  707.4 23.9 %scatter_fusion = f32[5889,96]{1,0:T(8,128)} fusion(f32[5889,96]{1,0:T(8,128)} %get-tuple-element.322, s32[4096]{0:T(1024)S(1)} %bitcast.141, f32[4096,96]{1,0:T(8,128)} %copy.63), kind=kCustom, calls=%fused_computation.17.clone.1 | custom fusion | flops 393216 | bytes 4734976 | tf_op jit(solution)/shard_map/while/body/eval_jaxpr/scatter-add | solution.py:109
  755.4 23.9 %scatter_fusion = f32[5889,96]{1,0:T(8,128)} fusion(f32[5889,96]{1,0:T(8,128)} %get-tuple-element.322, s32[4096]{0:T(1024)S(1)} %bitcast.141, f32[4096,96]{1,0:T(8,128)} %copy.63), kind=kCustom, calls=%fused_computation.17.clone.1 | custom fusion | flops 393216 | bytes 4734976 | tf_op jit(solution)/shard_map/while/body/eval_jaxpr/scatter-add | solution.py:109
  803.5 23.9 %scatter_fusion = f32[5889,96]{1,0:T(8,128)} fusion(f32[5889,96]{1,0:T(8,128)} %get-tuple-element.322, s32[4096]{0:T(1024)S(1)} %bitcast.141, f32[4096,96]{1,0:T(8,128)} %copy.63), kind=kCustom, calls=%fused_computation.17.clone.1 | custom fusion | flops 393216 | bytes 4734976 | tf_op jit(solution)/shard_map/while/body/eval_jaxpr/scatter-add | solution.py:109
  851.5 23.9 %scatter_fusion = f32[5889,96]{1,0:T(8,128)} fusion(f32[5889,96]{1,0:T(8,128)} %get-tuple-element.322, s32[4096]{0:T(1024)S(1)} %bitcast.141, f32[4096,96]{1,0:T(8,128)} %copy.63), kind=kCustom, calls=%fused_computation.17.clone.1 | custom fusion | flops 393216 | bytes 4734976 | tf_op jit(solution)/shard_map/while/body/eval_jaxpr/scatter-add | solution.py:109
  899.5 23.9 %scatter_fusion = f32[5889,96]{1,0:T(8,128)} fusion(f32[5889,96]{1,0:T(8,128)} %get-tuple-element.322, s32[4096]{0:T(1024)S(1)} %bitcast.141, f32[4096,96]{1,0:T(8,128)} %copy.63), kind=kCustom, calls=%fused_computation.17.clone.1 | custom fusion | flops 393216 | bytes 4734976 | tf_op jit(solution)/shard_map/while/body/eval_jaxpr/scatter-add | solution.py:109
  947.5 24.0 %scatter_fusion = f32[5889,96]{1,0:T(8,128)} fusion(f32[5889,96]{1,0:T(8,128)} %get-tuple-element.322, s32[4096]{0:T(1024)S(1)} %bitcast.141, f32[4096,96]{1,0:T(8,128)} %copy.63), kind=kCustom, calls=%fused_computation.17.clone.1 | custom fusion | flops 393216 | bytes 4734976 | tf_op jit(solution)/shard_map/while/body/eval_jaxpr/scatter-add | solution.py:109
  995.5 23.9 %scatter_fusion = f32[5889,96]{1,0:T(8,128)} fusion(f32[5889,96]{1,0:T(8,128)} %get-tuple-element.322, s32[4096]{0:T(1024)S(1)} %bitcast.141, f32[4096,96]{1,0:T(8,128)} %copy.63), kind=kCustom, calls=%fused_computation.17.clone.1 | custom fusion | flops 393216 | bytes 4734976 | tf_op jit(solution)/shard_map/while/body/eval_jaxpr/scatter-add | solution.py:109
  1043.5 23.9 %scatter_fusion = f32[5889,96]{1,0:T(8,128)} fusion(f32[5889,96]{1,0:T(8,128)} %get-tuple-element.322, s32[4096]{0:T(1024)S(1)} %bitcast.141, f32[4096,96]{1,0:T(8,128)} %copy.63), kind=kCustom, calls=%fused_computation.17.clone.1 | custom fusion | flops 393216 | bytes 4734976 | tf_op jit(solution)/shard_map/while/body/eval_jaxpr/scatter-add | solution.py:109
  1091.6 23.9 %scatter_fusion = f32[5889,96]{1,0:T(8,128)} fusion(f32[5889,96]{1,0:T(8,128)} %get-tuple-element.322, s32[4096]{0:T(1024)S(1)} %bitcast.141, f32[4096,96]{1,0:T(8,128)} %copy.63), kind=kCustom, calls=%fused_computation.17.clone.1 | custom fusion | flops 393216 | bytes 4734976 | tf_op jit(solution)/shard_map/while/body/eval_jaxpr/scatter-add | solution.py:109
  1139.6 23.9 %scatter_fusion = f32[5889,96]{1,0:T(8,128)} fusion(f32[5889,96]{1,0:T(8,128)} %get-tuple-element.322, s32[4096]{0:T(1024)S(1)} %bitcast.141, f32[4096,96]{1,0:T(8,128)} %copy.63), kind=kCustom, calls=%fused_computation.17.clone.1 | custom fusion | flops 393216 | bytes 4734976 | tf_op jit(solution)/shard_map/while/body/eval_jaxpr/scatter-add | solution.py:109
  1187.6 23.9 %scatter_fusion = f32[5889,96]{1,0:T(8,128)} fusion(f32[5889,96]{1,0:T(8,128)} %get-tuple-element.322, s32[4096]{0:T(1024)S(1)} %bitcast.141, f32[4096,96]{1,0:T(8,128)} %copy.63), kind=kCustom, calls=%fused_computation.17.clone.1 | custom fusion | flops 393216 | bytes 4734976 | tf_op jit(solution)/shard_map/while/body/eval_jaxpr/scatter-add | solution.py:109
  1235.6 23.9 %scatter_fusion = f32[5889,96]{1,0:T(8,128)} fusion(f32[5889,96]{1,0:T(8,128)} %get-tuple-element.322, s32[4096]{0:T(1024)S(1)} %bitcast.141, f32[4096,96]{1,0:T(8,128)} %copy.63), kind=kCustom, calls=%fused_computation.17.clone.1 | custom fusion | flops 393216 | bytes 4734976 | tf_op jit(solution)/shard_map/while/body/eval_jaxpr/scatter-add | solution.py:109
  1283.6 23.9 %scatter_fusion = f32[5889,96]{1,0:T(8,128)} fusion(f32[5889,96]{1,0:T(8,128)} %get-tuple-element.322, s32[4096]{0:T(1024)S(1)} %bitcast.141, f32[4096,96]{1,0:T(8,128)} %copy.63), kind=kCustom, calls=%fused_computation.17.clone.1 | custom fusion | flops 393216 | bytes 4734976 | tf_op jit(solution)/shard_map/while/body/eval_jaxpr/scatter-add | solution.py:109
  1331.6 23.9 %scatter_fusion = f32[5889,96]{1,0:T(8,128)} fusion(f32[5889,96]{1,0:T(8,128)} %get-tuple-element.322, s32[4096]{0:T(1024)S(1)} %bitcast.141, f32[4096,96]{1,0:T(8,128)} %copy.63), kind=kCustom, calls=%fused_computation.17.clone.1 | custom fusion | flops 393216 | bytes 4734976 | tf_op jit(solution)/shard_map/while/body/eval_jaxpr/scatter-add | solution.py:109
  1379.7 23.9 %scatter_fusion = f32[5889,96]{1,0:T(8,128)} fusion(f32[5889,96]{1,0:T(8,128)} %get-tuple-element.322, s32[4096]{0:T(1024)S(1)} %bitcast.141, f32[4096,96]{1,0:T(8,128)} %copy.63), kind=kCustom, calls=%fused_computation.17.clone.1 | custom fusion | flops 393216 | bytes 4734976 | tf_op jit(solution)/shard_map/while/body/eval_jaxpr/scatter-add | solution.py:109
  1427.7 23.9 %scatter_fusion = f32[5889,96]{1,0:T(8,128)} fusion(f32[5889,96]{1,0:T(8,128)} %get-tuple-element.322, s32[4096]{0:T(1024)S(1)} %bitcast.141, f32[4096,96]{1,0:T(8,128)} %copy.63), kind=kCustom, calls=%fused_computation.17.clone.1 | custom fusion | flops 393216 | bytes 4734976 | tf_op jit(solution)/shard_map/while/body/eval_jaxpr/scatter-add | solution.py:109
  1475.7 24.0 %scatter_fusion = f32[5889,96]{1,0:T(8,128)} fusion(f32[5889,96]{1,0:T(8,128)} %get-tuple-element.322, s32[4096]{0:T(1024)S(1)} %bitcast.141, f32[4096,96]{1,0:T(8,128)} %copy.63), kind=kCustom, calls=%fused_computation.17.clone.1 | custom fusion | flops 393216 | bytes 4734976 | tf_op jit(solution)/shard_map/while/body/eval_jaxpr/scatter-add | solution.py:109
  1523.7 24.0 %scatter_fusion = f32[5889,96]{1,0:T(8,128)} fusion(f32[5889,96]{1,0:T(8,128)} %get-tuple-element.322, s32[4096]{0:T(1024)S(1)} %bitcast.141, f32[4096,96]{1,0:T(8,128)} %copy.63), kind=kCustom, calls=%fused_computation.17.clone.1 | custom fusion | flops 393216 | bytes 4734976 | tf_op jit(solution)/shard_map/while/body/eval_jaxpr/scatter-add | solution.py:109
  1571.7 23.9 %scatter_fusion = f32[5889,96]{1,0:T(8,128)} fusion(f32[5889,96]{1,0:T(8,128)} %get-tuple-element.322, s32[4096]{0:T(1024)S(1)} %bitcast.141, f32[4096,96]{1,0:T(8,128)} %copy.63), kind=kCustom, calls=%fused_computation.17.clone.1 | custom fusion | flops 393216 | bytes 4734976 | tf_op jit(solution)/shard_map/while/body/eval_jaxpr/scatter-add | solution.py:109
  1619.8 24.0 %scatter_fusion = f32[5889,96]{1,0:T(8,128)} fusion(f32[5889,96]{1,0:T(8,128)} %get-tuple-element.322, s32[4096]{0:T(1024)S(1)} %bitcast.141, f32[4096,96]{1,0:T(8,128)} %copy.63), kind=kCustom, calls=%fused_computation.17.clone.1 | custom fusion | flops 393216 | bytes 4734976 | tf_op jit(solution)/shard_map/while/body/eval_jaxpr/scatter-add | solution.py:109
  1667.8 23.9 %scatter_fusion = f32[5889,96]{1,0:T(8,128)} fusion(f32[5889,96]{1,0:T(8,128)} %get-tuple-element.322, s32[4096]{0:T(1024)S(1)} %bitcast.141, f32[4096,96]{1,0:T(8,128)} %copy.63), kind=kCustom, calls=%fused_computation.17.clone.1 | custom fusion | flops 393216 | bytes 4734976 | tf_op jit(solution)/shard_map/while/body/eval_jaxpr/scatter-add | solution.py:109
  1715.8 24.0 %scatter_fusion = f32[5889,96]{1,0:T(8,128)} fusion(f32[5889,96]{1,0:T(8,128)} %get-tuple-element.322, s32[4096]{0:T(1024)S(1)} %bitcast.141, f32[4096,96]{1,0:T(8,128)} %copy.63), kind=kCustom, calls=%fused_computation.17.clone.1 | custom fusion | flops 393216 | bytes 4734976 | tf_op jit(solution)/shard_map/while/body/eval_jaxpr/scatter-add | solution.py:109
  1763.8 23.9 %scatter_fusion = f32[5889,96]{1,0:T(8,128)} fusion(f32[5889,96]{1,0:T(8,128)} %get-tuple-element.322, s32[4096]{0:T(1024)S(1)} %bitcast.141, f32[4096,96]{1,0:T(8,128)} %copy.63), kind=kCustom, calls=%fused_computation.17.clone.1 | custom fusion | flops 393216 | bytes 4734976 | tf_op jit(solution)/shard_map/while/body/eval_jaxpr/scatter-add | solution.py:109
  1811.8 23.9 %scatter_fusion = f32[5889,96]{1,0:T(8,128)} fusion(f32[5889,96]{1,0:T(8,128)} %get-tuple-element.322, s32[4096]{0:T(1024)S(1)} %bitcast.141, f32[4096,96]{1,0:T(8,128)} %copy.63), kind=kCustom, calls=%fused_computation.17.clone.1 | custom fusion | flops 393216 | bytes 4734976 | tf_op jit(solution)/shard_map/while/body/eval_jaxpr/scatter-add | solution.py:109
  1859.9 23.9 %scatter_fusion = f32[5889,96]{1,0:T(8,128)} fusion(f32[5889,96]{1,0:T(8,128)} %get-tuple-element.322, s32[4096]{0:T(1024)S(1)} %bitcast.141, f32[4096,96]{1,0:T(8,128)} %copy.63), kind=kCustom, calls=%fused_computation.17.clone.1 | custom fusion | flops 393216 | bytes 4734976 | tf_op jit(solution)/shard_map/while/body/eval_jaxpr/scatter-add | solution.py:109
  1907.9 23.9 %scatter_fusion = f32[5889,96]{1,0:T(8,128)} fusion(f32[5889,96]{1,0:T(8,128)} %get-tuple-element.322, s32[4096]{0:T(1024)S(1)} %bitcast.141, f32[4096,96]{1,0:T(8,128)} %copy.63), kind=kCustom, calls=%fused_computation.17.clone.1 | custom fusion | flops 393216 | bytes 4734976 | tf_op jit(solution)/shard_map/while/body/eval_jaxpr/scatter-add | solution.py:109
  1946.3 29.7 %scatter_custom_fusion.3 = f32[4097,96]{1,0:T(8,128)} fusion(s32[4992]{0:T(1024)} %fusion.43, f32[4992,96]{1,0:T(8,128)} %copy.40, f32[]{:T(128)} %constant.109.clone.1), kind=kCustom, calls=%fused_computation.67 | custom fusion | flops 479232 | bytes 1573760 | tf_op jit(solution)/shard_map/scatter-add | solution.py:70
  2033.7 95.5 %all-reduce.4.cloned.1.call-done = (f32[27,96,96]{2,1,0:T(8,128)}, f32[8,192,96]{1,2,0:T(8,128)}) async-done(((f32[27,96,96]{2,1,0:T(8,128)}, f32[8,192,96]{1,2,0:T(8,128)}), (f32[27,96,96]{2,1,0:T(8,128)}, f32[8,192,96]{1,2,0:T(8,128)})) %all-reduce.4.cloned.1.call-update) | async-done | bytes 1585168 | tf_op jit(solution)/shard_map/psum | solution.py:130
  (738 shorter events, 1334.1 us)
Async XLA Ops:
  7.2 2122.0 %all-reduce.4.cloned.1.call-start = ((), (), s32[]{:S(2)}) async-start(), calls=%async_computation | async-start | bytes 4227072 | tf_op jit(solution)/shard_map/psum | solution.py:130
  28.6 43.7 %collective-permute-start.2 = (s32[128]{0:T(128)}, s32[128]{0:T(128)}, u32[]{:S(2)}, u32[]{:S(2)}) collective-permute-start(s32[128]{0:T(128)} %get-tuple-element.197), channel_id=1, source_target_pairs={{0,4},{1,5},{2,6},{3,7},{4,0},{5,1},{6,2},{7,3},{8,12},{9,13},{10,... | collective-permute-start | bytes 1544 | tf_op jit(solution)/shard_map/ppermute | solution.py:10
  30.6 46.1 %collective-permute-start.1 = (s32[128]{0:T(128)}, s32[128]{0:T(128)}, u32[]{:S(2)}, u32[]{:S(2)}) collective-permute-start(s32[128]{0:T(128)} %get-tuple-element.198), channel_id=1, source_target_pairs={{0,2},{1,3},{2,0},{3,1},{4,6},{5,7},{6,4},{7,5},{8,10},{9,11},{10,... | collective-permute-start | bytes 1544 | tf_op jit(solution)/shard_map/ppermute | solution.py:10
  33.6 45.0 %collective-permute-start = (s32[128]{0:T(128)}, s32[128]{0:T(128)}, u32[]{:S(2)}, u32[]{:S(2)}) collective-permute-start(s32[128]{0:T(128)} %get-tuple-element.199), channel_id=1, source_target_pairs={{0,1},{1,0},{2,3},{3,2},{4,5},{5,4},{6,7},{7,6},{8,9},{9,8},{10,11... | collective-permute-start | bytes 1544 | tf_op jit(solution)/shard_map/ppermute | solution.py:10
  34.2 47.6 %collective-permute-start.4 = (s32[128]{0:T(128)}, s32[128]{0:T(128)}, u32[]{:S(2)}, u32[]{:S(2)}) collective-permute-start(s32[128]{0:T(128)} %get-tuple-element.195), channel_id=1, source_target_pairs={{0,16},{16,0},{32,48},{48,32},{64,80},{80,64},{96,112},{112,96},{1... | collective-permute-start | bytes 1544 | tf_op jit(solution)/shard_map/ppermute | solution.py:10
  34.2 50.5 %collective-permute-start.3 = (s32[128]{0:T(128)}, s32[128]{0:T(128)}, u32[]{:S(2)}, u32[]{:S(2)}) collective-permute-start(s32[128]{0:T(128)} %get-tuple-element.196), channel_id=1, source_target_pairs={{0,8},{1,9},{2,10},{3,11},{4,12},{5,13},{6,14},{7,15},{8,0},{9,1},... | collective-permute-start | bytes 1544 | tf_op jit(solution)/shard_map/ppermute | solution.py:10
  72.3 14.3 collective-permute-start.6
  76.7 19.1 collective-permute-start.5
  78.6 38.6 %collective-permute-start.7 = (bf16[256,96]{1,0:T(8,128)(2,1)}, bf16[256,96]{1,0:T(8,128)(2,1)}, u32[]{:S(2)}, u32[]{:S(2)}) collective-permute-start(bf16[256,96]{1,0:T(8,128)(2,1)} %broadcast_select_fusion.13), channel_id=1, source_target_pairs={{0,1},{1,0},{2,3},{3,2},{4,5},{5,4},{6,7},{7,6},{8,9},{9,8},{10,11... | collective-permute-start | bytes 147464 | tf_op jit(solution)/shard_map/ppermute | solution.py:10
  81.8 37.7 %collective-permute-start.8 = (bf16[256,96]{1,0:T(8,128)(2,1)}, bf16[256,96]{1,0:T(8,128)(2,1)}, u32[]{:S(2)}, u32[]{:S(2)}) collective-permute-start(bf16[256,96]{1,0:T(8,128)(2,1)} %broadcast_select_fusion.12), channel_id=1, source_target_pairs={{0,2},{1,3},{2,0},{3,1},{4,6},{5,7},{6,4},{7,5},{8,10},{9,11},{10,... | collective-permute-start | bytes 147464 | tf_op jit(solution)/shard_map/ppermute | solution.py:10
  84.8 39.1 %collective-permute-start.9 = (bf16[256,96]{1,0:T(8,128)(2,1)}, bf16[256,96]{1,0:T(8,128)(2,1)}, u32[]{:S(2)}, u32[]{:S(2)}) collective-permute-start(bf16[256,96]{1,0:T(8,128)(2,1)} %broadcast_select_fusion.11), channel_id=1, source_target_pairs={{0,4},{1,5},{2,6},{3,7},{4,0},{5,1},{6,2},{7,3},{8,12},{9,13},{10,... | collective-permute-start | bytes 147464 | tf_op jit(solution)/shard_map/ppermute | solution.py:10
  86.6 38.8 %collective-permute-start.10 = (bf16[256,96]{1,0:T(8,128)(2,1)}, bf16[256,96]{1,0:T(8,128)(2,1)}, u32[]{:S(2)}, u32[]{:S(2)}) collective-permute-start(bf16[256,96]{1,0:T(8,128)(2,1)} %broadcast_select_fusion.10), channel_id=1, source_target_pairs={{0,8},{1,9},{2,10},{3,11},{4,12},{5,13},{6,14},{7,15},{8,0},{9,1},... | collective-permute-start | bytes 147464 | tf_op jit(solution)/shard_map/ppermute | solution.py:10
  95.8 32.4 %collective-permute-start.11 = (bf16[256,96]{1,0:T(8,128)(2,1)}, bf16[256,96]{1,0:T(8,128)(2,1)}, u32[]{:S(2)}, u32[]{:S(2)}) collective-permute-start(bf16[256,96]{1,0:T(8,128)(2,1)} %broadcast_select_fusion.9), channel_id=1, source_target_pairs={{0,16},{16,0},{32,48},{48,32},{64,80},{80,64},{96,112},{112,96},{1... | collective-permute-start | bytes 147464 | tf_op jit(solution)/shard_map/ppermute | solution.py:10
  117.3 15.5 collective-permute-start.12
  119.5 460.9 %collective-permute-start.22 = (bf16[128,192]{1,0:T(8,128)(2,1)}, bf16[128,192]{1,0:T(8,128)(2,1)}, u32[]{:S(2)}, u32[]{:S(2)}) collective-permute-start(bf16[128,192]{1,0:T(8,128)(2,1)} %broadcast_select_fusion.5), channel_id=1, source_target_pairs={{0,2},{1,3},{2,0},{3,1},{4,6},{5,7},{6,4},{7,5},{8,10},{9,11},{10,... | collective-permute-start | bytes 147464 | tf_op jit(solution)/shard_map/ppermute | solution.py:10
  123.8 455.0 %collective-permute-start.21 = (bf16[128,192]{1,0:T(8,128)(2,1)}, bf16[128,192]{1,0:T(8,128)(2,1)}, u32[]{:S(2)}, u32[]{:S(2)}) collective-permute-start(bf16[128,192]{1,0:T(8,128)(2,1)} %broadcast_select_fusion.6), channel_id=1, source_target_pairs={{0,1},{1,0},{2,3},{3,2},{4,5},{5,4},{6,7},{7,6},{8,9},{9,8},{10,11... | collective-permute-start | bytes 147464 | tf_op jit(solution)/shard_map/ppermute | solution.py:10
  125.4 457.7 %collective-permute-start.23 = (bf16[128,192]{1,0:T(8,128)(2,1)}, bf16[128,192]{1,0:T(8,128)(2,1)}, u32[]{:S(2)}, u32[]{:S(2)}) collective-permute-start(bf16[128,192]{1,0:T(8,128)(2,1)} %broadcast_select_fusion.4), channel_id=1, source_target_pairs={{0,4},{1,5},{2,6},{3,7},{4,0},{5,1},{6,2},{7,3},{8,12},{9,13},{10,... | collective-permute-start | bytes 147464 | tf_op jit(solution)/shard_map/ppermute | solution.py:10
  128.2 455.6 %collective-permute-start.24 = (bf16[128,192]{1,0:T(8,128)(2,1)}, bf16[128,192]{1,0:T(8,128)(2,1)}, u32[]{:S(2)}, u32[]{:S(2)}) collective-permute-start(bf16[128,192]{1,0:T(8,128)(2,1)} %broadcast_select_fusion.3), channel_id=1, source_target_pairs={{0,8},{1,9},{2,10},{3,11},{4,12},{5,13},{6,14},{7,15},{8,0},{9,1},... | collective-permute-start | bytes 147464 | tf_op jit(solution)/shard_map/ppermute | solution.py:10
  138.6 446.1 %collective-permute-start.25 = (bf16[128,192]{1,0:T(8,128)(2,1)S(1)}, bf16[128,192]{1,0:T(8,128)(2,1)}, u32[]{:S(2)}, u32[]{:S(2)}) collective-permute-start(bf16[128,192]{1,0:T(8,128)(2,1)S(1)} %broadcast_select_fusion.2), channel_id=1, source_target_pairs={{0,16},{16,0},{32,48},{48,32},{64,80},{80,64},{96,112},{112,96},{1... | collective-permute-start | bytes 147464 | tf_op jit(solution)/shard_map/ppermute | solution.py:10
  578.8 6.7 collective-permute-start.26
  631.9 1301.2 %collective-permute-start.14 = (bf16[128,96]{1,0:T(8,128)(2,1)S(1)}, bf16[128,96]{1,0:T(8,128)(2,1)S(1)}, u32[]{:S(2)}, u32[]{:S(2)}) collective-permute-start(bf16[128,96]{1,0:T(8,128)(2,1)S(1)} %get-tuple-element.178), channel_id=1, source_target_pairs={{0,1},{1,0},{2,3},{3,2},{4,5},{5,4},{6,7},{7,6},{8,9},{9,8},{10,11... | collective-permute-start | bytes 73736 | tf_op jit(solution)/shard_map/ppermute | solution.py:10
  1932.4 7.4 collective-permute-start.16
  1932.4 8.1 collective-permute-start.17
  1933.1 8.2 collective-permute-start.18
  1933.1 8.9 collective-permute-start.19
  1981.2 12.2 collective-permute-start.28
  1982.1 11.8 collective-permute-start.29
  1987.4 19.9 collective-permute-start.30
  1988.3 23.7 %collective-permute-start.31 = (bf16[256,96]{1,0:T(8,128)(2,1)S(1)}, bf16[256,96]{1,0:T(8,128)(2,1)S(1)}, u32[]{:S(2)}, u32[]{:S(2)}) collective-permute-start(bf16[256,96]{1,0:T(8,128)(2,1)S(1)} %get-tuple-element.168), channel_id=1, source_target_pairs={{0,8},{1,9},{2,10},{3,11},{4,12},{5,13},{6,14},{7,15},{8,0},{9,1},... | collective-permute-start | bytes 147464 | tf_op jit(solution)/shard_map/ppermute | solution.py:10
  1992.7 24.0 %collective-permute-start.32 = (bf16[256,96]{1,0:T(8,128)(2,1)S(1)}, bf16[256,96]{1,0:T(8,128)(2,1)S(1)}, u32[]{:S(2)}, u32[]{:S(2)}) collective-permute-start(bf16[256,96]{1,0:T(8,128)(2,1)S(1)} %get-tuple-element.167), channel_id=1, source_target_pairs={{0,16},{16,0},{32,48},{48,32},{64,80},{80,64},{96,112},{112,96},{1... | collective-permute-start | bytes 147464 | tf_op jit(solution)/shard_map/ppermute | solution.py:10
  1993.5 28.0 %collective-permute-start.33 = (bf16[256,96]{1,0:T(8,128)(2,1)S(1)}, bf16[256,96]{1,0:T(8,128)(2,1)S(1)}, u32[]{:S(2)}, u32[]{:S(2)}) collective-permute-start(bf16[256,96]{1,0:T(8,128)(2,1)S(1)} %get-tuple-element.166), channel_id=1, source_target_pairs={{0,32},{16,48},{32,0},{48,16},{64,96},{80,112},{96,64},{112,80},{1... | collective-permute-start | bytes 147464 | tf_op jit(solution)/shard_map/ppermute | solution.py:10
  1994.0 32.2 %collective-permute-start.34 = (bf16[256,96]{1,0:T(8,128)(2,1)S(1)}, bf16[256,96]{1,0:T(8,128)(2,1)S(1)}, u32[]{:S(2)}, u32[]{:S(2)}) collective-permute-start(bf16[256,96]{1,0:T(8,128)(2,1)S(1)} %get-tuple-element.165), channel_id=1, source_target_pairs={{0,64},{16,80},{32,96},{48,112},{64,0},{80,16},{96,32},{112,48},{1... | collective-permute-start | bytes 147464 | tf_op jit(solution)/shard_map/ppermute | solution.py:10
  (75 other events, 1299.1 us)
Sparse Core Ops, SparseCore 0:
  1979.2 149.8 all-reduce.3
where the time goes:
time: 2160 us; the launch traced here: 2140 us
  local copies, waits for them, and re-layouts  932 us (43%)
  other arithmetic  798 us (37%)
  matrix products  242 us (11%)
  waiting for transfers between devices  103 us (5%)
  starting transfers between devices  47.5 us (2%)
    scatter-add x27, other arithmetic, backward_step(): return (grad_table.at[cols].add(contrib), dweight)  647 us
    gather x27, local copies, waits for them, and re-layouts, backward_step(): taken = jnp.take(table, cols, axis=0)  403 us
    gather x27, local copies, waits for them, and re-layouts, forward_step(): taken = jnp.take(table, cols, axis=0)  327 us
    dot_general x27, matrix products, backward_step(): lax.dot_general(grad_pre, taken, (((0,), (0,)), ((), ())), preferred_elem...  102 us
    psum x1, waiting for transfers between devices, shards(): sub_total, down_total = lax.psum((grad_sub, grad_down), ('group', 'member'))  95.5 us
    dot_general x27, matrix products, forward_step(): jnp.dot(taken, weight.T, preferred_element_type=jnp.float32)  83.8 us
    dot_general x27, local copies, waits for them, and re-layouts, backward_step(): contrib = jnp.dot(grad_pre, weight, preferred_element_type=jnp.float32)  49.2 us
    ppermute x35, starting transfers between devices, from_partner(): return lax.ppermute(value, axis, pairs)  47.5 us
  transfers between devices with their start and end apart: 36, of which 4 were waited for; matrix products, arithmetic and copies ran while one was open for 87% of the time, Pallas kernels for 0%

commit v1 on v0

v1 whole, which is shorter than its diff:
```python
import functools

import jax
import jax.numpy as jnp
from jax import lax
from jax.experimental import pallas as pl
from jax.experimental.pallas import tpu as pltpu
from jax.sharding import PartitionSpec as P

LANES = 128
SUB = 8
DIGIT = 64
SMEM = pltpu.SMEM
F32 = jnp.float32
BF16 = jnp.bfloat16
I32 = jnp.int32


def from_partner(value, level, bits_member):
    axis, stride = ("member", level) if level < bits_member else ("group", level - bits_member)
    mask = 2**stride
    pairs = [(source, source ^ mask) for source in range(lax.axis_size(axis))]
    return lax.ppermute(value, axis, pairs)


def vmem_full(shape):
    return pl.BlockSpec(shape, lambda *_: (0,) * len(shape))


def smem_full(shape):
    return pl.BlockSpec(shape, lambda *_: (0,) * len(shape), memory_space=SMEM)


def copy_rows(count, unroll, index, source, target):
    def body(step, _):
        base = pl.multiple_of(step * unroll, unroll)
        for j in range(unroll):
            target[pl.ds(base + j, 1), :] = source[pl.ds(index(base + j), 1), :]
        return 0

    lax.fori_loop(0, count // unroll, body, 0)


def add_rows(count, unroll, index, source, tables):
    lanes = len(tables)

    def body(step, _):
        base = pl.multiple_of(step * unroll, unroll)
        for start in range(0, unroll, lanes):
            spots = [index(base + start + j) for j in range(lanes)]
            sums = [
                tables[j][pl.ds(spots[j], 1), :] + source[pl.ds(base + start + j, 1), :]
                for j in range(lanes)
            ]
            for j in range(lanes):
                tables[j][pl.ds(spots[j], 1), :] = sums[j]
        return 0

    lax.fori_loop(0, count // unroll, body, 0)


def prepare_kernel(levels, me_ref, rows_ref, owner_ref, coarse_ref, octant_ref, feats_ref, *refs, coarse_dev, slots):
    messages = refs[:levels]
    table_ref, pos_ref, parent_ref, self_ref, buf = refs[levels:]
    chans, vdev = feats_ref.shape
    halo = rows_ref.shape[1] // levels
    noct_keys = 8 * coarse_dev
    fill = jnp.zeros((LANES - chans, LANES), F32)
    for c in range(vdev // LANES):
        cols = pl.ds(c * LANES, LANES)
        block = jnp.concatenate([feats_ref[:, cols].astype(F32), fill], axis=0)
        table_ref[cols, :] = block.T
    copy_rows(levels * halo, 64, lambda r: rows_ref[0, r], table_ref, buf)

    differ = jnp.bitwise_xor(owner_ref[...], me_ref[0])
    level_id = lax.broadcasted_iota(I32, (SUB, LANES), 0)
    bit = jnp.where(level_id < levels, jnp.left_shift(jnp.ones_like(level_id), level_id), 0)
    chunks = vdev // LANES
    classes = []
    for c in range(chunks):
        part = jnp.broadcast_to(differ[:, c * LANES : (c + 1) * LANES], (SUB, LANES))
        classes.append(jnp.where((part == bit) & (level_id < levels), 1.0, 0.0).astype(F32))
    upper = lax.broadcasted_iota(I32, (LANES, LANES), 0) <= lax.broadcasted_iota(I32, (LANES, LANES), 1)
    prefix = jnp.dot(
        jnp.concatenate(classes, axis=0).astype(BF16),
        jnp.where(upper, 1.0, 0.0).astype(BF16),
        preferred_element_type=F32,
    )
    carry = jnp.zeros((SUB, 1), F32)
    start = (level_id * slots).astype(F32)
    digit_rows = []
    digit_id = lax.broadcasted_iota(I32, (SUB, LANES), 0)
    for c in range(chunks):
        cols = pl.ds(c * LANES, LANES)
        inclusive = prefix[c * SUB : (c + 1) * SUB]
        spot = classes[c] * (start + inclusive - 1.0 + carry)
        carry = carry + inclusive[:, LANES - 1 :]
        remote = jnp.sum(classes[c], axis=0, keepdims=True) > 0.5
        position = jnp.where(remote, jnp.sum(spot, axis=0, keepdims=True).astype(I32), levels * slots)
        keys = octant_ref[:, cols] * coarse_dev + coarse_ref[:, cols]
        pos_ref[:, cols] = position
        parent_ref[:, cols] = jnp.where(remote, noct_keys + position, keys)
        self_ref[:, cols] = jnp.where(remote, noct_keys, keys)
        high = jnp.broadcast_to(lax.shift_right_logical(keys, 6) - DIGIT, (SUB, LANES))
        low = jnp.broadcast_to(keys & (DIGIT - 1), (SUB, LANES))
        digits = jnp.where(digit_id == 0, high, jnp.where(digit_id == 1, low, 0))
        digit_rows.append(digits.astype(F32).astype(BF16))
    digits = jnp.concatenate(digit_rows, axis=1)
    slot_id = lax.broadcasted_iota(I32, (slots, LANES), 0)
    for level in range(levels):
        hot = []
        for c in range(chunks):
            position = jnp.broadcast_to(pos_ref[:, pl.ds(c * LANES, LANES)], (slots, LANES))
            hot.append(jnp.where(position == slot_id + level * slots, 1.0, 0.0).astype(BF16))
        found = lax.dot_general(
            digits, jnp.concatenate(hot, axis=1), (((1,), (1,)), ((), ())), preferred_element_type=F32
        )
        found = found + jnp.where(digit_id == 0, float(DIGIT), 0.0)
        messages[level][pl.ds(0, halo), :] = buf[pl.ds(level * halo, halo), :].astype(BF16)
        messages[level][pl.ds(halo, 2 * SUB), :] = jnp.concatenate(
            [found, jnp.zeros((SUB, LANES), F32)], axis=0
        ).astype(BF16)


def parents_kernel(levels, keys_ref, coarse_ref, weight_ref, *refs):
    outs = refs[:levels]
    table_ref, wide, buf = refs[levels:]
    noct = weight_ref.shape[0]
    ndev = coarse_ref.shape[0]
    slots = outs[0].shape[0]
    for o in range(noct):
        grad = jnp.dot(coarse_ref[...], weight_ref[o], preferred_element_type=F32)
        grad = grad.astype(BF16).astype(F32)
        table_ref[pl.ds(o * ndev, ndev), :] = grad
        wide[pl.ds(o * ndev, ndev), :] = grad
    wide[pl.ds(noct * ndev, SUB), :] = jnp.zeros((SUB, LANES), F32)
    copy_rows(levels * slots, 64, lambda r: keys_ref[0, r], wide, buf)
    for level in range(levels):
        outs[level][...] = buf[pl.ds(level * slots, slots), :].astype(BF16)


def gather_kernel(levels, halo, index_ref, local_ref, *refs):
    received = refs[:levels]
    out_ref, table, buf = refs[levels:]
    vdev = local_ref.shape[0]

    @pl.when(pl.program_id(0) == 0)
    def _():
        table[pl.ds(0, vdev), :] = local_ref[...]
        for level in range(levels):
            table[pl.ds(vdev + level * halo, halo), :] = received[level][pl.ds(0, halo), :].astype(F32)
        table[pl.ds(vdev + levels * halo, SUB), :] = jnp.zeros((SUB, LANES), F32)

    chunk = buf.shape[0]

    def body(step, _):
        base = pl.multiple_of(step * chunk, chunk)
        for j in range(chunk):
            buf[pl.ds(j, 1), :] = table[pl.ds(index_ref[0, 0, base + j], 1), :]
        out_ref[pl.ds(base, chunk), :] = buf[...].astype(BF16)
        return 0

    lax.fori_loop(0, vdev // chunk, body, 0)


def middle_kernel(levels, parent_ref, pos_ref, self_ref, pre_ref, table_ref, *refs, tables):
    returned = refs[:levels]
    grad_ref, pool_ref = refs[levels : levels + 2]
    sends = refs[levels + 2 : 2 * levels + 2]
    wide, rows, act, out = refs[2 * levels + 2 : 2 * levels + 6]
    pools = refs[2 * levels + 6 :]
    vdev = pre_ref.shape[0]
    keys = table_ref.shape[0]
    slots = returned[0].shape[0]
    wide[pl.ds(0, keys), :] = table_ref[...]
    for level in range(levels):
        wide[pl.ds(keys + level * slots, slots), :] = returned[level][...].astype(F32)
    copy_rows(vdev, 64, lambda r: parent_ref[0, r], wide, rows)

    def point(step, _):
        part = pl.ds(pl.multiple_of(step * 256, 256), 256)
        pre = pre_ref[part, :]
        sig = 1.0 / (1.0 + jnp.exp(-pre))
        act[part, :] = (pre * sig).astype(BF16).astype(F32)
        grad_ref[part, :] = (rows[part, :] * (sig * (1.0 + pre * (1.0 - sig)))).astype(BF16)
        return 0

    lax.fori_loop(0, vdev // 256, point, 0)

    def send(step, _):
        base = pl.multiple_of(step * 64, 64)
        for j in range(64):
            out[pl.ds(pos_ref[0, base + j], 1), :] = act[pl.ds(base + j, 1), :]
        return 0

    out[...] = jnp.zeros_like(out)
    lax.fori_loop(0, vdev // 64, send, 0)
    for level in range(levels):
        sends[level][...] = out[pl.ds(level * slots, slots), :].astype(BF16)
    for pool in pools:
        pool[...] = jnp.zeros_like(pool)
    add_rows(vdev, 64, lambda r: self_ref[0, r], act, pools)
    total = pools[0][pl.ds(0, keys), :]
    for pool in pools[1:]:
        total = total + pool[pl.ds(0, keys), :]
    pool_ref[...] = total


def pool_kernel(levels, keys_ref, pool_ref, grad_ref, weight_ref, *refs):
    received = refs[:levels]
    coarse_ref, down_ref, rows = refs[levels : levels + 3]
    pools = refs[levels + 3 :]
    slots = received[0].shape[0]
    noct, _, chans = down_ref.shape
    ndev = grad_ref.shape[1]
    for level in range(levels):
        rows[pl.ds(level * slots, slots), :] = received[level][...].astype(F32)
    for pool in pools:
        pool[...] = jnp.zeros_like(pool)
    add_rows(levels * slots, 64, lambda r: keys_ref[0, r], rows, pools)
    coarse = jnp.zeros(coarse_ref.shape, F32)
    for o in range(noct):
        part = pl.ds(o * ndev, ndev)
        total = pool_ref[part, :]
        for pool in pools:
            total = total + pool[part, :]
        pooled = total.astype(BF16)
        coarse = coarse + lax.dot_general(
            weight_ref[o], pooled, (((1,), (1,)), ((), ())), preferred_element_type=F32
        )
        down = jnp.dot(grad_ref[...], pooled, preferred_element_type=F32)
        down_ref[o] = down[:, :chans]
    coarse_ref[...] = coarse.astype(BF16)


def scatter_kernel(levels, halo, index_ref, terms_ref, local_ref, *refs):
    backs = refs[:levels]
    tables = refs[levels:]
    vdev = local_ref.shape[0]

    @pl.when(pl.program_id(0) == 0)
    def _():
        for table in tables:
            table[...] = jnp.zeros_like(table)

    add_rows(vdev, 64, lambda r: index_ref[0, 0, r], terms_ref, tables)

    @pl.when(pl.program_id(0) == pl.num_programs(0) - 1)
    def _():
        def total(part):
            result = tables[0][part, :]
            for table in tables[1:]:
                result = result + table[part, :]
            return result

        local_ref[...] = total(pl.ds(0, vdev))
        for level in range(levels):
            backs[level][...] = total(pl.ds(vdev + level * halo, halo)).astype(BF16)


def finish_kernel(levels, rows_ref, local_ref, *refs):
    incoming = refs[:levels]
    out_ref, rows = refs[levels : levels + 2]
    tables = refs[levels + 2 :]
    halo = incoming[0].shape[0]
    chans, vdev = out_ref.shape
    for level in range(levels):
        rows[pl.ds(level * halo, halo), :] = incoming[level][...].astype(F32)
    for table in tables:
        table[...] = jnp.zeros_like(table)
    add_rows(levels * halo, 64, lambda r: rows_ref[0, r], rows, tables)
    for c in range(vdev // LANES):
        part = pl.ds(c * LANES, LANES)
        total = local_ref[part, :]
        for table in tables:
            total = total + table[part, :]
        out_ref[:, part] = total.T[:chans]


def shape(dims, dtype):
    return jax.ShapeDtypeStruct(dims, dtype)


def params():
    return pltpu.CompilerParams(vmem_limit_bytes=56 << 20)


def shards(feats, kmap, send_rows, w_sub, owner, coarse_id, octant, w_down, grad_coarse):
    chans, vdev = feats.shape
    _, levels, halo = send_rows.shape
    kvol = kmap.shape[0]
    noct, c2, _ = w_down.shape
    coarse_dev = grad_coarse.shape[1]
    keys = noct * coarse_dev
    slots = vdev // 32
    bits_member = lax.axis_size("member").bit_length() - 1
    myself = lax.axis_index(("group", "member")).astype(I32).reshape(1)
    lane_pad = LANES - chans
    outgoing = send_rows.reshape(1, levels * halo)
    table_rows = vdev + levels * halo + SUB
    index = kmap.reshape(kvol, 1, vdev)

    w_pad = jnp.pad(w_sub, ((0, 0), (0, lane_pad), (0, lane_pad)))
    w_forward = w_pad.transpose(0, 2, 1).reshape(kvol * LANES, LANES)
    w_backward = w_pad.transpose(1, 0, 2).reshape(LANES, kvol * LANES)
    down_pad = jnp.pad(w_down, ((0, 0), (0, 0), (0, lane_pad)))

    prepared = pl.pallas_call(
        functools.partial(prepare_kernel, levels, coarse_dev=coarse_dev, slots=slots),
        in_specs=[pl.BlockSpec(memory_space=SMEM), smem_full((1, levels * halo))]
        + [vmem_full((1, vdev))] * 3
        + [vmem_full((chans, vdev))],
        out_specs=[vmem_full((halo + 2 * SUB, LANES))] * levels
        + [vmem_full((vdev, LANES))]
        + [vmem_full((1, vdev))] * 3,
        out_shape=[shape((halo + 2 * SUB, LANES), BF16)] * levels
        + [shape((vdev, LANES), F32)]
        + [shape((1, vdev), I32)] * 3,
        scratch_shapes=[pltpu.VMEM((levels * halo, LANES), F32)],
        compiler_params=params(),
        name="prepare",
    )(myself, outgoing, owner.reshape(1, vdev), coarse_id.reshape(1, vdev), octant.reshape(1, vdev), feats)
    messages = prepared[:levels]
    table, position, parent, own_key = prepared[levels:]
    received = [from_partner(messages[level], level, bits_member) for level in range(levels)]

    digits = jnp.stack([got[halo : halo + 2] for got in received]).astype(F32)
    got_keys = (digits[:, 0] * DIGIT + digits[:, 1]).astype(I32).reshape(1, levels * slots)

    grads = pl.pallas_call(
        functools.partial(parents_kernel, levels),
        in_specs=[smem_full((1, levels * slots)), vmem_full((coarse_dev, c2)), vmem_full((noct, c2, LANES))],
        out_specs=[vmem_full((slots, LANES))] * levels + [vmem_full((keys, LANES))],
        out_shape=[shape((slots, LANES), BF16)] * levels + [shape((keys, LANES), F32)],
        scratch_shapes=[pltpu.VMEM((keys + SUB, LANES), F32), pltpu.VMEM((levels * slots, LANES), F32)],
        compiler_params=params(),
        name="parents",
    )(got_keys, grad_coarse.T, down_pad)
    grad_pooled = grads[levels]
    returned = [from_partner(grads[level], level, bits_member) for level in range(levels)]

    gathered = pl.pallas_call(
        functools.partial(gather_kernel, levels, halo),
        grid=(kvol,),
        in_specs=[
            pl.BlockSpec((1, 1, vdev), lambda k: (k, 0, 0), memory_space=SMEM),
            vmem_full((vdev, LANES)),
        ]
        + [vmem_full((halo + 2 * SUB, LANES))] * levels,
        out_specs=pl.BlockSpec((vdev, LANES), lambda k: (0, k)),
        out_shape=shape((vdev, kvol * LANES), BF16),
        scratch_shapes=[pltpu.VMEM((table_rows, LANES), F32), pltpu.VMEM((256, LANES), F32)],
        compiler_params=params(),
        cost_estimate=pl.CostEstimate(flops=0, bytes_accessed=300_000_000, transcendentals=0),
        name="gather",
    )(index, table, *received)

    pre = jnp.dot(gathered, w_forward, preferred_element_type=F32)

    pools = 4
    middle = pl.pallas_call(
        functools.partial(middle_kernel, levels, tables=pools),
        in_specs=[smem_full((1, vdev))] * 3
        + [vmem_full((vdev, LANES)), vmem_full((keys, LANES))]
        + [vmem_full((slots, LANES))] * levels,
        out_specs=[vmem_full((vdev, LANES)), vmem_full((keys, LANES))] + [vmem_full((slots, LANES))] * levels,
        out_shape=[shape((vdev, LANES), BF16), shape((keys, LANES), F32)] + [shape((slots, LANES), BF16)] * levels,
        scratch_shapes=[
            pltpu.VMEM((keys + levels * slots, LANES), F32),
            pltpu.VMEM((vdev, LANES), F32),
            pltpu.VMEM((vdev, LANES), F32),
            pltpu.VMEM((levels * slots + SUB, LANES), F32),
        ]
        + [pltpu.VMEM((keys + SUB, LANES), F32)] * pools,
        compiler_params=params(),
        name="middle",
    )(parent, position, own_key, pre, grad_pooled, *returned)
    grad_pre, pool_part = middle[:2]
    came = [from_partner(middle[2 + level], level, bits_member) for level in range(levels)]

    grad_w = lax.dot_general(grad_pre, gathered, (((0,), (0,)), ((), ())), preferred_element_type=F32)
    grad_w = grad_w.reshape(LANES, kvol, LANES)[:chans, :, :chans].transpose(1, 0, 2)
    terms = jnp.dot(grad_pre, w_backward, preferred_element_type=F32)

    coarse_out, grad_down = pl.pallas_call(
        functools.partial(pool_kernel, levels),
        in_specs=[
            smem_full((1, levels * slots)),
            vmem_full((keys, LANES)),
            vmem_full((c2, coarse_dev)),
            vmem_full((noct, c2, LANES)),
        ]
        + [vmem_full((slots, LANES))] * levels,
        out_specs=[vmem_full((c2, coarse_dev)), vmem_full((noct, c2, chans))],
        out_shape=[shape((c2, coarse_dev), BF16), shape((noct, c2, chans), F32)],
        scratch_shapes=[pltpu.VMEM((levels * slots, LANES), F32)]
        + [pltpu.VMEM((keys + SUB, LANES), F32)] * pools,
        compiler_params=params(),
        name="pool",
    )(got_keys, pool_part, grad_coarse, down_pad, *came)

    grad_w, grad_down, terms = lax.optimization_barrier((grad_w, grad_down, terms))
    grad_w, grad_down = lax.psum((grad_w, grad_down), ("group", "member"))

    accumulators = 8
    scattered = pl.pallas_call(
        functools.partial(scatter_kernel, levels, halo),
        grid=(kvol,),
        in_specs=[
            pl.BlockSpec((1, 1, vdev), lambda k: (k, 0, 0), memory_space=SMEM),
            pl.BlockSpec((vdev, LANES), lambda k: (0, k)),
        ],
        out_specs=[vmem_full((vdev, LANES))] + [vmem_full((halo, LANES))] * levels,
        out_shape=[shape((vdev, LANES), F32)] + [shape((halo, LANES), BF16)] * levels,
        scratch_shapes=[pltpu.VMEM((table_rows, LANES), F32)] * accumulators,
        compiler_params=params(),
        cost_estimate=pl.CostEstimate(flops=0, bytes_accessed=400_000_000, transcendentals=0),
        name="scatter",
    )(index, terms)
    incoming = [from_partner(scattered[1 + level], level, bits_member) for level in range(levels)]

    grad_feats = pl.pallas_call(
        functools.partial(finish_kernel, levels),
        in_specs=[smem_full((1, levels * halo)), vmem_full((vdev, LANES))] + [vmem_full((halo, LANES))] * levels,
        out_specs=vmem_full((chans, vdev)),
        out_shape=shape((chans, vdev), F32),
        scratch_shapes=[pltpu.VMEM((levels * halo, LANES), F32)] + [pltpu.VMEM((vdev, LANES), F32)] * 4,
        compiler_params=params(),
        name="finish",
    )(outgoing, scattered[0], *incoming)
    return coarse_out, grad_feats, grad_w, grad_down


def solution(mesh):
    both = ("group", "member")
    in_specs = (
        P(None, both),
        P(None, both),
        P(both, None, None),
        P(),
        P(both, None),
        P(both),
        P(both),
        P(),
        P(None, both),
    )
    out_specs = (P(None, both), P(None, both), P(), P())
    return jax.shard_map(shards, mesh=mesh, in_specs=in_specs, out_specs=out_specs, check_vma=False)
```

time: 2160 us -> 398 us (0.18)
  local copies, waits for them, and re-layouts: 932 us -> 12.3 us
  other arithmetic: 798 us -> 0.62 us
  Pallas kernels: 0 us -> 245 us
  matrix products: 242 us -> 50.9 us
  waiting for transfers between devices: 103 us -> 33.1 us
    gather x69 -> x0, local copies, waits for them, and re-layouts: 765 us -> none  [the longest x27 403 us: backward_step(): taken = jnp.take(table, cols, axis=0)]
    scatter-add x35 -> x0, other arithmetic: 709 us -> none  [the longest x27 647 us: backward_step(): return (grad_table.at[cols].add(contrib), dweight)]
    pallas_call x0 -> x7, Pallas kernels: none -> 245 us  [the longest x1 105 us: shards(): pl.pallas_call(functools.partial(scatter_kernel, levels, halo), grid=(kvo...]
    dot_general x83 -> x3, matrix products: 235 us -> 50.9 us  [the longest x1 21.6 us: shards(): terms = jnp.dot(grad_pre, w_backward, preferred_element_type=F32)]
    psum x1, waiting for transfers between devices: 95.5 us -> 22.8 us  [shards(): grad_w, grad_down = lax.psum((grad_w, grad_down), ('group', 'member'))]
    select_n x52 -> x0, other arithmetic: 52.8 us -> none  [the longest x27 28.3 us: backward_step(): return (grad_table.at[cols].add(contrib), dweight)]
    dot_general x27 -> x0, local copies, waits for them, and re-layouts: 49.2 us -> none  [backward_step(): contrib = jnp.dot(grad_pre, weight, preferred_element_type=jnp.float32)]
    scatter x2 -> x0, local copies, waits for them, and re-layouts: 26.6 us -> none  [the longest x1 15.5 us: shards(): jnp.full((levels * slots + 1,), sentinel, jnp.int32).at[position]]
  transfers between devices with their start and end apart: 36 -> 29, of which waited for: 4 -> 8; matrix products, arithmetic and copies ran while one was open for 87% -> 14% of each run, Pallas kernels for 0% -> 53%
where the time goes in v1:
time: 398 us; the launch traced here: 397 us
  Pallas kernels  245 us (62%)
  matrix products  50.9 us (13%)
  starting transfers between devices  41 us (10%)
  waiting for transfers between devices  33.1 us (8%)
  between operations  14.5 us (4%)
  local copies, waits for them, and re-layouts  12.3 us (3%)
    pallas_call x1, Pallas kernels, shards(): pl.pallas_call(functools.partial(scatter_kernel, levels, halo), grid=(kvo...  105 us
    pallas_call x1, Pallas kernels, shards(): pl.pallas_call(functools.partial(gather_kernel, levels, halo), grid=(kvol...  99.3 us
    ppermute x28, starting transfers between devices, from_partner(): return lax.ppermute(value, axis, pairs)  40.9 us
    psum x1, waiting for transfers between devices, shards(): grad_w, grad_down = lax.psum((grad_w, grad_down), ('group', 'member'))  22.8 us
    dot_general x1, matrix products, shards(): terms = jnp.dot(grad_pre, w_backward, preferred_element_type=F32)  21.6 us
    pallas_call x1, Pallas kernels, shards(): pl.pallas_call(functools.partial(middle_kernel, levels, tables=pools), in...  18.4 us
    dot_general x1, matrix products, shards(): lax.dot_general(grad_pre, gathered, (((0,), (0,)), ((), ())), preferred_e...  15.1 us
    dot_general x1, matrix products, shards(): pre = jnp.dot(gathered, w_forward, preferred_element_type=F32)  14.2 us
  transfers between devices with their start and end apart: 29, of which 8 were waited for; matrix products, arithmetic and copies ran while one was open for 14% of the time, Pallas kernels for 53%

profile of v1, /device:TPU:0, one launch (start us, length us, event | category | flops | bytes accessed | tf_op | source)
XLA Modules:
  0.0 397.5 jit_solution(5135645473357129981)
XLA Ops:
  7.2 6.1 %prepare.1 = (bf16[272,128]{1,0:T(8,128)(2,1)}, bf16[272,128]{1,0:T(8,128)(2,1)}, bf16[272,128]{1,0:T(8,128)(2,1)}, bf16[272,128]{1,0:T(8,128)(2,1)}, bf16[272,1...) custom-call(s32[1]{0:T(128)} %bitcast.me_ref, ...), custom_call_target="tpu_custom_call" | custom-call | tf_op jit(solution)/shard_map/prepare/pallas_call | solution.py:308
  13.3 1.6 collective-permute-start
  15.0 2.7 collective-permute-start.1
  17.7 1.9 collective-permute-start.2
  19.6 3.6 collective-permute-start.3
  23.2 1.8 copy.16
  25.0 1.8 pad.9.weight_ref
  26.8 1.6 collective-permute-start.5
  28.4 2.9 collective-permute-start.6
  31.6 3.9 collective-permute-done.6.refs_6_
  36.2 3.9 parents.1
  40.4 1.7 collective-permute-start.8
  44.8 99.3 %gather.1 = bf16[4096,3456]{1,0:T(8,128)(2,1)} custom-call(s32[27,1,4096]{2,1,0:T(1,128)} %reshape.68.index_ref, f32[4096,128]{1,0:T(8,128)} %get-tuple-element.55.local_ref, bf16[272,128]{1,0:T(8,128)(2,1)} %copy-done.4, bf16[272,128]{1,0:T(8,128)(2,1)} %copy-done.5, bf16[272,128]{1,0:T(8,128)(2,1)} %copy-done.6, bf16[272,128]{1,0:T(8,128)(2,1)} %copy-done.7, ...), custom_call_target="tpu_custom_call" | custom-call | bytes 300000000 | tf_op jit(solution)/shard_map/gather/pallas_call | solution.py:342
  144.3 2.6 collective-permute-start.13
  146.9 14.2 %fusion.2.pre_ref = f32[4096,128]{1,0:T(8,128)} fusion(bf16[4096,3456]{1,0:T(8,128)(2,1)} %gather.1, bf16[3456,128]{1,0:T(8,128)(2,1)S(1)} %bitcast.52), kind=kOutput, calls=%fused_computation.19 | convolution fusion | flops 3623878656 | bytes 31293440 | tf_op jit(solution)/shard_map/dot_general | solution.py:358
  161.8 18.4 %middle.1 = (bf16[4096,128]{1,0:T(8,128)(2,1)}, f32[4096,128]{1,0:T(8,128)}, bf16[128,128]{1,0:T(8,128)(2,1)}, bf16[128,128]{1,0:T(8,128)(2,1)}, bf16[128,128]{1...) custom-call(s32[1,4096]{1,0:T(1,128)} %get-tuple-element.52.parent_r, ...), custom_call_target="tpu_custom_call" | custom-call | tf_op jit(solution)/shard_map/middle/pallas_call | solution.py:361
  180.8 3.7 collective-permute-start.15
  184.5 1.5 collective-permute-start.16
  186.0 21.6 %fusion.4.terms_ref = f32[4096,3456]{1,0:T(8,128)} fusion(bf16[4096,128]{1,0:T(8,128)(2,1)} %get-tuple-element.73, bf16[128,3456]{0,1:T(8,128)(2,1)S(1)} %bitcast.53), kind=kOutput, calls=%fused_computation.21 | convolution fusion | flops 3623878656 | bytes 58556416 | tf_op jit(solution)/shard_map/dot_general | solution.py:383
  207.7 15.1 %fusion.3 = f32[128,3456]{0,1:T(8,128)S(1)} fusion(bf16[4096,128]{1,0:T(8,128)(2,1)S(1)} %copy-done, bf16[4096,3456]{1,0:T(8,128)(2,1)} %gather.1), kind=kOutput, calls=%fused_computation.20 | convolution fusion | flops 3623878656 | bytes 31129600 | tf_op jit(solution)/shard_map/dot_general | solution.py:381
  222.8 4.1 %collective-permute-start.17 = (bf16[128,128]{1,0:T(8,128)(2,1)S(1)}, bf16[128,128]{1,0:T(8,128)(2,1)S(1)}, u32[]{:S(2)}, u32[]{:S(2)}) collective-permute-start(bf16[128,128]{1,0:T(8,128)(2,1)S(1)} %copy-done.38), channel_id=1, source_target_pairs={{0,8},{1,9},{2,10},{3,11},{4,12},{5,13},{6,14},{7,15},{8,0},{9,1},... | collective-permute-start | bytes 98312 | tf_op jit(solution)/shard_map/ppermute | solution.py:23
  227.7 3.3 collective-permute-start.20
  234.0 5.6 %pool.1 = (bf16[192,512]{1,0:T(8,128)(2,1)}, f32[8,192,96]{2,1,0:T(8,128)}) custom-call(s32[1,896]{1,0:T(1,128)} %fusion.1.keys_ref, f32[4096,128]{1,0:T(8,128)} %get-tuple-element.64.pool_ref, bf16[192,512]{1,0:T(8,128)(2,1)} %grad_ref.1, bf16[8,192,128]{2,1,0:T(8,128)(2,1)} %pad.9.weight_ref, bf16[128,128]{1,0:T(8,128)(2,1)} %copy-done.23, ...), custom_call_target="tpu_custom_call" | custom-call | tf_op jit(solution)/shard_map/pool/pallas_call | solution.py:385
  239.6 105.4 %scatter.1 = (f32[4096,128]{1,0:T(8,128)}, bf16[256,128]{1,0:T(8,128)(2,1)}, bf16[256,128]{1,0:T(8,128)(2,1)}, bf16[256,128]{1,0:T(8,128)(2,1)}, bf16[256,128]{1...) custom-call(s32[27,1,4096]{2,1,0:T(1,128)} %reshape.68.index_ref, ...), custom_call_target="tpu_custom_call" | custom-call | bytes 400000000 | tf_op jit(solution)/shard_map/scatter/pallas_call | solution.py:406
  345.0 1.9 collective-permute-start.22
  347.6 1.9 collective-permute-done.21.refs_0_
  349.5 1.5 collective-permute-start.26
  351.1 3.0 collective-permute-start.27
  354.6 2.5 collective-permute-done.27.refs_6_
  357.7 6.4 %finish.1 = f32[96,4096]{1,0:T(8,128)} custom-call(s32[1,1792]{1,0:T(1,128)} %bitcast.56, f32[4096,128]{1,0:T(8,128)} %get-tuple-element.76.local_ref, bf16[256,128]{1,0:T(8,128)(2,1)} %copy-done.11, bf16[256,128]{1,0:T(8,128)(2,1)} %copy-done.12, bf16[256,128]{1,0:T(8,128)(2,1)} %copy-done.13, bf16[256,128]{1,0:T(8,128)(2,1)} %copy-done.14, ...), custom_call_target="tpu_custom_call" | custom-call | tf_op jit(solution)/shard_map/finish/pallas_call | solution.py:422
  364.1 22.8 %all-reduce.5.cloned.1.call-done = (f32[27,96,96]{1,2,0:T(8,128)}, f32[8,192,96]{2,1,0:T(8,128)}) async-done(((f32[27,96,96]{1,2,0:T(8,128)}, f32[8,192,96]{2,1,0:T(8,128)}), (f32[27,96,96]{1,2,0:T(8,128)}, f32[8,192,96]{2,1,0:T(8,128)})) %all-reduce.5.cloned.1.call-update) | async-done | bytes 1585168 | tf_op jit(solution)/shard_map/psum | solution.py:403
  386.9 2.9 copy.18
  (136 shorter events, 11.9 us)
Async XLA Ops:
  7.2 36.2 %copy-start.2 = (bf16[27,96,96]{2,1,0:T(8,128)(2,1)S(1)}, bf16[27,96,96]{2,1,0:T(8,128)(2,1)}, u32[]{:S(2)}) copy-start(bf16[27,96,96]{2,1,0:T(8,128)(2,1)} %param.12) | copy-start | bytes 1492996
  7.2 379.7 %all-reduce.5.cloned.1.call-start = ((), (), s32[]{:S(2)}) async-start(), calls=%async_computation | async-start | bytes 4227072 | tf_op jit(solution)/shard_map/psum | solution.py:403
  13.3 13.5 %collective-permute-start = (bf16[272,128]{1,0:T(8,128)(2,1)}, bf16[272,128]{1,0:T(8,128)(2,1)S(1)}, u32[]{:S(2)}, u32[]{:S(2)}) collective-permute-start(bf16[272,128]{1,0:T(8,128)(2,1)} %get-tuple-element.45), channel_id=1, source_target_pairs={{0,1},{1,0},{2,3},{3,2},{4,5},{5,4},{6,7},{7,6},{8,9},{9,8},{10,11... | collective-permute-start | bytes 208904 | tf_op jit(solution)/shard_map/ppermute | solution.py:23
  15.0 13.4 %collective-permute-start.1 = (bf16[272,128]{1,0:T(8,128)(2,1)}, bf16[272,128]{1,0:T(8,128)(2,1)S(1)}, u32[]{:S(2)}, u32[]{:S(2)}) collective-permute-start(bf16[272,128]{1,0:T(8,128)(2,1)} %get-tuple-element.46), channel_id=1, source_target_pairs={{0,2},{1,3},{2,0},{3,1},{4,6},{5,7},{6,4},{7,5},{8,10},{9,11},{10,... | collective-permute-start | bytes 208904 | tf_op jit(solution)/shard_map/ppermute | solution.py:23
  17.7 13.6 %collective-permute-start.2 = (bf16[272,128]{1,0:T(8,128)(2,1)}, bf16[272,128]{1,0:T(8,128)(2,1)S(1)}, u32[]{:S(2)}, u32[]{:S(2)}) collective-permute-start(bf16[272,128]{1,0:T(8,128)(2,1)} %get-tuple-element.47), channel_id=1, source_target_pairs={{0,4},{1,5},{2,6},{3,7},{4,0},{5,1},{6,2},{7,3},{8,12},{9,13},{10,... | collective-permute-start | bytes 208904 | tf_op jit(solution)/shard_map/ppermute | solution.py:23
  19.6 11.7 %collective-permute-start.3 = (bf16[272,128]{1,0:T(8,128)(2,1)}, bf16[272,128]{1,0:T(8,128)(2,1)S(1)}, u32[]{:S(2)}, u32[]{:S(2)}) collective-permute-start(bf16[272,128]{1,0:T(8,128)(2,1)} %get-tuple-element.48), channel_id=1, source_target_pairs={{0,8},{1,9},{2,10},{3,11},{4,12},{5,13},{6,14},{7,15},{8,0},{9,1},... | collective-permute-start | bytes 208904 | tf_op jit(solution)/shard_map/ppermute | solution.py:23
  23.2 8.2 %collective-permute-start.4 = (bf16[272,128]{1,0:T(8,128)(2,1)}, bf16[272,128]{1,0:T(8,128)(2,1)S(1)}, u32[]{:S(2)}, u32[]{:S(2)}) collective-permute-start(bf16[272,128]{1,0:T(8,128)(2,1)} %get-tuple-element.49), channel_id=1, source_target_pairs={{0,16},{16,0},{32,48},{48,32},{64,80},{80,64},{96,112},{112,96},{1... | collective-permute-start | bytes 208904 | tf_op jit(solution)/shard_map/ppermute | solution.py:23
  26.8 4.8 %collective-permute-start.5 = (bf16[272,128]{1,0:T(8,128)(2,1)}, bf16[272,128]{1,0:T(8,128)(2,1)S(1)}, u32[]{:S(2)}, u32[]{:S(2)}) collective-permute-start(bf16[272,128]{1,0:T(8,128)(2,1)} %get-tuple-element.50), channel_id=1, source_target_pairs={{0,32},{16,48},{32,0},{48,16},{64,96},{80,112},{96,64},{112,80},{1... | collective-permute-start | bytes 208904 | tf_op jit(solution)/shard_map/ppermute | solution.py:23
  28.4 7.2 %collective-permute-start.6 = (bf16[272,128]{1,0:T(8,128)(2,1)}, bf16[272,128]{1,0:T(8,128)(2,1)S(1)}, u32[]{:S(2)}, u32[]{:S(2)}) collective-permute-start(bf16[272,128]{1,0:T(8,128)(2,1)} %get-tuple-element.51), channel_id=1, source_target_pairs={{0,64},{16,80},{32,96},{48,112},{64,0},{80,16},{96,32},{112,48},{1... | collective-permute-start | bytes 208904 | tf_op jit(solution)/shard_map/ppermute | solution.py:23
  40.1 103.9 %collective-permute-start.7 = (bf16[128,128]{1,0:T(8,128)(2,1)}, bf16[128,128]{1,0:T(8,128)(2,1)S(1)}, u32[]{:S(2)}, u32[]{:S(2)}) collective-permute-start(bf16[128,128]{1,0:T(8,128)(2,1)} %get-tuple-element.57), channel_id=1, source_target_pairs={{0,1},{1,0},{2,3},{3,2},{4,5},{5,4},{6,7},{7,6},{8,9},{9,8},{10,11... | collective-permute-start | bytes 98312 | tf_op jit(solution)/shard_map/ppermute | solution.py:23
  40.4 103.9 %collective-permute-start.8 = (bf16[128,128]{1,0:T(8,128)(2,1)}, bf16[128,128]{1,0:T(8,128)(2,1)S(1)}, u32[]{:S(2)}, u32[]{:S(2)}) collective-permute-start(bf16[128,128]{1,0:T(8,128)(2,1)} %get-tuple-element.58), channel_id=1, source_target_pairs={{0,2},{1,3},{2,0},{3,1},{4,6},{5,7},{6,4},{7,5},{8,10},{9,11},{10,... | collective-permute-start | bytes 98312 | tf_op jit(solution)/shard_map/ppermute | solution.py:23
  44.1 117.1 %collective-permute-start.9 = (bf16[128,128]{1,0:T(8,128)(2,1)S(1)}, bf16[128,128]{1,0:T(8,128)(2,1)S(1)}, u32[]{:S(2)}, u32[]{:S(2)}) collective-permute-start(bf16[128,128]{1,0:T(8,128)(2,1)S(1)} %copy-done.40), channel_id=1, source_target_pairs={{0,4},{1,5},{2,6},{3,7},{4,0},{5,1},{6,2},{7,3},{8,12},{9,13},{10,... | collective-permute-start | bytes 98312 | tf_op jit(solution)/shard_map/ppermute | solution.py:23
  44.2 117.0 %collective-permute-start.10 = (bf16[128,128]{1,0:T(8,128)(2,1)S(1)}, bf16[128,128]{1,0:T(8,128)(2,1)S(1)}, u32[]{:S(2)}, u32[]{:S(2)}) collective-permute-start(bf16[128,128]{1,0:T(8,128)(2,1)S(1)} %copy-done.39), channel_id=1, source_target_pairs={{0,8},{1,9},{2,10},{3,11},{4,12},{5,13},{6,14},{7,15},{8,0},{9,1},... | collective-permute-start | bytes 98312 | tf_op jit(solution)/shard_map/ppermute | solution.py:23
  44.8 116.3 %collective-permute-start.11 = (bf16[128,128]{1,0:T(8,128)(2,1)S(1)}, bf16[128,128]{1,0:T(8,128)(2,1)S(1)}, u32[]{:S(2)}, u32[]{:S(2)}) collective-permute-start(bf16[128,128]{1,0:T(8,128)(2,1)S(1)} %copy-done.37), channel_id=1, source_target_pairs={{0,16},{16,0},{32,48},{48,32},{64,80},{80,64},{96,112},{112,96},{1... | collective-permute-start | bytes 98312 | tf_op jit(solution)/shard_map/ppermute | solution.py:23
  44.8 99.3 %copy-start.35 = (bf16[128,128]{1,0:T(8,128)(2,1)S(1)}, bf16[128,128]{1,0:T(8,128)(2,1)}, u32[]{:S(2)}) copy-start(bf16[128,128]{1,0:T(8,128)(2,1)} %get-tuple-element.62) | copy-start | bytes 98308
  44.8 99.5 %copy-start.33 = (bf16[128,128]{1,0:T(8,128)(2,1)S(1)}, bf16[128,128]{1,0:T(8,128)(2,1)}, u32[]{:S(2)}) copy-start(bf16[128,128]{1,0:T(8,128)(2,1)} %get-tuple-element.63) | copy-start | bytes 98308
  144.1 17.1 %collective-permute-start.12 = (bf16[128,128]{1,0:T(8,128)(2,1)S(1)}, bf16[128,128]{1,0:T(8,128)(2,1)S(1)}, u32[]{:S(2)}, u32[]{:S(2)}) collective-permute-start(bf16[128,128]{1,0:T(8,128)(2,1)S(1)} %copy-done.35), channel_id=1, source_target_pairs={{0,32},{16,48},{32,0},{48,16},{64,96},{80,112},{96,64},{112,80},{1... | collective-permute-start | bytes 98312 | tf_op jit(solution)/shard_map/ppermute | solution.py:23
  144.3 16.9 %collective-permute-start.13 = (bf16[128,128]{1,0:T(8,128)(2,1)S(1)}, bf16[128,128]{1,0:T(8,128)(2,1)S(1)}, u32[]{:S(2)}, u32[]{:S(2)}) collective-permute-start(bf16[128,128]{1,0:T(8,128)(2,1)S(1)} %copy-done.33), channel_id=1, source_target_pairs={{0,64},{16,80},{32,96},{48,112},{64,0},{80,16},{96,32},{112,48},{1... | collective-permute-start | bytes 98312 | tf_op jit(solution)/shard_map/ppermute | solution.py:23
  180.2 46.7 %collective-permute-start.14 = (bf16[128,128]{1,0:T(8,128)(2,1)}, bf16[128,128]{1,0:T(8,128)(2,1)S(1)}, u32[]{:S(2)}, u32[]{:S(2)}) collective-permute-start(bf16[128,128]{1,0:T(8,128)(2,1)} %get-tuple-element.65), channel_id=1, source_target_pairs={{0,1},{1,0},{2,3},{3,2},{4,5},{5,4},{6,7},{7,6},{8,9},{9,8},{10,11... | collective-permute-start | bytes 98312 | tf_op jit(solution)/shard_map/ppermute | solution.py:23
  180.8 46.9 %collective-permute-start.15 = (bf16[128,128]{1,0:T(8,128)(2,1)}, bf16[128,128]{1,0:T(8,128)(2,1)S(1)}, u32[]{:S(2)}, u32[]{:S(2)}) collective-permute-start(bf16[128,128]{1,0:T(8,128)(2,1)} %get-tuple-element.66), channel_id=1, source_target_pairs={{0,2},{1,3},{2,0},{3,1},{4,6},{5,7},{6,4},{7,5},{8,10},{9,11},{10,... | collective-permute-start | bytes 98312 | tf_op jit(solution)/shard_map/ppermute | solution.py:23
  184.5 47.6 %collective-permute-start.16 = (bf16[128,128]{1,0:T(8,128)(2,1)}, bf16[128,128]{1,0:T(8,128)(2,1)S(1)}, u32[]{:S(2)}, u32[]{:S(2)}) collective-permute-start(bf16[128,128]{1,0:T(8,128)(2,1)} %get-tuple-element.67), channel_id=1, source_target_pairs={{0,4},{1,5},{2,6},{3,7},{4,0},{5,1},{6,2},{7,3},{8,12},{9,13},{10,... | collective-permute-start | bytes 98312 | tf_op jit(solution)/shard_map/ppermute | solution.py:23
  222.8 9.4 %collective-permute-start.17 = (bf16[128,128]{1,0:T(8,128)(2,1)S(1)}, bf16[128,128]{1,0:T(8,128)(2,1)S(1)}, u32[]{:S(2)}, u32[]{:S(2)}) collective-permute-start(bf16[128,128]{1,0:T(8,128)(2,1)S(1)} %copy-done.38), channel_id=1, source_target_pairs={{0,8},{1,9},{2,10},{3,11},{4,12},{5,13},{6,14},{7,15},{8,0},{9,1},... | collective-permute-start | bytes 98312 | tf_op jit(solution)/shard_map/ppermute | solution.py:23
  226.9 5.3 %collective-permute-start.18 = (bf16[128,128]{1,0:T(8,128)(2,1)S(1)}, bf16[128,128]{1,0:T(8,128)(2,1)S(1)}, u32[]{:S(2)}, u32[]{:S(2)}) collective-permute-start(bf16[128,128]{1,0:T(8,128)(2,1)S(1)} %copy-done.36), channel_id=1, source_target_pairs={{0,16},{16,0},{32,48},{48,32},{64,80},{80,64},{96,112},{112,96},{1... | collective-permute-start | bytes 98312 | tf_op jit(solution)/shard_map/ppermute | solution.py:23
  226.9 5.3 %collective-permute-start.19 = (bf16[128,128]{1,0:T(8,128)(2,1)S(1)}, bf16[128,128]{1,0:T(8,128)(2,1)S(1)}, u32[]{:S(2)}, u32[]{:S(2)}) collective-permute-start(bf16[128,128]{1,0:T(8,128)(2,1)S(1)} %copy-done.34), channel_id=1, source_target_pairs={{0,32},{16,48},{32,0},{48,16},{64,96},{80,112},{96,64},{112,80},{1... | collective-permute-start | bytes 98312 | tf_op jit(solution)/shard_map/ppermute | solution.py:23
  227.7 5.7 %collective-permute-start.20 = (bf16[128,128]{1,0:T(8,128)(2,1)S(1)}, bf16[128,128]{1,0:T(8,128)(2,1)S(1)}, u32[]{:S(2)}, u32[]{:S(2)}) collective-permute-start(bf16[128,128]{1,0:T(8,128)(2,1)S(1)} %copy-done.32), channel_id=1, source_target_pairs={{0,64},{16,80},{32,96},{48,112},{64,0},{80,16},{96,32},{112,48},{1... | collective-permute-start | bytes 98312 | tf_op jit(solution)/shard_map/ppermute | solution.py:23
  345.0 4.5 %collective-permute-start.21 = (bf16[256,128]{1,0:T(8,128)(2,1)}, bf16[256,128]{1,0:T(8,128)(2,1)S(1)}, u32[]{:S(2)}, u32[]{:S(2)}) collective-permute-start(bf16[256,128]{1,0:T(8,128)(2,1)} %get-tuple-element.77), channel_id=1, source_target_pairs={{0,1},{1,0},{2,3},{3,2},{4,5},{5,4},{6,7},{7,6},{8,9},{9,8},{10,11... | collective-permute-start | bytes 196616 | tf_op jit(solution)/shard_map/ppermute | solution.py:23
  345.0 6.1 %collective-permute-start.22 = (bf16[256,128]{1,0:T(8,128)(2,1)}, bf16[256,128]{1,0:T(8,128)(2,1)S(1)}, u32[]{:S(2)}, u32[]{:S(2)}) collective-permute-start(bf16[256,128]{1,0:T(8,128)(2,1)} %get-tuple-element.78), channel_id=1, source_target_pairs={{0,2},{1,3},{2,0},{3,1},{4,6},{5,7},{6,4},{7,5},{8,10},{9,11},{10,... | collective-permute-start | bytes 196616 | tf_op jit(solution)/shard_map/ppermute | solution.py:23
  346.9 7.2 %collective-permute-start.23 = (bf16[256,128]{1,0:T(8,128)(2,1)}, bf16[256,128]{1,0:T(8,128)(2,1)S(1)}, u32[]{:S(2)}, u32[]{:S(2)}) collective-permute-start(bf16[256,128]{1,0:T(8,128)(2,1)} %get-tuple-element.79), channel_id=1, source_target_pairs={{0,4},{1,5},{2,6},{3,7},{4,0},{5,1},{6,2},{7,3},{8,12},{9,13},{10,... | collective-permute-start | bytes 196616 | tf_op jit(solution)/shard_map/ppermute | solution.py:23
  346.9 7.2 %collective-permute-start.24 = (bf16[256,128]{1,0:T(8,128)(2,1)}, bf16[256,128]{1,0:T(8,128)(2,1)S(1)}, u32[]{:S(2)}, u32[]{:S(2)}) collective-permute-start(bf16[256,128]{1,0:T(8,128)(2,1)} %get-tuple-element.80), channel_id=1, source_target_pairs={{0,8},{1,9},{2,10},{3,11},{4,12},{5,13},{6,14},{7,15},{8,0},{9,1},... | collective-permute-start | bytes 196616 | tf_op jit(solution)/shard_map/ppermute | solution.py:23
  347.6 6.5 %collective-permute-start.25 = (bf16[256,128]{1,0:T(8,128)(2,1)}, bf16[256,128]{1,0:T(8,128)(2,1)S(1)}, u32[]{:S(2)}, u32[]{:S(2)}) collective-permute-start(bf16[256,128]{1,0:T(8,128)(2,1)} %get-tuple-element.81), channel_id=1, source_target_pairs={{0,16},{16,0},{32,48},{48,32},{64,80},{80,64},{96,112},{112,96},{1... | collective-permute-start | bytes 196616 | tf_op jit(solution)/shard_map/ppermute | solution.py:23
  349.5 5.1 %collective-permute-start.26 = (bf16[256,128]{1,0:T(8,128)(2,1)}, bf16[256,128]{1,0:T(8,128)(2,1)S(1)}, u32[]{:S(2)}, u32[]{:S(2)}) collective-permute-start(bf16[256,128]{1,0:T(8,128)(2,1)} %get-tuple-element.82), channel_id=1, source_target_pairs={{0,32},{16,48},{32,0},{48,16},{64,96},{80,112},{96,64},{112,80},{1... | collective-permute-start | bytes 196616 | tf_op jit(solution)/shard_map/ppermute | solution.py:23
  351.1 6.0 %collective-permute-start.27 = (bf16[256,128]{1,0:T(8,128)(2,1)}, bf16[256,128]{1,0:T(8,128)(2,1)S(1)}, u32[]{:S(2)}, u32[]{:S(2)}) collective-permute-start(bf16[256,128]{1,0:T(8,128)(2,1)} %get-tuple-element.83), channel_id=1, source_target_pairs={{0,64},{16,80},{32,96},{48,112},{64,0},{80,16},{96,32},{112,48},{1... | collective-permute-start | bytes 196616 | tf_op jit(solution)/shard_map/ppermute | solution.py:23
  (38 other events, 318.0 us)
Sparse Core Ops, SparseCore 0:
  239.7 147.1 all-reduce.4

commit v2 on v1

v2 whole, which is shorter than its diff:
```python
import functools

import jax
import jax.numpy as jnp
from jax import lax
from jax.experimental import pallas as pl
from jax.experimental.pallas import tpu as pltpu
from jax.sharding import PartitionSpec as P

LANES = 128
SUB = 8
DIGIT = 64
SMEM = pltpu.SMEM
F32 = jnp.float32
BF16 = jnp.bfloat16
I32 = jnp.int32


def from_partner(value, level, bits_member):
    axis, stride = ("member", level) if level < bits_member else ("group", level - bits_member)
    mask = 2**stride
    pairs = [(source, source ^ mask) for source in range(lax.axis_size(axis))]
    return lax.ppermute(value, axis, pairs)


def vmem_full(shape):
    return pl.BlockSpec(shape, lambda *_: (0,) * len(shape))


def smem_full(shape):
    return pl.BlockSpec(shape, lambda *_: (0,) * len(shape), memory_space=SMEM)


def copy_rows(count, unroll, index, source, target):
    def body(step, _):
        base = pl.multiple_of(step * unroll, unroll)
        for j in range(unroll):
            target[pl.ds(base + j, 1), :] = source[pl.ds(index(base + j), 1), :]
        return 0

    lax.fori_loop(0, count // unroll, body, 0)


def add_rows(count, unroll, index, source, tables):
    lanes = len(tables)

    def body(step, _):
        base = pl.multiple_of(step * unroll, unroll)
        for start in range(0, unroll, lanes):
            spots = [index(base + start + j) for j in range(lanes)]
            sums = [
                tables[j][pl.ds(spots[j], 1), :] + source[pl.ds(base + start + j, 1), :]
                for j in range(lanes)
            ]
            for j in range(lanes):
                tables[j][pl.ds(spots[j], 1), :] = sums[j]
        return 0

    lax.fori_loop(0, count // unroll, body, 0)


def prepare_kernel(levels, me_ref, rows_ref, owner_ref, coarse_ref, octant_ref, feats_ref, *refs, noct, coarse_dev, slots):
    messages = refs[:levels]
    table_ref, self_ref, list_ref, pos_ref, buf = refs[levels:]
    chans, vdev = feats_ref.shape
    halo = rows_ref.shape[1] // levels
    noct_keys = noct * coarse_dev
    fill = jnp.zeros((LANES - chans, LANES), F32)
    for c in range(vdev // LANES):
        cols = pl.ds(c * LANES, LANES)
        block = jnp.concatenate([feats_ref[:, cols].astype(F32), fill], axis=0)
        table_ref[cols, :] = block.T
    copy_rows(levels * halo, 64, lambda r: rows_ref[0, r], table_ref, buf)

    differ = jnp.bitwise_xor(owner_ref[...], me_ref[0])
    level_id = lax.broadcasted_iota(I32, (SUB, LANES), 0)
    bit = jnp.where(level_id < levels, jnp.left_shift(jnp.ones_like(level_id), level_id), 0)
    chunks = vdev // LANES
    classes = []
    for c in range(chunks):
        part = jnp.broadcast_to(differ[:, c * LANES : (c + 1) * LANES], (SUB, LANES))
        classes.append(jnp.where((part == bit) & (level_id < levels), 1.0, 0.0).astype(F32))
    upper = lax.broadcasted_iota(I32, (LANES, LANES), 0) <= lax.broadcasted_iota(I32, (LANES, LANES), 1)
    prefix = jnp.dot(
        jnp.concatenate(classes, axis=0).astype(BF16),
        jnp.where(upper, 1.0, 0.0).astype(BF16),
        preferred_element_type=F32,
    )
    carry = jnp.zeros((SUB, 1), F32)
    start = (level_id * slots).astype(F32)
    digit_rows = []
    digit_id = lax.broadcasted_iota(I32, (SUB, LANES), 0)
    for c in range(chunks):
        cols = pl.ds(c * LANES, LANES)
        inclusive = prefix[c * SUB : (c + 1) * SUB]
        spot = classes[c] * (start + inclusive - 1.0 + carry)
        carry = carry + inclusive[:, LANES - 1 :]
        remote = jnp.sum(classes[c], axis=0, keepdims=True) > 0.5
        position = jnp.where(remote, jnp.sum(spot, axis=0, keepdims=True).astype(I32), levels * slots)
        keys = octant_ref[:, cols] * coarse_dev + coarse_ref[:, cols]
        pos_ref[:, cols] = position
        self_ref[:, cols] = jnp.where(remote, noct_keys, keys)
        voxel = lax.broadcasted_iota(I32, (SUB, LANES), 1) + c * LANES
        number = jnp.where(digit_id < 2, jnp.broadcast_to(keys, (SUB, LANES)), voxel)
        high = lax.shift_right_logical(number, 6) - DIGIT
        low = number & (DIGIT - 1)
        digits = jnp.where(digit_id < 4, jnp.where((digit_id & 1) == 0, high, low), 0)
        digit_rows.append(digits.astype(F32).astype(BF16))
    digits = jnp.concatenate(digit_rows, axis=1)
    slot_id = lax.broadcasted_iota(I32, (slots, LANES), 0)
    for level in range(levels):
        hot = []
        for c in range(chunks):
            position = jnp.broadcast_to(pos_ref[:, pl.ds(c * LANES, LANES)], (slots, LANES))
            hot.append(jnp.where(position == slot_id + level * slots, 1.0, 0.0).astype(BF16))
        found = lax.dot_general(
            digits, jnp.concatenate(hot, axis=1), (((1,), (1,)), ((), ())), preferred_element_type=F32
        )
        found = found + jnp.where((digit_id & 1) == 0, float(DIGIT), 0.0)
        list_ref[:, pl.ds(level * slots, slots)] = (found[2:3] * float(DIGIT) + found[3:4]).astype(I32)
        messages[level][pl.ds(0, halo), :] = buf[pl.ds(level * halo, halo), :].astype(BF16)
        messages[level][pl.ds(halo, 2 * SUB), :] = jnp.concatenate(
            [found, jnp.zeros((SUB, LANES), F32)], axis=0
        ).astype(BF16)


def parents_kernel(self_ref, coarse_ref, weight_ref, wide_ref, rows_ref):
    noct = weight_ref.shape[0]
    ndev = coarse_ref.shape[0]
    for o in range(noct):
        grad = jnp.dot(coarse_ref[...], weight_ref[o], preferred_element_type=F32)
        wide_ref[pl.ds(o * ndev, ndev), :] = grad.astype(BF16).astype(F32)
    wide_ref[pl.ds(noct * ndev, SUB), :] = jnp.zeros((SUB, LANES), F32)
    copy_rows(rows_ref.shape[0], 64, lambda r: self_ref[0, r], wide_ref, rows_ref)


def answer_kernel(levels, keys_ref, wide_ref, *refs):
    outs = refs[:levels]
    buf = refs[levels]
    slots = outs[0].shape[0]
    copy_rows(levels * slots, 64, lambda r: keys_ref[0, r], wide_ref, buf)
    for level in range(levels):
        outs[level][...] = buf[pl.ds(level * slots, slots), :].astype(BF16)


def index_copy(index_ref, spot, piece, store, sem, width):
    pieces = index_ref.shape[2] // width
    row = lax.div(piece, pieces)
    start = pl.multiple_of(lax.rem(piece, pieces) * width, width)
    return pltpu.make_async_copy(index_ref.at[row, :, pl.ds(start, width)], store, sem)


def walk(index_ref, stores, sems, vdev, chunk, step_of):
    k = pl.program_id(0)
    total = pl.num_programs(0)
    width = stores[0].shape[1]
    many = len(stores)
    pieces = vdev // width

    @pl.when(k == 0)
    def _():
        for b in range(many):
            index_copy(index_ref, b, b, stores[b], sems.at[b], width).start()

    def body(turn, _):
        for b in range(many):
            piece = k * pieces + turn * many + b
            index_copy(index_ref, b, piece, stores[b], sems.at[b], width).wait()
            for sub in range(width // chunk):
                base = pl.multiple_of((turn * many + b) * width + sub * chunk, chunk)
                step_of(base, sub % 2, stores[b], sub * chunk, b == 0 and sub == 0, turn)

            @pl.when(piece + many < total * pieces)
            def _():
                index_copy(index_ref, b, piece + many, stores[b], sems.at[b], width).start()

        return 0

    lax.fori_loop(0, pieces // many, body, 0)


def gather_kernel(levels, halo, index_ref, local_ref, weight_ref, *refs):
    received = refs[:levels]
    out_ref, pre_ref, table, buf0, buf1 = refs[levels : levels + 5]
    stores = refs[levels + 5 : -1]
    sems = refs[-1]
    bufs = (buf0, buf1)
    vdev = local_ref.shape[0]
    chunk = buf0.shape[0]

    @pl.when(pl.program_id(0) == 0)
    def _():
        table[pl.ds(0, vdev), :] = local_ref[...]
        for level in range(levels):
            table[pl.ds(vdev + level * halo, halo), :] = received[level][pl.ds(0, halo), :].astype(F32)
        table[pl.ds(vdev + levels * halo, SUB), :] = jnp.zeros((SUB, LANES), F32)
        pre_ref[...] = jnp.zeros_like(pre_ref)
        buf1[...] = jnp.zeros_like(buf1)

    def use(buf, base, live):
        taken = buf[...].astype(BF16)
        part = pl.ds(base, chunk)
        out_ref[part, :] = taken
        term = jnp.dot(taken, weight_ref[0], preferred_element_type=F32)
        if live is not None:
            term = term * live
        pre_ref[part, :] += term

    def step(base, parity, store, entry, first, turn):
        buf = bufs[parity]
        for j in range(chunk):
            buf[pl.ds(j, 1), :] = table[pl.ds(store[0, entry + j], 1), :]
        if first:
            behind = pl.multiple_of(jnp.maximum(base - chunk, 0), chunk)
            use(bufs[1 - parity], behind, jnp.minimum(turn, 1).astype(F32))
        else:
            use(bufs[1 - parity], pl.multiple_of(base - chunk, chunk), None)

    walk(index_ref, stores, sems, vdev, chunk, step)
    use(buf1, vdev - chunk, None)


def middle_kernel(levels, list_ref, pre_ref, rows_ref, *refs):
    returned = refs[:levels]
    grad_ref, turned_ref, act_ref = refs[levels : levels + 3]
    sends = refs[levels + 3 : 2 * levels + 3]
    rows, back, act, out = refs[2 * levels + 3 :]
    vdev = pre_ref.shape[0]
    slots = returned[0].shape[0]
    rows[pl.ds(0, vdev), :] = rows_ref[...]
    for level in range(levels):
        back[pl.ds(level * slots, slots), :] = returned[level][...].astype(F32)

    def patch(step, _):
        base = pl.multiple_of(step * 64, 64)
        for j in range(64):
            rows[pl.ds(list_ref[0, base + j], 1), :] = back[pl.ds(base + j, 1), :]
        return 0

    lax.fori_loop(0, levels * slots // 64, patch, 0)

    for step in range(vdev // LANES):
        part = pl.ds(step * LANES, LANES)
        pre = pre_ref[part, :]
        sig = 1.0 / (1.0 + jnp.exp(-pre))
        value = (pre * sig).astype(BF16).astype(F32)
        act[part, :] = value
        act_ref[part, :] = value
        grad = rows[part, :] * (sig * (1.0 + pre * (1.0 - sig)))
        grad_ref[part, :] = grad.astype(BF16)
        turned_ref[:, part] = grad.T.astype(BF16)
    act[pl.ds(vdev, SUB), :] = jnp.zeros((SUB, LANES), F32)
    copy_rows(levels * slots, 64, lambda r: list_ref[0, r], act, out)
    for level in range(levels):
        sends[level][...] = out[pl.ds(level * slots, slots), :].astype(BF16)


def weights_kernel(turned_ref, taken_ref, out_ref):
    wide = jnp.dot(turned_ref[...], taken_ref[...], preferred_element_type=F32)
    many, rows, cols = out_ref.shape
    for j in range(many):
        out_ref[j] = wide[:rows, j * LANES : j * LANES + cols]


def pool_kernel(levels, keys_ref, self_ref, act_ref, grad_ref, weight_ref, *refs):
    received = refs[:levels]
    coarse_ref, down_ref, rows = refs[levels : levels + 3]
    pools = refs[levels + 3 :]
    slots = received[0].shape[0]
    noct, _, chans = down_ref.shape
    ndev = grad_ref.shape[1]
    for level in range(levels):
        rows[pl.ds(level * slots, slots), :] = received[level][...].astype(F32)
    for pool in pools:
        pool[...] = jnp.zeros_like(pool)
    add_rows(act_ref.shape[0], 64, lambda r: self_ref[0, r], act_ref, pools)
    add_rows(levels * slots, 64, lambda r: keys_ref[0, r], rows, pools)
    coarse = jnp.zeros(coarse_ref.shape, F32)
    for o in range(noct):
        part = pl.ds(o * ndev, ndev)
        total = pools[0][part, :]
        for pool in pools[1:]:
            total = total + pool[part, :]
        pooled = total.astype(BF16)
        coarse = coarse + lax.dot_general(
            weight_ref[o], pooled, (((1,), (1,)), ((), ())), preferred_element_type=F32
        )
        down = jnp.dot(grad_ref[...], pooled, preferred_element_type=F32)
        down_ref[o] = down[:, :chans]
    coarse_ref[...] = coarse.astype(BF16)


def scatter_kernel(levels, halo, stages, index_ref, grad_ref, weight_ref, local_ref, *refs):
    backs = refs[:levels]
    buf0, buf1 = refs[levels : levels + 2]
    stores = refs[levels + 2 : levels + 2 + stages]
    tables = refs[levels + 2 + stages : -1]
    sems = refs[-1]
    bufs = (buf0, buf1)
    vdev = local_ref.shape[0]
    chunk = buf0.shape[0]
    lanes = len(tables)
    k = pl.program_id(0)
    last = pl.num_programs(0) - 1

    def ready(base, offset, buf):
        buf[...] = jnp.dot(grad_ref[pl.ds(base, chunk), :], weight_ref[offset], preferred_element_type=F32)

    @pl.when(k == 0)
    def _():
        for table in tables:
            table[...] = jnp.zeros_like(table)
        ready(0, 0, buf0)

    def step(base, parity, store, entry, first, turn):
        buf = bufs[parity]
        over = base + chunk == vdev
        ahead = pl.multiple_of(jnp.where(over, 0, base + chunk), chunk)
        ready(ahead, jnp.minimum(jnp.where(over, k + 1, k), last), bufs[1 - parity])
        for start in range(0, chunk, lanes):
            spots = [store[0, entry + start + j] for j in range(lanes)]
            sums = [tables[j][pl.ds(spots[j], 1), :] + buf[pl.ds(start + j, 1), :] for j in range(lanes)]
            for j in range(lanes):
                tables[j][pl.ds(spots[j], 1), :] = sums[j]

    walk(index_ref, stores, sems, vdev, chunk, step)

    @pl.when(k == last)
    def _():
        def total(part):
            result = tables[0][part, :]
            for table in tables[1:]:
                result = result + table[part, :]
            return result

        local_ref[...] = total(pl.ds(0, vdev))
        for level in range(levels):
            backs[level][...] = total(pl.ds(vdev + level * halo, halo)).astype(BF16)


def finish_kernel(levels, rows_ref, local_ref, *refs):
    incoming = refs[:levels]
    out_ref, rows = refs[levels : levels + 2]
    tables = refs[levels + 2 :]
    halo = incoming[0].shape[0]
    chans, vdev = out_ref.shape
    for level in range(levels):
        rows[pl.ds(level * halo, halo), :] = incoming[level][...].astype(F32)
    for table in tables:
        table[...] = jnp.zeros_like(table)
    add_rows(levels * halo, 64, lambda r: rows_ref[0, r], rows, tables)
    for c in range(vdev // LANES):
        part = pl.ds(c * LANES, LANES)
        total = local_ref[part, :]
        for table in tables:
            total = total + table[part, :]
        out_ref[:, part] = total.T[:chans]


def shape(dims, dtype):
    return jax.ShapeDtypeStruct(dims, dtype)


def params():
    return pltpu.CompilerParams(vmem_limit_bytes=56 << 20)


def shards(feats, kmap, send_rows, w_sub, owner, coarse_id, octant, w_down, grad_coarse):
    chans, vdev = feats.shape
    _, levels, halo = send_rows.shape
    kvol = kmap.shape[0]
    noct, c2, _ = w_down.shape
    coarse_dev = grad_coarse.shape[1]
    keys = noct * coarse_dev
    slots = vdev // 32
    bits_member = lax.axis_size("member").bit_length() - 1
    myself = lax.axis_index(("group", "member")).astype(I32).reshape(1)
    lane_pad = LANES - chans
    outgoing = send_rows.reshape(1, levels * halo)
    table_rows = vdev + levels * halo + SUB
    index = kmap.reshape(kvol, 1, vdev)

    w_backward = jnp.pad(w_sub, ((0, 0), (0, lane_pad), (0, lane_pad)))
    w_forward = w_backward.transpose(0, 2, 1)
    down_pad = jnp.pad(w_down, ((0, 0), (0, 0), (0, lane_pad)))

    prepared = pl.pallas_call(
        functools.partial(prepare_kernel, levels, noct=noct, coarse_dev=coarse_dev, slots=slots),
        in_specs=[pl.BlockSpec(memory_space=SMEM), smem_full((1, levels * halo))]
        + [vmem_full((1, vdev))] * 3
        + [vmem_full((chans, vdev))],
        out_specs=[vmem_full((halo + 2 * SUB, LANES))] * levels
        + [vmem_full((vdev, LANES)), vmem_full((1, vdev)), vmem_full((1, levels * slots))],
        out_shape=[shape((halo + 2 * SUB, LANES), BF16)] * levels
        + [shape((vdev, LANES), F32), shape((1, vdev), I32), shape((1, levels * slots), I32)],
        scratch_shapes=[pltpu.VMEM((1, vdev), I32), pltpu.VMEM((levels * halo, LANES), F32)],
        compiler_params=params(),
        name="prepare",
    )(myself, outgoing, owner.reshape(1, vdev), coarse_id.reshape(1, vdev), octant.reshape(1, vdev), feats)
    messages = prepared[:levels]
    table, own_key, send_list = prepared[levels:]
    received = [from_partner(messages[level], level, bits_member) for level in range(levels)]

    wide, rows = pl.pallas_call(
        parents_kernel,
        in_specs=[smem_full((1, vdev)), vmem_full((coarse_dev, c2)), vmem_full((noct, c2, LANES))],
        out_specs=[vmem_full((keys + SUB, LANES)), vmem_full((vdev, LANES))],
        out_shape=[shape((keys + SUB, LANES), F32), shape((vdev, LANES), F32)],
        compiler_params=params(),
        name="parents",
    )(own_key, grad_coarse.T, down_pad)

    digits = jnp.stack([got[halo : halo + 2] for got in received]).astype(F32)
    got_keys = (digits[:, 0] * DIGIT + digits[:, 1]).astype(I32).reshape(1, levels * slots)
    answers = pl.pallas_call(
        functools.partial(answer_kernel, levels),
        in_specs=[smem_full((1, levels * slots)), vmem_full((keys + SUB, LANES))],
        out_specs=[vmem_full((slots, LANES))] * levels,
        out_shape=[shape((slots, LANES), BF16)] * levels,
        scratch_shapes=[pltpu.VMEM((levels * slots, LANES), F32)],
        compiler_params=params(),
        name="answer",
    )(got_keys, wide)
    returned = [from_partner(answers[level], level, bits_member) for level in range(levels)]

    stages, width, chunk = 4, 512, 256
    staging = [pltpu.SMEM((1, width), I32)] * stages
    gathered, pre = pl.pallas_call(
        functools.partial(gather_kernel, levels, halo),
        grid=(kvol,),
        in_specs=[
            pl.BlockSpec(memory_space=pl.ANY),
            vmem_full((vdev, LANES)),
            pl.BlockSpec((1, LANES, LANES), lambda k: (k, 0, 0)),
        ]
        + [vmem_full((halo + 2 * SUB, LANES))] * levels,
        out_specs=[pl.BlockSpec((vdev, LANES), lambda k: (0, k)), vmem_full((vdev, LANES))],
        out_shape=[shape((vdev, kvol * LANES), BF16), shape((vdev, LANES), F32)],
        scratch_shapes=[pltpu.VMEM((table_rows, LANES), F32)]
        + [pltpu.VMEM((chunk, LANES), F32)] * 2
        + staging
        + [pltpu.SemaphoreType.DMA((stages,))],
        compiler_params=params(),
        cost_estimate=pl.CostEstimate(flops=0, bytes_accessed=300_000_000, transcendentals=0),
        name="gather",
    )(index, table, w_forward, *received)

    middle = pl.pallas_call(
        functools.partial(middle_kernel, levels),
        in_specs=[smem_full((1, levels * slots))]
        + [vmem_full((vdev, LANES))] * 2
        + [vmem_full((slots, LANES))] * levels,
        out_specs=[vmem_full((vdev, LANES)), vmem_full((LANES, vdev)), vmem_full((vdev, LANES))]
        + [vmem_full((slots, LANES))] * levels,
        out_shape=[shape((vdev, LANES), BF16), shape((LANES, vdev), BF16), shape((vdev, LANES), F32)]
        + [shape((slots, LANES), BF16)] * levels,
        scratch_shapes=[
            pltpu.VMEM((vdev + SUB, LANES), F32),
            pltpu.VMEM((levels * slots, LANES), F32),
            pltpu.VMEM((vdev + SUB, LANES), F32),
            pltpu.VMEM((levels * slots, LANES), F32),
        ],
        compiler_params=params(),
        name="middle",
    )(send_list, pre, rows, *returned)
    grad_pre, grad_turned, act = middle[:3]
    came = [from_partner(middle[3 + level], level, bits_member) for level in range(levels)]

    group = 3
    grad_w = pl.pallas_call(
        weights_kernel,
        grid=(kvol // group,),
        in_specs=[vmem_full((LANES, vdev)), pl.BlockSpec((vdev, group * LANES), lambda k: (0, k))],
        out_specs=pl.BlockSpec((group, chans, chans), lambda k: (k, 0, 0)),
        out_shape=shape((kvol, chans, chans), F32),
        compiler_params=params(),
        cost_estimate=pl.CostEstimate(flops=0, bytes_accessed=40_000_000, transcendentals=0),
        name="weights",
    )(grad_turned, gathered)

    coarse_out, grad_down = pl.pallas_call(
        functools.partial(pool_kernel, levels),
        in_specs=[
            smem_full((1, levels * slots)),
            smem_full((1, vdev)),
            vmem_full((vdev, LANES)),
            vmem_full((c2, coarse_dev)),
            vmem_full((noct, c2, LANES)),
        ]
        + [vmem_full((slots, LANES))] * levels,
        out_specs=[vmem_full((c2, coarse_dev)), vmem_full((noct, c2, chans))],
        out_shape=[shape((c2, coarse_dev), BF16), shape((noct, c2, chans), F32)],
        scratch_shapes=[pltpu.VMEM((levels * slots, LANES), F32)]
        + [pltpu.VMEM((keys + SUB, LANES), F32)] * 8,
        compiler_params=params(),
        name="pool",
    )(got_keys, own_key, act, grad_coarse, down_pad, *came)

    grad_w, grad_down, grad_pre = lax.optimization_barrier((grad_w, grad_down, grad_pre))
    grad_w, grad_down = lax.psum((grad_w, grad_down), ("group", "member"))

    accumulators = 8
    scattered = pl.pallas_call(
        functools.partial(scatter_kernel, levels, halo, stages),
        grid=(kvol,),
        in_specs=[
            pl.BlockSpec(memory_space=pl.ANY),
            vmem_full((vdev, LANES)),
            vmem_full((kvol, LANES, LANES)),
        ],
        out_specs=[vmem_full((vdev, LANES))] + [vmem_full((halo, LANES))] * levels,
        out_shape=[shape((vdev, LANES), F32)] + [shape((halo, LANES), BF16)] * levels,
        scratch_shapes=[pltpu.VMEM((chunk, LANES), F32)] * 2
        + staging
        + [pltpu.VMEM((table_rows, LANES), F32)] * accumulators
        + [pltpu.SemaphoreType.DMA((stages,))],
        compiler_params=params(),
        cost_estimate=pl.CostEstimate(flops=0, bytes_accessed=400_000_000, transcendentals=0),
        name="scatter",
    )(index, grad_pre, w_backward)
    incoming = [from_partner(scattered[1 + level], level, bits_member) for level in range(levels)]

    grad_feats = pl.pallas_call(
        functools.partial(finish_kernel, levels),
        in_specs=[smem_full((1, levels * halo)), vmem_full((vdev, LANES))] + [vmem_full((halo, LANES))] * levels,
        out_specs=vmem_full((chans, vdev)),
        out_shape=shape((chans, vdev), F32),
        scratch_shapes=[pltpu.VMEM((levels * halo, LANES), F32)] + [pltpu.VMEM((vdev, LANES), F32)] * 4,
        compiler_params=params(),
        name="finish",
    )(outgoing, scattered[0], *incoming)
    return coarse_out, grad_feats, grad_w, grad_down


def solution(mesh):
    both = ("group", "member")
    in_specs = (
        P(None, both),
        P(None, both),
        P(both, None, None),
        P(),
        P(both, None),
        P(both),
        P(both),
        P(),
        P(None, both),
    )
    out_specs = (P(None, both), P(None, both), P(), P())
    return jax.shard_map(shards, mesh=mesh, in_specs=in_specs, out_specs=out_specs, check_vma=False)
```

time: 398 us -> 370 us (0.930)
  matrix products: 50.9 us -> 0 us
  waiting for transfers between devices: 33.1 us -> 47.4 us
  Pallas kernels: 245 us -> 257 us
  starting transfers between devices: 41 us -> 36 us
    dot_general x3 -> x0, matrix products: 50.9 us -> none  [the longest x1 21.6 us: shards(): terms = jnp.dot(grad_pre, w_backward, preferred_element_type=F32)]
    psum x1, waiting for transfers between devices: 22.8 us -> 33.9 us  [shards(): grad_w, grad_down = lax.psum((grad_w, grad_down), ('group', 'member'))]
    pallas_call x1, Pallas kernels: 99.3 us -> 109 us  [shards(): pl.pallas_call(functools.partial(gather_kernel, levels, halo), grid=(kvol...]
    ppermute x28, starting transfers between devices: 40.9 us -> 35.9 us  [from_partner(): return lax.ppermute(value, axis, pairs)]
    pallas_call x4 -> x6, Pallas kernels: 134 us -> 132 us  [the longest x1 93.9 us: shards(): pl.pallas_call(functools.partial(scatter_kernel, levels, halo, stages), g...]
  transfers between devices with their start and end apart: 29 -> 29, of which waited for: 8 -> 10; matrix products, arithmetic and copies ran while one was open for 14% -> 2% of each run, Pallas kernels for 53% -> 63%
where the time goes in v2:
time: 370 us; the launch traced here: 369 us
  Pallas kernels  257 us (69%)
  waiting for transfers between devices  47.4 us (13%)
  starting transfers between devices  36 us (10%)
  between operations  14.4 us (4%)
  local copies, waits for them, and re-layouts  13.2 us (4%)
    pallas_call x1, Pallas kernels, shards(): pl.pallas_call(functools.partial(gather_kernel, levels, halo), grid=(kvol...  109 us
    pallas_call x1, Pallas kernels, shards(): pl.pallas_call(functools.partial(scatter_kernel, levels, halo, stages), g...  93.9 us
    ppermute x28, starting transfers between devices, from_partner(): return lax.ppermute(value, axis, pairs)  35.9 us
    psum x1, waiting for transfers between devices, shards(): grad_w, grad_down = lax.psum((grad_w, grad_down), ('group', 'member'))  33.9 us
    pallas_call x1, Pallas kernels, shards(): pl.pallas_call(weights_kernel, grid=(kvol // group,), in_specs=[vmem_full...  14.7 us
    ppermute x28, waiting for transfers between devices, from_partner(): return lax.ppermute(value, axis, pairs)  13.5 us
    pallas_call x1, Pallas kernels, shards(): pl.pallas_call(functools.partial(pool_kernel, levels), in_specs=[smem_ful...  9.45 us
  transfers between devices with their start and end apart: 29, of which 10 were waited for; matrix products, arithmetic and copies ran while one was open for 2% of the time, Pallas kernels for 63%

profile of v2, /device:TPU:0, one launch (start us, length us, event | category | flops | bytes accessed | tf_op | source)
XLA Modules:
  0.0 369.0 jit_solution(9868432332194176098)
XLA Ops:
  7.2 6.0 %prepare.1 = (bf16[272,128]{1,0:T(8,128)(2,1)}, bf16[272,128]{1,0:T(8,128)(2,1)}, bf16[272,128]{1,0:T(8,128)(2,1)}, bf16[272,128]{1,0:T(8,128)(2,1)}, bf16[272,1...) custom-call(s32[1]{0:T(128)} %bitcast.me_ref, ...), custom_call_target="tpu_custom_call" | custom-call | tf_op jit(solution)/shard_map/prepare/pallas_call | solution.py:387
  13.2 1.7 collective-permute-start
  14.9 2.7 collective-permute-start.1
  17.6 1.9 collective-permute-start.2
  19.5 3.6 collective-permute-start.3
  23.1 1.8 copy.14
  24.9 1.8 pad.9.weight_ref
  26.7 7.3 %parents.1 = (f32[4104,128]{1,0:T(8,128)}, f32[4096,128]{1,0:T(8,128)}) custom-call(s32[1,4096]{1,0:T(1,128)} %get-tuple-element.55.self_ref, bf16[512,192]{1,0:T(8,128)(2,1)} %bitcast.38, bf16[8,192,128]{2,1,0:T(8,128)(2,1)} %pad.9.weight_ref), custom_call_target="tpu_custom_call" | custom-call | tf_op jit(solution)/shard_map/parents/pallas_call | solution.py:404
  34.1 1.6 collective-permute-start.5
  35.6 2.9 collective-permute-start.6
  38.9 3.9 %collective-permute-done.6.refs_6_ = bf16[272,128]{1,0:T(8,128)(2,1)S(1)} collective-permute-done((bf16[272,128]{1,0:T(8,128)(2,1)}, bf16[272,128]{1,0:T(8,128)(2,1)S(1)}, u32[]{:S(2)}, u32[]{:S(2)}) %collective-permute-start.6) | collective-permute-done | bytes 69664 | tf_op jit(solution)/shard_map/ppermute | solution.py:23
  43.4 3.1 answer.1
  46.8 1.7 collective-permute-start.8
  49.2 1.5 collective-permute-done.7.refs_0_
  50.8 1.6 collective-permute-done.8.refs_1_
  52.4 1.8 collective-permute-start.13
  56.9 1.6 copy.13.weight_ref
  58.5 109.3 %gather.1 = (bf16[4096,3456]{1,0:T(8,128)(2,1)}, f32[4096,128]{1,0:T(8,128)}) custom-call(s32[27,1,4096]{2,1,0:T(1,128)} %reshape.59.index_ref, f32[4096,128]{1,0:T(8,128)} %get-tuple-element.57.local_ref, bf16[27,128,128]{2,1,0:T(8,128)(2,1)} %copy.13.weight_ref, bf16[272,128]{1,0:T(8,128)(2,1)} %copy-done.3, bf16[272,128]{1,0:T(8,128)(2,1)} %copy-done.4, ...), custom_call_target="tpu_custom_call" | custom-call | bytes 300000000 | tf_op jit(solution)/shard_map/gather/pallas_call | solution.py:428
  168.6 7.2 %middle.1 = (bf16[4096,128]{1,0:T(8,128)(2,1)}, bf16[128,4096]{1,0:T(8,128)(2,1)}, f32[4096,128]{1,0:T(8,128)}, bf16[128,128]{1,0:T(8,128)(2,1)}, bf16[128,128]{...) custom-call(s32[1,896]{1,0:T(1,128)} %get-tuple-element.56.list_ref,, ...), custom_call_target="tpu_custom_call" | custom-call | tf_op jit(solution)/shard_map/middle/pallas_call | solution.py:448
  175.8 1.8 collective-permute-start.14
  179.0 4.1 %collective-permute-start.17 = (bf16[128,128]{1,0:T(8,128)(2,1)}, bf16[128,128]{1,0:T(8,128)(2,1)S(1)}, u32[]{:S(2)}, u32[]{:S(2)}) collective-permute-start(bf16[128,128]{1,0:T(8,128)(2,1)} %get-tuple-element.72), channel_id=1, source_target_pairs={{0,8},{1,9},{2,10},{3,11},{4,12},{5,13},{6,14},{7,15},{8,0},{9,1},... | collective-permute-start | bytes 98312 | tf_op jit(solution)/shard_map/ppermute | solution.py:23
  183.9 3.0 collective-permute-start.20
  186.9 14.7 %weights.1 = f32[27,96,96]{2,1,0:T(8,128)} custom-call(bf16[128,4096]{1,0:T(8,128)(2,1)} %get-tuple-element.77.turned_ref, bf16[4096,3456]{1,0:T(8,128)(2,1)} %get-tuple-element.78.taken_ref), custom_call_target="tpu_custom_call" | custom-call | bytes 40000000 | tf_op jit(solution)/shard_map/weights/pallas_call | solution.py:470
  202.2 9.4 %pool.1 = (bf16[192,512]{1,0:T(8,128)(2,1)}, f32[8,192,96]{2,1,0:T(8,128)}) custom-call(s32[1,896]{1,0:T(1,128)} %fusion.1.keys_ref, s32[1,4096]{1,0:T(1,128)} %get-tuple-element.55.self_ref, f32[4096,128]{1,0:T(8,128)} %get-tuple-element.68.act_ref, bf16[192,512]{1,0:T(8,128)(2,1)} %grad_ref.1, bf16[8,192,128]{2,1,0:T(8,128)(2,1)} %pad.9.weight_ref, ...), custom_call_target="tpu_custom_call" | custom-call | tf_op jit(solution)/shard_map/pool/pallas_call | solution.py:481
  211.7 93.9 %scatter.1 = (f32[4096,128]{1,0:T(8,128)}, bf16[256,128]{1,0:T(8,128)(2,1)}, bf16[256,128]{1,0:T(8,128)(2,1)}, bf16[256,128]{1,0:T(8,128)(2,1)}, bf16[256,128]{1...) custom-call(s32[27,1,4096]{2,1,0:T(1,128)} %reshape.59.index_ref, ...), custom_call_target="tpu_custom_call" | custom-call | bytes 400000000 | tf_op jit(solution)/shard_map/scatter/pallas_call | solution.py:503
  305.7 2.0 collective-permute-start.22
  307.7 2.0 collective-permute-start.24
  313.7 1.8 collective-permute-done.26.refs_5_
  315.5 2.3 collective-permute-done.27.refs_6_
  318.4 6.4 %finish.1 = f32[96,4096]{1,0:T(8,128)} custom-call(s32[1,1792]{1,0:T(1,128)} %bitcast.40, f32[4096,128]{1,0:T(8,128)} %get-tuple-element.82.local_ref, bf16[256,128]{1,0:T(8,128)(2,1)} %copy-done.10, bf16[256,128]{1,0:T(8,128)(2,1)} %copy-done.11, bf16[256,128]{1,0:T(8,128)(2,1)} %copy-done.12, bf16[256,128]{1,0:T(8,128)(2,1)} %copy-done.13, ...), custom_call_target="tpu_custom_call" | custom-call | tf_op jit(solution)/shard_map/finish/pallas_call | solution.py:523
  324.9 33.9 %all-reduce.5.cloned.1.call-done = (f32[27,96,96]{2,1,0:T(8,128)}, f32[8,192,96]{2,1,0:T(8,128)}) async-done(((f32[27,96,96]{2,1,0:T(8,128)}, f32[8,192,96]{2,1,0:T(8,128)}), (f32[27,96,96]{2,1,0:T(8,128)}, f32[8,192,96]{2,1,0:T(8,128)})) %all-reduce.5.cloned.1.call-update) | async-done | bytes 1585168 | tf_op jit(solution)/shard_map/psum | solution.py:500
  358.8 2.5 copy.23
  (114 shorter events, 13.7 us)
Async XLA Ops:
  7.2 351.6 %all-reduce.5.cloned.1.call-start = ((), (), s32[]{:S(2)}) async-start(), calls=%async_computation | async-start | bytes 4227072 | tf_op jit(solution)/shard_map/psum | solution.py:500
  13.2 40.9 %copy-start.1 = (bf16[27,96,96]{2,1,0:T(8,128)(2,1)S(1)}, bf16[27,96,96]{2,1,0:T(8,128)(2,1)}, u32[]{:S(2)}) copy-start(bf16[27,96,96]{2,1,0:T(8,128)(2,1)} %param.12) | copy-start | bytes 1492996
  13.2 20.8 %collective-permute-start = (bf16[272,128]{1,0:T(8,128)(2,1)}, bf16[272,128]{1,0:T(8,128)(2,1)S(1)}, u32[]{:S(2)}, u32[]{:S(2)}) collective-permute-start(bf16[272,128]{1,0:T(8,128)(2,1)} %get-tuple-element.48), channel_id=1, source_target_pairs={{0,1},{1,0},{2,3},{3,2},{4,5},{5,4},{6,7},{7,6},{8,9},{9,8},{10,11... | collective-permute-start | bytes 208904 | tf_op jit(solution)/shard_map/ppermute | solution.py:23
  14.9 20.7 %collective-permute-start.1 = (bf16[272,128]{1,0:T(8,128)(2,1)}, bf16[272,128]{1,0:T(8,128)(2,1)S(1)}, u32[]{:S(2)}, u32[]{:S(2)}) collective-permute-start(bf16[272,128]{1,0:T(8,128)(2,1)} %get-tuple-element.49), channel_id=1, source_target_pairs={{0,2},{1,3},{2,0},{3,1},{4,6},{5,7},{6,4},{7,5},{8,10},{9,11},{10,... | collective-permute-start | bytes 208904 | tf_op jit(solution)/shard_map/ppermute | solution.py:23
  17.6 20.9 %collective-permute-start.2 = (bf16[272,128]{1,0:T(8,128)(2,1)}, bf16[272,128]{1,0:T(8,128)(2,1)S(1)}, u32[]{:S(2)}, u32[]{:S(2)}) collective-permute-start(bf16[272,128]{1,0:T(8,128)(2,1)} %get-tuple-element.50), channel_id=1, source_target_pairs={{0,4},{1,5},{2,6},{3,7},{4,0},{5,1},{6,2},{7,3},{8,12},{9,13},{10,... | collective-permute-start | bytes 208904 | tf_op jit(solution)/shard_map/ppermute | solution.py:23
  19.5 19.0 %collective-permute-start.3 = (bf16[272,128]{1,0:T(8,128)(2,1)}, bf16[272,128]{1,0:T(8,128)(2,1)S(1)}, u32[]{:S(2)}, u32[]{:S(2)}) collective-permute-start(bf16[272,128]{1,0:T(8,128)(2,1)} %get-tuple-element.51), channel_id=1, source_target_pairs={{0,8},{1,9},{2,10},{3,11},{4,12},{5,13},{6,14},{7,15},{8,0},{9,1},... | collective-permute-start | bytes 208904 | tf_op jit(solution)/shard_map/ppermute | solution.py:23
  23.1 15.5 %collective-permute-start.4 = (bf16[272,128]{1,0:T(8,128)(2,1)}, bf16[272,128]{1,0:T(8,128)(2,1)S(1)}, u32[]{:S(2)}, u32[]{:S(2)}) collective-permute-start(bf16[272,128]{1,0:T(8,128)(2,1)} %get-tuple-element.52), channel_id=1, source_target_pairs={{0,16},{16,0},{32,48},{48,32},{64,80},{80,64},{96,112},{112,96},{1... | collective-permute-start | bytes 208904 | tf_op jit(solution)/shard_map/ppermute | solution.py:23
  34.1 21.5 %copy-start.3 = (bf16[272,128]{1,0:T(8,128)(2,1)}, bf16[272,128]{1,0:T(8,128)(2,1)S(1)}, u32[]{:S(2)}) copy-start(bf16[272,128]{1,0:T(8,128)(2,1)S(1)} %collective-permute-done.refs_0_) | copy-start | bytes 208900
  34.1 4.8 %collective-permute-start.5 = (bf16[272,128]{1,0:T(8,128)(2,1)}, bf16[272,128]{1,0:T(8,128)(2,1)S(1)}, u32[]{:S(2)}, u32[]{:S(2)}) collective-permute-start(bf16[272,128]{1,0:T(8,128)(2,1)} %get-tuple-element.53), channel_id=1, source_target_pairs={{0,32},{16,48},{32,0},{48,16},{64,96},{80,112},{96,64},{112,80},{1... | collective-permute-start | bytes 208904 | tf_op jit(solution)/shard_map/ppermute | solution.py:23
  35.6 19.9 %copy-start.4 = (bf16[272,128]{1,0:T(8,128)(2,1)}, bf16[272,128]{1,0:T(8,128)(2,1)S(1)}, u32[]{:S(2)}) copy-start(bf16[272,128]{1,0:T(8,128)(2,1)S(1)} %collective-permute-done.1.refs_1_) | copy-start | bytes 208900
  35.6 7.2 %collective-permute-start.6 = (bf16[272,128]{1,0:T(8,128)(2,1)}, bf16[272,128]{1,0:T(8,128)(2,1)S(1)}, u32[]{:S(2)}, u32[]{:S(2)}) collective-permute-start(bf16[272,128]{1,0:T(8,128)(2,1)} %get-tuple-element.54), channel_id=1, source_target_pairs={{0,64},{16,80},{32,96},{48,112},{64,0},{80,16},{96,32},{112,48},{1... | collective-permute-start | bytes 208904 | tf_op jit(solution)/shard_map/ppermute | solution.py:23
  46.6 4.1 %collective-permute-start.7 = (bf16[128,128]{1,0:T(8,128)(2,1)}, bf16[128,128]{1,0:T(8,128)(2,1)S(1)}, u32[]{:S(2)}, u32[]{:S(2)}) collective-permute-start(bf16[128,128]{1,0:T(8,128)(2,1)} %get-tuple-element.61), channel_id=1, source_target_pairs={{0,1},{1,0},{2,3},{3,2},{4,5},{5,4},{6,7},{7,6},{8,9},{9,8},{10,11... | collective-permute-start | bytes 98312 | tf_op jit(solution)/shard_map/ppermute | solution.py:23
  46.8 5.6 %collective-permute-start.8 = (bf16[128,128]{1,0:T(8,128)(2,1)}, bf16[128,128]{1,0:T(8,128)(2,1)S(1)}, u32[]{:S(2)}, u32[]{:S(2)}) collective-permute-start(bf16[128,128]{1,0:T(8,128)(2,1)} %get-tuple-element.62), channel_id=1, source_target_pairs={{0,2},{1,3},{2,0},{3,1},{4,6},{5,7},{6,4},{7,5},{8,10},{9,11},{10,... | collective-permute-start | bytes 98312 | tf_op jit(solution)/shard_map/ppermute | solution.py:23
  48.5 119.4 %collective-permute-start.9 = (bf16[128,128]{1,0:T(8,128)(2,1)}, bf16[128,128]{1,0:T(8,128)(2,1)S(1)}, u32[]{:S(2)}, u32[]{:S(2)}) collective-permute-start(bf16[128,128]{1,0:T(8,128)(2,1)} %get-tuple-element.63), channel_id=1, source_target_pairs={{0,4},{1,5},{2,6},{3,7},{4,0},{5,1},{6,2},{7,3},{8,12},{9,13},{10,... | collective-permute-start | bytes 98312 | tf_op jit(solution)/shard_map/ppermute | solution.py:23
  48.5 119.4 %collective-permute-start.10 = (bf16[128,128]{1,0:T(8,128)(2,1)}, bf16[128,128]{1,0:T(8,128)(2,1)S(1)}, u32[]{:S(2)}, u32[]{:S(2)}) collective-permute-start(bf16[128,128]{1,0:T(8,128)(2,1)} %get-tuple-element.64), channel_id=1, source_target_pairs={{0,8},{1,9},{2,10},{3,11},{4,12},{5,13},{6,14},{7,15},{8,0},{9,1},... | collective-permute-start | bytes 98312 | tf_op jit(solution)/shard_map/ppermute | solution.py:23
  49.2 118.8 %collective-permute-start.11 = (bf16[128,128]{1,0:T(8,128)(2,1)}, bf16[128,128]{1,0:T(8,128)(2,1)S(1)}, u32[]{:S(2)}, u32[]{:S(2)}) collective-permute-start(bf16[128,128]{1,0:T(8,128)(2,1)} %get-tuple-element.65), channel_id=1, source_target_pairs={{0,16},{16,0},{32,48},{48,32},{64,80},{80,64},{96,112},{112,96},{1... | collective-permute-start | bytes 98312 | tf_op jit(solution)/shard_map/ppermute | solution.py:23
  50.7 117.2 %collective-permute-start.12 = (bf16[128,128]{1,0:T(8,128)(2,1)}, bf16[128,128]{1,0:T(8,128)(2,1)S(1)}, u32[]{:S(2)}, u32[]{:S(2)}) collective-permute-start(bf16[128,128]{1,0:T(8,128)(2,1)} %get-tuple-element.66), channel_id=1, source_target_pairs={{0,32},{16,48},{32,0},{48,16},{64,96},{80,112},{96,64},{112,80},{1... | collective-permute-start | bytes 98312 | tf_op jit(solution)/shard_map/ppermute | solution.py:23
  52.4 115.5 %collective-permute-start.13 = (bf16[128,128]{1,0:T(8,128)(2,1)}, bf16[128,128]{1,0:T(8,128)(2,1)S(1)}, u32[]{:S(2)}, u32[]{:S(2)}) collective-permute-start(bf16[128,128]{1,0:T(8,128)(2,1)} %get-tuple-element.67), channel_id=1, source_target_pairs={{0,64},{16,80},{32,96},{48,112},{64,0},{80,16},{96,32},{112,48},{1... | collective-permute-start | bytes 98312 | tf_op jit(solution)/shard_map/ppermute | solution.py:23
  175.8 7.3 %collective-permute-start.14 = (bf16[128,128]{1,0:T(8,128)(2,1)}, bf16[128,128]{1,0:T(8,128)(2,1)S(1)}, u32[]{:S(2)}, u32[]{:S(2)}) collective-permute-start(bf16[128,128]{1,0:T(8,128)(2,1)} %get-tuple-element.69), channel_id=1, source_target_pairs={{0,1},{1,0},{2,3},{3,2},{4,5},{5,4},{6,7},{7,6},{8,9},{9,8},{10,11... | collective-permute-start | bytes 98312 | tf_op jit(solution)/shard_map/ppermute | solution.py:23
  177.6 6.3 %collective-permute-start.15 = (bf16[128,128]{1,0:T(8,128)(2,1)}, bf16[128,128]{1,0:T(8,128)(2,1)S(1)}, u32[]{:S(2)}, u32[]{:S(2)}) collective-permute-start(bf16[128,128]{1,0:T(8,128)(2,1)} %get-tuple-element.70), channel_id=1, source_target_pairs={{0,2},{1,3},{2,0},{3,1},{4,6},{5,7},{6,4},{7,5},{8,10},{9,11},{10,... | collective-permute-start | bytes 98312 | tf_op jit(solution)/shard_map/ppermute | solution.py:23
  178.5 23.0 %collective-permute-start.16 = (bf16[128,128]{1,0:T(8,128)(2,1)}, bf16[128,128]{1,0:T(8,128)(2,1)S(1)}, u32[]{:S(2)}, u32[]{:S(2)}) collective-permute-start(bf16[128,128]{1,0:T(8,128)(2,1)} %get-tuple-element.71), channel_id=1, source_target_pairs={{0,4},{1,5},{2,6},{3,7},{4,0},{5,1},{6,2},{7,3},{8,12},{9,13},{10,... | collective-permute-start | bytes 98312 | tf_op jit(solution)/shard_map/ppermute | solution.py:23
  179.0 22.6 %collective-permute-start.17 = (bf16[128,128]{1,0:T(8,128)(2,1)}, bf16[128,128]{1,0:T(8,128)(2,1)S(1)}, u32[]{:S(2)}, u32[]{:S(2)}) collective-permute-start(bf16[128,128]{1,0:T(8,128)(2,1)} %get-tuple-element.72), channel_id=1, source_target_pairs={{0,8},{1,9},{2,10},{3,11},{4,12},{5,13},{6,14},{7,15},{8,0},{9,1},... | collective-permute-start | bytes 98312 | tf_op jit(solution)/shard_map/ppermute | solution.py:23
  183.1 18.5 %collective-permute-start.18 = (bf16[128,128]{1,0:T(8,128)(2,1)}, bf16[128,128]{1,0:T(8,128)(2,1)S(1)}, u32[]{:S(2)}, u32[]{:S(2)}) collective-permute-start(bf16[128,128]{1,0:T(8,128)(2,1)} %get-tuple-element.73), channel_id=1, source_target_pairs={{0,16},{16,0},{32,48},{48,32},{64,80},{80,64},{96,112},{112,96},{1... | collective-permute-start | bytes 98312 | tf_op jit(solution)/shard_map/ppermute | solution.py:23
  183.1 18.5 %collective-permute-start.19 = (bf16[128,128]{1,0:T(8,128)(2,1)}, bf16[128,128]{1,0:T(8,128)(2,1)S(1)}, u32[]{:S(2)}, u32[]{:S(2)}) collective-permute-start(bf16[128,128]{1,0:T(8,128)(2,1)} %get-tuple-element.74), channel_id=1, source_target_pairs={{0,32},{16,48},{32,0},{48,16},{64,96},{80,112},{96,64},{112,80},{1... | collective-permute-start | bytes 98312 | tf_op jit(solution)/shard_map/ppermute | solution.py:23
  183.9 17.7 %collective-permute-start.20 = (bf16[128,128]{1,0:T(8,128)(2,1)}, bf16[128,128]{1,0:T(8,128)(2,1)S(1)}, u32[]{:S(2)}, u32[]{:S(2)}) collective-permute-start(bf16[128,128]{1,0:T(8,128)(2,1)} %get-tuple-element.75), channel_id=1, source_target_pairs={{0,64},{16,80},{32,96},{48,112},{64,0},{80,16},{96,32},{112,48},{1... | collective-permute-start | bytes 98312 | tf_op jit(solution)/shard_map/ppermute | solution.py:23
  305.6 4.9 %collective-permute-start.21 = (bf16[256,128]{1,0:T(8,128)(2,1)}, bf16[256,128]{1,0:T(8,128)(2,1)S(1)}, u32[]{:S(2)}, u32[]{:S(2)}) collective-permute-start(bf16[256,128]{1,0:T(8,128)(2,1)} %get-tuple-element.83), channel_id=1, source_target_pairs={{0,1},{1,0},{2,3},{3,2},{4,5},{5,4},{6,7},{7,6},{8,9},{9,8},{10,11... | collective-permute-start | bytes 196616 | tf_op jit(solution)/shard_map/ppermute | solution.py:23
  305.7 6.1 %collective-permute-start.22 = (bf16[256,128]{1,0:T(8,128)(2,1)}, bf16[256,128]{1,0:T(8,128)(2,1)S(1)}, u32[]{:S(2)}, u32[]{:S(2)}) collective-permute-start(bf16[256,128]{1,0:T(8,128)(2,1)} %get-tuple-element.84), channel_id=1, source_target_pairs={{0,2},{1,3},{2,0},{3,1},{4,6},{5,7},{6,4},{7,5},{8,10},{9,11},{10,... | collective-permute-start | bytes 196616 | tf_op jit(solution)/shard_map/ppermute | solution.py:23
  307.7 5.6 %collective-permute-start.23 = (bf16[256,128]{1,0:T(8,128)(2,1)}, bf16[256,128]{1,0:T(8,128)(2,1)S(1)}, u32[]{:S(2)}, u32[]{:S(2)}) collective-permute-start(bf16[256,128]{1,0:T(8,128)(2,1)} %get-tuple-element.85), channel_id=1, source_target_pairs={{0,4},{1,5},{2,6},{3,7},{4,0},{5,1},{6,2},{7,3},{8,12},{9,13},{10,... | collective-permute-start | bytes 196616 | tf_op jit(solution)/shard_map/ppermute | solution.py:23
  307.7 6.0 %collective-permute-start.24 = (bf16[256,128]{1,0:T(8,128)(2,1)}, bf16[256,128]{1,0:T(8,128)(2,1)S(1)}, u32[]{:S(2)}, u32[]{:S(2)}) collective-permute-start(bf16[256,128]{1,0:T(8,128)(2,1)} %get-tuple-element.86), channel_id=1, source_target_pairs={{0,8},{1,9},{2,10},{3,11},{4,12},{5,13},{6,14},{7,15},{8,0},{9,1},... | collective-permute-start | bytes 196616 | tf_op jit(solution)/shard_map/ppermute | solution.py:23
  309.7 4.0 %collective-permute-start.25 = (bf16[256,128]{1,0:T(8,128)(2,1)}, bf16[256,128]{1,0:T(8,128)(2,1)S(1)}, u32[]{:S(2)}, u32[]{:S(2)}) collective-permute-start(bf16[256,128]{1,0:T(8,128)(2,1)} %get-tuple-element.87), channel_id=1, source_target_pairs={{0,16},{16,0},{32,48},{48,32},{64,80},{80,64},{96,112},{112,96},{1... | collective-permute-start | bytes 196616 | tf_op jit(solution)/shard_map/ppermute | solution.py:23
  310.5 5.0 %collective-permute-start.26 = (bf16[256,128]{1,0:T(8,128)(2,1)}, bf16[256,128]{1,0:T(8,128)(2,1)S(1)}, u32[]{:S(2)}, u32[]{:S(2)}) collective-permute-start(bf16[256,128]{1,0:T(8,128)(2,1)} %get-tuple-element.88), channel_id=1, source_target_pairs={{0,32},{16,48},{32,0},{48,16},{64,96},{80,112},{96,64},{112,80},{1... | collective-permute-start | bytes 196616 | tf_op jit(solution)/shard_map/ppermute | solution.py:23
  311.8 6.0 %collective-permute-start.27 = (bf16[256,128]{1,0:T(8,128)(2,1)}, bf16[256,128]{1,0:T(8,128)(2,1)S(1)}, u32[]{:S(2)}, u32[]{:S(2)}) collective-permute-start(bf16[256,128]{1,0:T(8,128)(2,1)} %get-tuple-element.89), channel_id=1, source_target_pairs={{0,64},{16,80},{32,96},{48,112},{64,0},{80,16},{96,32},{112,48},{1... | collective-permute-start | bytes 196616 | tf_op jit(solution)/shard_map/ppermute | solution.py:23
  (28 other events, 180.3 us)
Sparse Core Ops, SparseCore 0:
  211.8 146.8 all-reduce.4

commit v3 on v2

--- a/solution.py
+++ b/solution.py
@@ -143,7 +143,7 @@
         outs[level][...] = buf[pl.ds(level * slots, slots), :].astype(BF16)
 
 
-def index_copy(index_ref, spot, piece, store, sem, width):
+def index_copy(index_ref, piece, store, sem, width):
     pieces = index_ref.shape[2] // width
     row = lax.div(piece, pieces)
     start = pl.multiple_of(lax.rem(piece, pieces) * width, width)
@@ -160,29 +160,29 @@
     @pl.when(k == 0)
     def _():
         for b in range(many):
-            index_copy(index_ref, b, b, stores[b], sems.at[b], width).start()
+            index_copy(index_ref, b, stores[b], sems.at[b], width).start()
 
     def body(turn, _):
         for b in range(many):
             piece = k * pieces + turn * many + b
-            index_copy(index_ref, b, piece, stores[b], sems.at[b], width).wait()
+            index_copy(index_ref, piece, stores[b], sems.at[b], width).wait()
             for sub in range(width // chunk):
                 base = pl.multiple_of((turn * many + b) * width + sub * chunk, chunk)
-                step_of(base, sub % 2, stores[b], sub * chunk, b == 0 and sub == 0, turn)
+                step_of(base, (b * (width // chunk) + sub) % 2, stores[b], sub * chunk)
 
             @pl.when(piece + many < total * pieces)
             def _():
-                index_copy(index_ref, b, piece + many, stores[b], sems.at[b], width).start()
+                index_copy(index_ref, piece + many, stores[b], sems.at[b], width).start()
 
         return 0
 
     lax.fori_loop(0, pieces // many, body, 0)
 
 
-def gather_kernel(levels, halo, index_ref, local_ref, weight_ref, *refs):
+def gather_kernel(levels, halo, index_ref, local_ref, *refs):
     received = refs[:levels]
-    out_ref, pre_ref, table, buf0, buf1 = refs[levels : levels + 5]
-    stores = refs[levels + 5 : -1]
+    out_ref, table, buf0, buf1 = refs[levels : levels + 4]
+    stores = refs[levels + 4 : -1]
     sems = refs[-1]
     bufs = (buf0, buf1)
     vdev = local_ref.shape[0]
@@ -194,30 +194,17 @@
         for level in range(levels):
             table[pl.ds(vdev + level * halo, halo), :] = received[level][pl.ds(0, halo), :].astype(F32)
         table[pl.ds(vdev + levels * halo, SUB), :] = jnp.zeros((SUB, LANES), F32)
-        pre_ref[...] = jnp.zeros_like(pre_ref)
         buf1[...] = jnp.zeros_like(buf1)
 
-    def use(buf, base, live):
-        taken = buf[...].astype(BF16)
-        part = pl.ds(base, chunk)
-        out_ref[part, :] = taken
-        term = jnp.dot(taken, weight_ref[0], preferred_element_type=F32)
-        if live is not None:
-            term = term * live
-        pre_ref[part, :] += term
-
-    def step(base, parity, store, entry, first, turn):
+    def step(base, parity, store, entry):
         buf = bufs[parity]
         for j in range(chunk):
             buf[pl.ds(j, 1), :] = table[pl.ds(store[0, entry + j], 1), :]
-        if first:
-            behind = pl.multiple_of(jnp.maximum(base - chunk, 0), chunk)
-            use(bufs[1 - parity], behind, jnp.minimum(turn, 1).astype(F32))
-        else:
-            use(bufs[1 - parity], pl.multiple_of(base - chunk, chunk), None)
+        behind = pl.multiple_of(jnp.maximum(base - chunk, 0), chunk)
+        out_ref[pl.ds(behind, chunk), :] = bufs[1 - parity][...].astype(BF16)
 
     walk(index_ref, stores, sems, vdev, chunk, step)
-    use(buf1, vdev - chunk, None)
+    out_ref[pl.ds(vdev - chunk, chunk), :] = buf1[...].astype(BF16)
 
 
 def middle_kernel(levels, list_ref, pre_ref, rows_ref, *refs):
@@ -257,17 +244,38 @@
 
 def weights_kernel(turned_ref, taken_ref, out_ref):
     wide = jnp.dot(turned_ref[...], taken_ref[...], preferred_element_type=F32)
-    many, rows, cols = out_ref.shape
+    many = wide.shape[1] // LANES
+    rows = out_ref.shape[0] // many
     for j in range(many):
-        out_ref[j] = wide[:rows, j * LANES : j * LANES + cols]
-
-
-def pool_kernel(levels, keys_ref, self_ref, act_ref, grad_ref, weight_ref, *refs):
+        out_ref[pl.ds(j * rows, rows), :] = wide[:rows, j * LANES : (j + 1) * LANES].astype(BF16)
+
+
+def unpack_kernel(full_ref, weights_ref, down_ref):
+    kvol, chans, _ = weights_ref.shape
+    noct, c2, _ = down_ref.shape
+    for k in range(kvol):
+        weights_ref[k] = full_ref[pl.ds(k * chans, chans), :][:, :chans]
+    first = kvol * chans
+    rest = LANES - chans
+    for o in range(noct - 1):
+        down_ref[o] = full_ref[pl.ds(first + o * c2, c2), :][:, :chans]
+    start = first + (noct - 1) * c2
+    down_ref[noct - 1, pl.ds(0, c2 - rest), :] = full_ref[pl.ds(start, c2 - rest), :][:, :chans]
+    lane = lax.broadcasted_iota(I32, (rest, LANES), 1)
+    tail = jnp.zeros((rest, LANES), F32)
+    for j in range(chans // rest):
+        piece = pltpu.roll(full_ref[pl.ds(first + j * rest, rest), :], rest * (j + 1), 1)
+        tail = jnp.where((lane >= j * rest) & (lane < (j + 1) * rest), piece, tail)
+    down_ref[noct - 1, pl.ds(c2 - rest, rest), :] = tail[:, :chans]
+
+
+def pool_kernel(levels, chans, keys_ref, self_ref, act_ref, grad_ref, weight_ref, *refs):
     received = refs[:levels]
     coarse_ref, down_ref, rows = refs[levels : levels + 3]
     pools = refs[levels + 3 :]
     slots = received[0].shape[0]
-    noct, _, chans = down_ref.shape
+    noct, c2, _ = weight_ref.shape
+    rest = LANES - chans
     ndev = grad_ref.shape[1]
     for level in range(levels):
         rows[pl.ds(level * slots, slots), :] = received[level][...].astype(F32)
@@ -276,7 +284,8 @@
     add_rows(act_ref.shape[0], 64, lambda r: self_ref[0, r], act_ref, pools)
     add_rows(levels * slots, 64, lambda r: keys_ref[0, r], rows, pools)
     coarse = jnp.zeros(coarse_ref.shape, F32)
-    for o in range(noct):
+    lane = lax.broadcasted_iota(I32, (rest, LANES), 1)
+    for o in reversed(range(noct)):
         part = pl.ds(o * ndev, ndev)
         total = pools[0][part, :]
         for pool in pools[1:]:
@@ -286,7 +295,16 @@
             weight_ref[o], pooled, (((1,), (1,)), ((), ())), preferred_element_type=F32
         )
         down = jnp.dot(grad_ref[...], pooled, preferred_element_type=F32)
-        down_ref[o] = down[:, :chans]
+        if o == noct - 1:
+            tail = down[c2 - rest :]
+            down = down[: c2 - rest]
+        if o == 0:
+            parts = []
+            for j in range(chans // rest):
+                piece = pltpu.roll(tail, (chans - rest * j) % LANES, 1)
+                parts.append(jnp.where(lane >= chans, piece, down[j * rest : (j + 1) * rest]))
+            down = jnp.concatenate(parts + [down[chans:]], axis=0)
+        down_ref[pl.ds(o * c2, down.shape[0]), :] = down.astype(BF16)
     coarse_ref[...] = coarse.astype(BF16)
 
 
@@ -312,7 +330,7 @@
             table[...] = jnp.zeros_like(table)
         ready(0, 0, buf0)
 
-    def step(base, parity, store, entry, first, turn):
+    def step(base, parity, store, entry):
         buf = bufs[parity]
         over = base + chunk == vdev
         ahead = pl.multiple_of(jnp.where(over, 0, base + chunk), chunk)
@@ -381,7 +399,7 @@
     index = kmap.reshape(kvol, 1, vdev)
 
     w_backward = jnp.pad(w_sub, ((0, 0), (0, lane_pad), (0, lane_pad)))
-    w_forward = w_backward.transpose(0, 2, 1)
+    w_forward = w_backward.transpose(0, 2, 1).reshape(kvol * LANES, LANES)
     down_pad = jnp.pad(w_down, ((0, 0), (0, 0), (0, lane_pad)))
 
     prepared = pl.pallas_call(
@@ -410,6 +428,9 @@
         name="parents",
     )(own_key, grad_coarse.T, down_pad)
 
+    *received, index, w_forward, w_backward, wide, rows = lax.optimization_barrier(
+        (*received, index, w_forward, w_backward, wide, rows)
+    )
     digits = jnp.stack([got[halo : halo + 2] for got in received]).astype(F32)
     got_keys = (digits[:, 0] * DIGIT + digits[:, 1]).astype(I32).reshape(1, levels * slots)
     answers = pl.pallas_call(
@@ -423,19 +444,18 @@
     )(got_keys, wide)
     returned = [from_partner(answers[level], level, bits_member) for level in range(levels)]
 
-    stages, width, chunk = 4, 512, 256
+    stages, width, chunk = 4, 1024, 512
     staging = [pltpu.SMEM((1, width), I32)] * stages
-    gathered, pre = pl.pallas_call(
+    gathered = pl.pallas_call(
         functools.partial(gather_kernel, levels, halo),
         grid=(kvol,),
         in_specs=[
             pl.BlockSpec(memory_space=pl.ANY),
             vmem_full((vdev, LANES)),
-            pl.BlockSpec((1, LANES, LANES), lambda k: (k, 0, 0)),
         ]
         + [vmem_full((halo + 2 * SUB, LANES))] * levels,
-        out_specs=[pl.BlockSpec((vdev, LANES), lambda k: (0, k)), vmem_full((vdev, LANES))],
-        out_shape=[shape((vdev, kvol * LANES), BF16), shape((vdev, LANES), F32)],
+        out_specs=pl.BlockSpec((vdev, LANES), lambda k: (0, k)),
+        out_shape=shape((vdev, kvol * LANES), BF16),
         scratch_shapes=[pltpu.VMEM((table_rows, LANES), F32)]
         + [pltpu.VMEM((chunk, LANES), F32)] * 2
         + staging
@@ -443,7 +463,8 @@
         compiler_params=params(),
         cost_estimate=pl.CostEstimate(flops=0, bytes_accessed=300_000_000, transcendentals=0),
         name="gather",
-    )(index, table, w_forward, *received)
+    )(index, table, *received)
+    pre = jnp.dot(gathered, w_forward, preferred_element_type=F32)
 
     middle = pl.pallas_call(
         functools.partial(middle_kernel, levels),
@@ -471,15 +492,15 @@
         weights_kernel,
         grid=(kvol // group,),
         in_specs=[vmem_full((LANES, vdev)), pl.BlockSpec((vdev, group * LANES), lambda k: (0, k))],
-        out_specs=pl.BlockSpec((group, chans, chans), lambda k: (k, 0, 0)),
-        out_shape=shape((kvol, chans, chans), F32),
+        out_specs=pl.BlockSpec((group * chans, LANES), lambda k: (k, 0)),
+        out_shape=shape((kvol * chans, LANES), BF16),
         compiler_params=params(),
         cost_estimate=pl.CostEstimate(flops=0, bytes_accessed=40_000_000, transcendentals=0),
         name="weights",
     )(grad_turned, gathered)
 
     coarse_out, grad_down = pl.pallas_call(
-        functools.partial(pool_kernel, levels),
+        functools.partial(pool_kernel, levels, chans),
         in_specs=[
             smem_full((1, levels * slots)),
             smem_full((1, vdev)),
@@ -488,16 +509,24 @@
             vmem_full((noct, c2, LANES)),
         ]
         + [vmem_full((slots, LANES))] * levels,
-        out_specs=[vmem_full((c2, coarse_dev)), vmem_full((noct, c2, chans))],
-        out_shape=[shape((c2, coarse_dev), BF16), shape((noct, c2, chans), F32)],
+        out_specs=[vmem_full((c2, coarse_dev)), vmem_full((noct * c2 - lane_pad, LANES))],
+        out_shape=[shape((c2, coarse_dev), BF16), shape((noct * c2 - lane_pad, LANES), BF16)],
         scratch_shapes=[pltpu.VMEM((levels * slots, LANES), F32)]
         + [pltpu.VMEM((keys + SUB, LANES), F32)] * 8,
         compiler_params=params(),
         name="pool",
     )(got_keys, own_key, act, grad_coarse, down_pad, *came)
 
-    grad_w, grad_down, grad_pre = lax.optimization_barrier((grad_w, grad_down, grad_pre))
-    grad_w, grad_down = lax.psum((grad_w, grad_down), ("group", "member"))
+    both = ("group", "member")
+    devices = lax.axis_size(both)
+    packed = jnp.concatenate([grad_w, grad_down], axis=0)
+    share = packed.shape[0] // devices
+    parts = lax.all_to_all(
+        packed.reshape(devices, share, LANES), both, split_axis=0, concat_axis=0, tiled=True
+    )
+    summed = jnp.sum(parts.astype(F32), axis=0)
+    summed, grad_pre = lax.optimization_barrier((summed, grad_pre))
+    full = lax.all_gather(summed, both, axis=0, tiled=True)
 
     accumulators = 8
     scattered = pl.pallas_call(
@@ -529,6 +558,14 @@
         compiler_params=params(),
         name="finish",
     )(outgoing, scattered[0], *incoming)
+    grad_w, grad_down = pl.pallas_call(
+        unpack_kernel,
+        in_specs=[vmem_full((devices * share, LANES))],
+        out_specs=[vmem_full((kvol, chans, chans)), vmem_full((noct, c2, chans))],
+        out_shape=[shape((kvol, chans, chans), F32), shape((noct, c2, chans), F32)],
+        compiler_params=params(),
+        name="unpack",
+    )(full)
     return coarse_out, grad_feats, grad_w, grad_down
 
 

time: 370 us -> 323 us (0.87)
  Pallas kernels: 257 us -> 213 us
  waiting for transfers between devices: 47.4 us -> 6.54 us
  blocking collectives: 0 us -> 23.3 us
  matrix products: 0 us -> 14 us
  local copies, waits for them, and re-layouts: 13.2 us -> 8.43 us
    pallas_call x1, Pallas kernels: 109 us -> 66.8 us  [shards(): pl.pallas_call(functools.partial(gather_kernel, levels, halo), grid=(kvol...]
    psum x1 -> x0, waiting for transfers between devices: 33.9 us -> none  [shards(): grad_w, grad_down = lax.psum((grad_w, grad_down), ('group', 'member'))]
    all_to_all x0 -> x1, blocking collectives: none -> 23.3 us  [shards(): lax.all_to_all(packed.reshape(devices, share, LANES), both, split_axis=0,...]
    dot_general x0 -> x1, matrix products: none -> 14 us  [shards(): pre = jnp.dot(gathered, w_forward, preferred_element_type=F32)]
    ppermute x28, waiting for transfers between devices: 13.5 us -> 6.52 us  [from_partner(): return lax.ppermute(value, axis, pairs)]
    unnamed x71 -> x75, local copies, waits for them, and re-layouts: 7.1 us -> 2.79 us
    pallas_call x1, Pallas kernels: 93.9 us -> 89.7 us  [shards(): pl.pallas_call(functools.partial(scatter_kernel, levels, halo, stages), g...]
    pallas_call x1 -> x2, Pallas kernels: 9.45 us -> 12.3 us  [the longest x1 9.3 us: shards(): pl.pallas_call(functools.partial(pool_kernel, levels, chans), in_specs=[s...]
  transfers between devices with their start and end apart: 29 -> 29, of which waited for: 10 -> 4; matrix products, arithmetic and copies ran while one was open for 2% -> 6% of each run, Pallas kernels for 63% -> 57%
where the time goes in v3:
time: 323 us; the launch traced here: 322 us
  Pallas kernels  213 us (66%)
  starting transfers between devices  39.6 us (12%)
  blocking collectives  23.3 us (7%)
  between operations  14.5 us (4%)
  matrix products  14 us (4%)
  local copies, waits for them, and re-layouts  8.43 us (3%)
  waiting for transfers between devices  6.54 us (2%)
    pallas_call x1, Pallas kernels, shards(): pl.pallas_call(functools.partial(scatter_kernel, levels, halo, stages), g...  89.7 us
    pallas_call x1, Pallas kernels, shards(): pl.pallas_call(functools.partial(gather_kernel, levels, halo), grid=(kvol...  66.8 us
    ppermute x28, starting transfers between devices, from_partner(): return lax.ppermute(value, axis, pairs)  39.6 us
    all_to_all x1, blocking collectives, shards(): lax.all_to_all(packed.reshape(devices, share, LANES), both, split_axis=0,...  23.3 us
    pallas_call x1, Pallas kernels, shards(): pl.pallas_call(weights_kernel, grid=(kvol // group,), in_specs=[vmem_full...  14.5 us
    dot_general x1, matrix products, shards(): pre = jnp.dot(gathered, w_forward, preferred_element_type=F32)  14 us
    pallas_call x1, Pallas kernels, shards(): pl.pallas_call(functools.partial(pool_kernel, levels, chans), in_specs=[s...  9.3 us
    pallas_call x1, Pallas kernels, shards(): pl.pallas_call(parents_kernel, in_specs=[smem_full((1, vdev)), vmem_full(...  7.32 us
  transfers between devices with their start and end apart: 29, of which 4 were waited for; matrix products, arithmetic and copies ran while one was open for 6% of the time, Pallas kernels for 57%

profile of v3, /device:TPU:0, one launch (start us, length us, event | category | flops | bytes accessed | tf_op | source)
XLA Modules:
  0.0 322.2 jit_solution(14978674121890373441)
XLA Ops:
  7.2 6.1 %prepare.1 = (bf16[272,128]{1,0:T(8,128)(2,1)}, bf16[272,128]{1,0:T(8,128)(2,1)}, bf16[272,128]{1,0:T(8,128)(2,1)}, bf16[272,128]{1,0:T(8,128)(2,1)}, bf16[272,1...) custom-call(s32[1]{0:T(128)} %bitcast.me_ref, ...), custom_call_target="tpu_custom_call" | custom-call | tf_op jit(solution)/shard_map/prepare/pallas_call | solution.py:405
  13.3 1.6 collective-permute-start
  15.0 2.7 collective-permute-start.1
  17.7 1.9 collective-permute-start.2
  19.6 3.6 %collective-permute-start.3 = (bf16[272,128]{1,0:T(8,128)(2,1)}, bf16[272,128]{1,0:T(8,128)(2,1)S(1)}, u32[]{:S(2)}, u32[]{:S(2)}) collective-permute-start(bf16[272,128]{1,0:T(8,128)(2,1)} %get-tuple-element.62), channel_id=1, source_target_pairs={{0,8},{1,9},{2,10},{3,11},{4,12},{5,13},{6,14},{7,15},{8,0},{9,1},... | collective-permute-start | bytes 208904 | tf_op jit(solution)/shard_map/ppermute | solution.py:23
  23.2 1.7 collective-permute-start.5
  24.9 2.9 collective-permute-start.6
  27.8 2.2 fusion.2
  30.8 1.3 reshape.65.index_ref
  32.1 1.3 copy.14
  34.3 7.3 %parents.1 = (f32[4104,128]{1,0:T(8,128)}, f32[4096,128]{1,0:T(8,128)}) custom-call(s32[1,4096]{1,0:T(1,128)} %get-tuple-element.66.self_ref, bf16[512,192]{1,0:T(8,128)(2,1)} %bitcast.29, bf16[8,192,128]{2,1,0:T(8,128)(2,1)} %pad.9.weight_ref), custom_call_target="tpu_custom_call" | custom-call | tf_op jit(solution)/shard_map/parents/pallas_call | solution.py:422
  42.4 3.1 answer.1
  45.7 1.7 collective-permute-start.8
  47.4 3.5 %collective-permute-start.10 = (bf16[128,128]{1,0:T(8,128)(2,1)}, bf16[128,128]{1,0:T(8,128)(2,1)S(1)}, u32[]{:S(2)}, u32[]{:S(2)}) collective-permute-start(bf16[128,128]{1,0:T(8,128)(2,1)} %get-tuple-element.85), channel_id=1, source_target_pairs={{0,8},{1,9},{2,10},{3,11},{4,12},{5,13},{6,14},{7,15},{8,0},{9,1},... | collective-permute-start | bytes 98312 | tf_op jit(solution)/shard_map/ppermute | solution.py:23
  51.0 66.8 %gather.1.taken_ref = bf16[4096,3456]{1,0:T(8,128)(2,1)} custom-call(s32[27,1,4096]{2,1,0:T(1,128)} %reshape.65.index_ref, f32[4096,128]{1,0:T(8,128)} %get-tuple-element.78.local_ref, bf16[272,128]{1,0:T(8,128)(2,1)} %copy-done.4, bf16[272,128]{1,0:T(8,128)(2,1)} %copy-done.5, bf16[272,128]{1,0:T(8,128)(2,1)} %copy-done.6, bf16[272,128]{1,0:T(8,128)(2,1)} %copy-done.7, ...), custom_call_target="tpu_custom_call" | custom-call | bytes 300000000 | tf_op jit(solution)/shard_map/gather/pallas_call | solution.py:449
  118.6 2.1 collective-permute-start.13
  120.7 14.0 %fusion.3.pre_ref = f32[4096,128]{1,0:T(8,128)} fusion(bf16[4096,3456]{1,0:T(8,128)(2,1)} %gather.1.taken_ref, bf16[3456,128]{1,0:T(8,128)(2,1)S(1)} %bitcast.30), kind=kOutput, calls=%fused_computation.15 | convolution fusion | flops 3623878656 | bytes 31293440 | tf_op jit(solution)/shard_map/dot_general | solution.py:467
  135.4 7.2 %middle.1 = (bf16[4096,128]{1,0:T(8,128)(2,1)}, bf16[128,4096]{1,0:T(8,128)(2,1)}, f32[4096,128]{1,0:T(8,128)}, bf16[128,128]{1,0:T(8,128)(2,1)}, bf16[128,128]{...) custom-call(s32[1,896]{1,0:T(1,128)} %get-tuple-element.76.list_ref,, ...), custom_call_target="tpu_custom_call" | custom-call | tf_op jit(solution)/shard_map/middle/pallas_call | solution.py:469
  143.2 2.3 collective-permute-start.15
  145.6 3.1 collective-permute-start.17
  149.1 4.1 %collective-permute-start.20 = (bf16[128,128]{1,0:T(8,128)(2,1)}, bf16[128,128]{1,0:T(8,128)(2,1)S(1)}, u32[]{:S(2)}, u32[]{:S(2)}) collective-permute-start(bf16[128,128]{1,0:T(8,128)(2,1)} %get-tuple-element.96), channel_id=1, source_target_pairs={{0,64},{16,80},{32,96},{48,112},{64,0},{80,16},{96,32},{112,48},{1... | collective-permute-start | bytes 98312 | tf_op jit(solution)/shard_map/ppermute | solution.py:23
  153.3 14.5 %weights.1 = bf16[2592,128]{1,0:T(8,128)(2,1)} custom-call(bf16[128,4096]{1,0:T(8,128)(2,1)} %get-tuple-element.98.turned_ref, bf16[4096,3456]{1,0:T(8,128)(2,1)} %gather.1.taken_ref), custom_call_target="tpu_custom_call" | custom-call | bytes 40000000 | tf_op jit(solution)/shard_map/weights/pallas_call | solution.py:491
  168.5 9.3 %pool.1 = (bf16[192,512]{1,0:T(8,128)(2,1)}, bf16[1504,128]{1,0:T(8,128)(2,1)}) custom-call(s32[1,896]{1,0:T(1,128)} %fusion.1.keys_ref, s32[1,4096]{1,0:T(1,128)} %get-tuple-element.66.self_ref, f32[4096,128]{1,0:T(8,128)} %get-tuple-element.89.act_ref, bf16[192,512]{1,0:T(8,128)(2,1)} %grad_ref.1, bf16[8,192,128]{2,1,0:T(8,128)(2,1)} %pad.9.weight_ref, ...), custom_call_target="tpu_custom_call" | custom-call | tf_op jit(solution)/shard_map/pool/pallas_call | solution.py:502
  178.9 23.3 %all_to_all.5 = bf16[128,32,128]{2,1,0:T(8,128)(2,1)S(1)} all-to-all(bf16[128,32,128]{2,1,0:T(8,128)(2,1)S(1)} %bitcast.28), channel_id=1, replica_groups=mesh['group'=8,'member'=16] {'group','member'}, dimensions={0} | all-to-all | bytes 2097152 | tf_op jit(solution)/shard_map/all_to_all | solution.py:524
  203.0 89.7 %scatter.1 = (f32[4096,128]{1,0:T(8,128)}, bf16[256,128]{1,0:T(8,128)(2,1)}, bf16[256,128]{1,0:T(8,128)(2,1)}, bf16[256,128]{1,0:T(8,128)(2,1)}, bf16[256,128]{1...) custom-call(s32[27,1,4096]{2,1,0:T(1,128)} %reshape.65.index_ref, ...), custom_call_target="tpu_custom_call" | custom-call | bytes 400000000 | tf_op jit(solution)/shard_map/scatter/pallas_call | solution.py:532
  293.4 2.0 collective-permute-start.22
  296.1 1.6 collective-permute-start.24
  298.0 1.4 collective-permute-done.22.refs_1_
  300.3 1.8 collective-permute-done.24.refs_3_
  302.9 2.4 collective-permute-done.27.refs_6_
  306.0 6.4 %finish.1 = f32[96,4096]{1,0:T(8,128)} custom-call(s32[1,1792]{1,0:T(1,128)} %bitcast.32, f32[4096,128]{1,0:T(8,128)} %get-tuple-element.103.local_ref, bf16[256,128]{1,0:T(8,128)(2,1)} %copy-done.11, bf16[256,128]{1,0:T(8,128)(2,1)} %copy-done.12, bf16[256,128]{1,0:T(8,128)(2,1)} %copy-done.13, bf16[256,128]{1,0:T(8,128)(2,1)} %copy-done.14, ...), custom_call_target="tpu_custom_call" | custom-call | tf_op jit(solution)/shard_map/finish/pallas_call | solution.py:552
  312.4 3.0 unpack.1
  (123 shorter events, 11.6 us)
Async XLA Ops:
  7.2 23.7 %copy-start.2 = (s32[27,4096]{1,0:T(8,128)S(1)}, s32[27,4096]{1,0:T(8,128)}, u32[]{:S(2)}) copy-start(s32[27,4096]{1,0:T(8,128)} %param.10) | copy-start | bytes 1327108
  7.2 305.2 %all-gather.2.cloned.1.call-start = ((), (), s32[]{:S(2)}) async-start(), calls=%async_computation.1 | async-start | bytes 2113536 | tf_op jit(solution)/shard_map/all_gather | solution.py:529
  13.3 9.9 %collective-permute-start = (bf16[272,128]{1,0:T(8,128)(2,1)}, bf16[272,128]{1,0:T(8,128)(2,1)S(1)}, u32[]{:S(2)}, u32[]{:S(2)}) collective-permute-start(bf16[272,128]{1,0:T(8,128)(2,1)} %get-tuple-element.59), channel_id=1, source_target_pairs={{0,1},{1,0},{2,3},{3,2},{4,5},{5,4},{6,7},{7,6},{8,9},{9,8},{10,11... | collective-permute-start | bytes 208904 | tf_op jit(solution)/shard_map/ppermute | solution.py:23
  15.0 9.9 %collective-permute-start.1 = (bf16[272,128]{1,0:T(8,128)(2,1)}, bf16[272,128]{1,0:T(8,128)(2,1)S(1)}, u32[]{:S(2)}, u32[]{:S(2)}) collective-permute-start(bf16[272,128]{1,0:T(8,128)(2,1)} %get-tuple-element.60), channel_id=1, source_target_pairs={{0,2},{1,3},{2,0},{3,1},{4,6},{5,7},{6,4},{7,5},{8,10},{9,11},{10,... | collective-permute-start | bytes 208904 | tf_op jit(solution)/shard_map/ppermute | solution.py:23
  17.7 23.9 %collective-permute-start.2 = (bf16[272,128]{1,0:T(8,128)(2,1)}, bf16[272,128]{1,0:T(8,128)(2,1)S(1)}, u32[]{:S(2)}, u32[]{:S(2)}) collective-permute-start(bf16[272,128]{1,0:T(8,128)(2,1)} %get-tuple-element.61), channel_id=1, source_target_pairs={{0,4},{1,5},{2,6},{3,7},{4,0},{5,1},{6,2},{7,3},{8,12},{9,13},{10,... | collective-permute-start | bytes 208904 | tf_op jit(solution)/shard_map/ppermute | solution.py:23
  19.6 22.0 %collective-permute-start.3 = (bf16[272,128]{1,0:T(8,128)(2,1)}, bf16[272,128]{1,0:T(8,128)(2,1)S(1)}, u32[]{:S(2)}, u32[]{:S(2)}) collective-permute-start(bf16[272,128]{1,0:T(8,128)(2,1)} %get-tuple-element.62), channel_id=1, source_target_pairs={{0,8},{1,9},{2,10},{3,11},{4,12},{5,13},{6,14},{7,15},{8,0},{9,1},... | collective-permute-start | bytes 208904 | tf_op jit(solution)/shard_map/ppermute | solution.py:23
  23.2 18.4 %collective-permute-start.4 = (bf16[272,128]{1,0:T(8,128)(2,1)}, bf16[272,128]{1,0:T(8,128)(2,1)S(1)}, u32[]{:S(2)}, u32[]{:S(2)}) collective-permute-start(bf16[272,128]{1,0:T(8,128)(2,1)} %get-tuple-element.63), channel_id=1, source_target_pairs={{0,16},{16,0},{32,48},{48,32},{64,80},{80,64},{96,112},{112,96},{1... | collective-permute-start | bytes 208904 | tf_op jit(solution)/shard_map/ppermute | solution.py:23
  23.2 18.4 %collective-permute-start.5 = (bf16[272,128]{1,0:T(8,128)(2,1)}, bf16[272,128]{1,0:T(8,128)(2,1)S(1)}, u32[]{:S(2)}, u32[]{:S(2)}) collective-permute-start(bf16[272,128]{1,0:T(8,128)(2,1)} %get-tuple-element.64), channel_id=1, source_target_pairs={{0,32},{16,48},{32,0},{48,16},{64,96},{80,112},{96,64},{112,80},{1... | collective-permute-start | bytes 208904 | tf_op jit(solution)/shard_map/ppermute | solution.py:23
  24.9 16.8 %collective-permute-start.6 = (bf16[272,128]{1,0:T(8,128)(2,1)}, bf16[272,128]{1,0:T(8,128)(2,1)S(1)}, u32[]{:S(2)}, u32[]{:S(2)}) collective-permute-start(bf16[272,128]{1,0:T(8,128)(2,1)} %get-tuple-element.65), channel_id=1, source_target_pairs={{0,64},{16,80},{32,96},{48,112},{64,0},{80,16},{96,32},{112,48},{1... | collective-permute-start | bytes 208904 | tf_op jit(solution)/shard_map/ppermute | solution.py:23
  45.4 72.4 %collective-permute-start.7 = (bf16[128,128]{1,0:T(8,128)(2,1)}, bf16[128,128]{1,0:T(8,128)(2,1)S(1)}, u32[]{:S(2)}, u32[]{:S(2)}) collective-permute-start(bf16[128,128]{1,0:T(8,128)(2,1)} %get-tuple-element.82), channel_id=1, source_target_pairs={{0,1},{1,0},{2,3},{3,2},{4,5},{5,4},{6,7},{7,6},{8,9},{9,8},{10,11... | collective-permute-start | bytes 98312 | tf_op jit(solution)/shard_map/ppermute | solution.py:23
  45.7 72.9 %collective-permute-start.8 = (bf16[128,128]{1,0:T(8,128)(2,1)}, bf16[128,128]{1,0:T(8,128)(2,1)S(1)}, u32[]{:S(2)}, u32[]{:S(2)}) collective-permute-start(bf16[128,128]{1,0:T(8,128)(2,1)} %get-tuple-element.83), channel_id=1, source_target_pairs={{0,2},{1,3},{2,0},{3,1},{4,6},{5,7},{6,4},{7,5},{8,10},{9,11},{10,... | collective-permute-start | bytes 98312 | tf_op jit(solution)/shard_map/ppermute | solution.py:23
  47.4 87.3 %collective-permute-start.9 = (bf16[128,128]{1,0:T(8,128)(2,1)}, bf16[128,128]{1,0:T(8,128)(2,1)S(1)}, u32[]{:S(2)}, u32[]{:S(2)}) collective-permute-start(bf16[128,128]{1,0:T(8,128)(2,1)} %get-tuple-element.84), channel_id=1, source_target_pairs={{0,4},{1,5},{2,6},{3,7},{4,0},{5,1},{6,2},{7,3},{8,12},{9,13},{10,... | collective-permute-start | bytes 98312 | tf_op jit(solution)/shard_map/ppermute | solution.py:23
  47.4 87.3 %collective-permute-start.10 = (bf16[128,128]{1,0:T(8,128)(2,1)}, bf16[128,128]{1,0:T(8,128)(2,1)S(1)}, u32[]{:S(2)}, u32[]{:S(2)}) collective-permute-start(bf16[128,128]{1,0:T(8,128)(2,1)} %get-tuple-element.85), channel_id=1, source_target_pairs={{0,8},{1,9},{2,10},{3,11},{4,12},{5,13},{6,14},{7,15},{8,0},{9,1},... | collective-permute-start | bytes 98312 | tf_op jit(solution)/shard_map/ppermute | solution.py:23
  50.9 83.8 %collective-permute-start.11 = (bf16[128,128]{1,0:T(8,128)(2,1)}, bf16[128,128]{1,0:T(8,128)(2,1)S(1)}, u32[]{:S(2)}, u32[]{:S(2)}) collective-permute-start(bf16[128,128]{1,0:T(8,128)(2,1)} %get-tuple-element.86), channel_id=1, source_target_pairs={{0,16},{16,0},{32,48},{48,32},{64,80},{80,64},{96,112},{112,96},{1... | collective-permute-start | bytes 98312 | tf_op jit(solution)/shard_map/ppermute | solution.py:23
  51.0 66.9 %copy-start.33 = (bf16[128,128]{1,0:T(8,128)(2,1)S(1)}, bf16[128,128]{1,0:T(8,128)(2,1)}, u32[]{:S(2)}) copy-start(bf16[128,128]{1,0:T(8,128)(2,1)} %get-tuple-element.87) | copy-start | bytes 98308
  51.0 67.6 %copy-start.32 = (bf16[128,128]{1,0:T(8,128)(2,1)S(1)}, bf16[128,128]{1,0:T(8,128)(2,1)}, u32[]{:S(2)}) copy-start(bf16[128,128]{1,0:T(8,128)(2,1)} %get-tuple-element.88) | copy-start | bytes 98308
  117.9 16.9 %collective-permute-start.12 = (bf16[128,128]{1,0:T(8,128)(2,1)S(1)}, bf16[128,128]{1,0:T(8,128)(2,1)S(1)}, u32[]{:S(2)}, u32[]{:S(2)}) collective-permute-start(bf16[128,128]{1,0:T(8,128)(2,1)S(1)} %copy-done.33), channel_id=1, source_target_pairs={{0,32},{16,48},{32,0},{48,16},{64,96},{80,112},{96,64},{112,80},{1... | collective-permute-start | bytes 98312 | tf_op jit(solution)/shard_map/ppermute | solution.py:23
  118.6 16.2 %collective-permute-start.13 = (bf16[128,128]{1,0:T(8,128)(2,1)S(1)}, bf16[128,128]{1,0:T(8,128)(2,1)S(1)}, u32[]{:S(2)}, u32[]{:S(2)}) collective-permute-start(bf16[128,128]{1,0:T(8,128)(2,1)S(1)} %copy-done.32), channel_id=1, source_target_pairs={{0,64},{16,80},{32,96},{48,112},{64,0},{80,16},{96,32},{112,48},{1... | collective-permute-start | bytes 98312 | tf_op jit(solution)/shard_map/ppermute | solution.py:23
  142.6 6.1 %collective-permute-start.14 = (bf16[128,128]{1,0:T(8,128)(2,1)}, bf16[128,128]{1,0:T(8,128)(2,1)S(1)}, u32[]{:S(2)}, u32[]{:S(2)}) collective-permute-start(bf16[128,128]{1,0:T(8,128)(2,1)} %get-tuple-element.90), channel_id=1, source_target_pairs={{0,1},{1,0},{2,3},{3,2},{4,5},{5,4},{6,7},{7,6},{8,9},{9,8},{10,11... | collective-permute-start | bytes 98312 | tf_op jit(solution)/shard_map/ppermute | solution.py:23
  143.2 5.9 %collective-permute-start.15 = (bf16[128,128]{1,0:T(8,128)(2,1)}, bf16[128,128]{1,0:T(8,128)(2,1)S(1)}, u32[]{:S(2)}, u32[]{:S(2)}) collective-permute-start(bf16[128,128]{1,0:T(8,128)(2,1)} %get-tuple-element.91), channel_id=1, source_target_pairs={{0,2},{1,3},{2,0},{3,1},{4,6},{5,7},{6,4},{7,5},{8,10},{9,11},{10,... | collective-permute-start | bytes 98312 | tf_op jit(solution)/shard_map/ppermute | solution.py:23
  145.6 22.2 %collective-permute-start.16 = (bf16[128,128]{1,0:T(8,128)(2,1)}, bf16[128,128]{1,0:T(8,128)(2,1)S(1)}, u32[]{:S(2)}, u32[]{:S(2)}) collective-permute-start(bf16[128,128]{1,0:T(8,128)(2,1)} %get-tuple-element.92), channel_id=1, source_target_pairs={{0,4},{1,5},{2,6},{3,7},{4,0},{5,1},{6,2},{7,3},{8,12},{9,13},{10,... | collective-permute-start | bytes 98312 | tf_op jit(solution)/shard_map/ppermute | solution.py:23
  145.6 22.3 %collective-permute-start.17 = (bf16[128,128]{1,0:T(8,128)(2,1)}, bf16[128,128]{1,0:T(8,128)(2,1)S(1)}, u32[]{:S(2)}, u32[]{:S(2)}) collective-permute-start(bf16[128,128]{1,0:T(8,128)(2,1)} %get-tuple-element.93), channel_id=1, source_target_pairs={{0,8},{1,9},{2,10},{3,11},{4,12},{5,13},{6,14},{7,15},{8,0},{9,1},... | collective-permute-start | bytes 98312 | tf_op jit(solution)/shard_map/ppermute | solution.py:23
  148.7 19.1 %collective-permute-start.18 = (bf16[128,128]{1,0:T(8,128)(2,1)}, bf16[128,128]{1,0:T(8,128)(2,1)S(1)}, u32[]{:S(2)}, u32[]{:S(2)}) collective-permute-start(bf16[128,128]{1,0:T(8,128)(2,1)} %get-tuple-element.94), channel_id=1, source_target_pairs={{0,16},{16,0},{32,48},{48,32},{64,80},{80,64},{96,112},{112,96},{1... | collective-permute-start | bytes 98312 | tf_op jit(solution)/shard_map/ppermute | solution.py:23
  148.7 19.2 %collective-permute-start.19 = (bf16[128,128]{1,0:T(8,128)(2,1)}, bf16[128,128]{1,0:T(8,128)(2,1)S(1)}, u32[]{:S(2)}, u32[]{:S(2)}) collective-permute-start(bf16[128,128]{1,0:T(8,128)(2,1)} %get-tuple-element.95), channel_id=1, source_target_pairs={{0,32},{16,48},{32,0},{48,16},{64,96},{80,112},{96,64},{112,80},{1... | collective-permute-start | bytes 98312 | tf_op jit(solution)/shard_map/ppermute | solution.py:23
  149.1 18.7 %collective-permute-start.20 = (bf16[128,128]{1,0:T(8,128)(2,1)}, bf16[128,128]{1,0:T(8,128)(2,1)S(1)}, u32[]{:S(2)}, u32[]{:S(2)}) collective-permute-start(bf16[128,128]{1,0:T(8,128)(2,1)} %get-tuple-element.96), channel_id=1, source_target_pairs={{0,64},{16,80},{32,96},{48,112},{64,0},{80,16},{96,32},{112,48},{1... | collective-permute-start | bytes 98312 | tf_op jit(solution)/shard_map/ppermute | solution.py:23
  292.7 5.1 %collective-permute-start.21 = (bf16[256,128]{1,0:T(8,128)(2,1)}, bf16[256,128]{1,0:T(8,128)(2,1)S(1)}, u32[]{:S(2)}, u32[]{:S(2)}) collective-permute-start(bf16[256,128]{1,0:T(8,128)(2,1)} %get-tuple-element.104), channel_id=1, source_target_pairs={{0,1},{1,0},{2,3},{3,2},{4,5},{5,4},{6,7},{7,6},{8,9},{9,8},{10,11... | collective-permute-start | bytes 196616 | tf_op jit(solution)/shard_map/ppermute | solution.py:23
  293.4 6.0 %collective-permute-start.22 = (bf16[256,128]{1,0:T(8,128)(2,1)}, bf16[256,128]{1,0:T(8,128)(2,1)S(1)}, u32[]{:S(2)}, u32[]{:S(2)}) collective-permute-start(bf16[256,128]{1,0:T(8,128)(2,1)} %get-tuple-element.105), channel_id=1, source_target_pairs={{0,2},{1,3},{2,0},{3,1},{4,6},{5,7},{6,4},{7,5},{8,10},{9,11},{10,... | collective-permute-start | bytes 196616 | tf_op jit(solution)/shard_map/ppermute | solution.py:23
  295.4 4.9 %collective-permute-start.23 = (bf16[256,128]{1,0:T(8,128)(2,1)}, bf16[256,128]{1,0:T(8,128)(2,1)S(1)}, u32[]{:S(2)}, u32[]{:S(2)}) collective-permute-start(bf16[256,128]{1,0:T(8,128)(2,1)} %get-tuple-element.106), channel_id=1, source_target_pairs={{0,4},{1,5},{2,6},{3,7},{4,0},{5,1},{6,2},{7,3},{8,12},{9,13},{10,... | collective-permute-start | bytes 196616 | tf_op jit(solution)/shard_map/ppermute | solution.py:23
  296.1 6.0 %collective-permute-start.24 = (bf16[256,128]{1,0:T(8,128)(2,1)}, bf16[256,128]{1,0:T(8,128)(2,1)S(1)}, u32[]{:S(2)}, u32[]{:S(2)}) collective-permute-start(bf16[256,128]{1,0:T(8,128)(2,1)} %get-tuple-element.107), channel_id=1, source_target_pairs={{0,8},{1,9},{2,10},{3,11},{4,12},{5,13},{6,14},{7,15},{8,0},{9,1},... | collective-permute-start | bytes 196616 | tf_op jit(solution)/shard_map/ppermute | solution.py:23
  297.7 4.3 %collective-permute-start.25 = (bf16[256,128]{1,0:T(8,128)(2,1)}, bf16[256,128]{1,0:T(8,128)(2,1)S(1)}, u32[]{:S(2)}, u32[]{:S(2)}) collective-permute-start(bf16[256,128]{1,0:T(8,128)(2,1)} %get-tuple-element.108), channel_id=1, source_target_pairs={{0,16},{16,0},{32,48},{48,32},{64,80},{80,64},{96,112},{112,96},{1... | collective-permute-start | bytes 196616 | tf_op jit(solution)/shard_map/ppermute | solution.py:23
  297.7 5.2 %collective-permute-start.26 = (bf16[256,128]{1,0:T(8,128)(2,1)}, bf16[256,128]{1,0:T(8,128)(2,1)S(1)}, u32[]{:S(2)}, u32[]{:S(2)}) collective-permute-start(bf16[256,128]{1,0:T(8,128)(2,1)} %get-tuple-element.109), channel_id=1, source_target_pairs={{0,32},{16,48},{32,0},{48,16},{64,96},{80,112},{96,64},{112,80},{1... | collective-permute-start | bytes 196616 | tf_op jit(solution)/shard_map/ppermute | solution.py:23
  299.4 6.0 %collective-permute-start.27 = (bf16[256,128]{1,0:T(8,128)(2,1)}, bf16[256,128]{1,0:T(8,128)(2,1)S(1)}, u32[]{:S(2)}, u32[]{:S(2)}) collective-permute-start(bf16[256,128]{1,0:T(8,128)(2,1)} %get-tuple-element.110), channel_id=1, source_target_pairs={{0,64},{16,80},{32,96},{48,112},{64,0},{80,16},{96,32},{112,48},{1... | collective-permute-start | bytes 196616 | tf_op jit(solution)/shard_map/ppermute | solution.py:23
  (31 other events, 223.4 us)
Sparse Core Ops, SparseCore 0:
  203.1 60.7 all-gather.1

commit v4 on v3

--- a/solution.py
+++ b/solution.py
@@ -29,6 +29,19 @@
 
 def smem_full(shape):
     return pl.BlockSpec(shape, lambda *_: (0,) * len(shape), memory_space=SMEM)
+
+
+def clear(tables):
+    count = tables[0].shape[0]
+    block = max(b for b in range(SUB, 257, SUB) if count % b == 0)
+
+    def body(step, _):
+        part = pl.ds(pl.multiple_of(step * block, block), block)
+        for table in tables:
+            table[part, :] = jnp.zeros((block, LANES), F32)
+        return 0
+
+    lax.fori_loop(0, count // block, body, 0)
 
 
 def copy_rows(count, unroll, index, source, target):
@@ -150,9 +163,8 @@
     return pltpu.make_async_copy(index_ref.at[row, :, pl.ds(start, width)], store, sem)
 
 
-def walk(index_ref, stores, sems, vdev, chunk, step_of):
+def walk(index_ref, stores, sems, vdev, chunk, total, step_of):
     k = pl.program_id(0)
-    total = pl.num_programs(0)
     width = stores[0].shape[1]
     many = len(stores)
     pieces = vdev // width
@@ -196,6 +208,8 @@
         table[pl.ds(vdev + levels * halo, SUB), :] = jnp.zeros((SUB, LANES), F32)
         buf1[...] = jnp.zeros_like(buf1)
 
+    last = pl.num_programs(0) - 1
+
     def step(base, parity, store, entry):
         buf = bufs[parity]
         for j in range(chunk):
@@ -203,8 +217,14 @@
         behind = pl.multiple_of(jnp.maximum(base - chunk, 0), chunk)
         out_ref[pl.ds(behind, chunk), :] = bufs[1 - parity][...].astype(BF16)
 
-    walk(index_ref, stores, sems, vdev, chunk, step)
-    out_ref[pl.ds(vdev - chunk, chunk), :] = buf1[...].astype(BF16)
+    @pl.when(pl.program_id(0) < last)
+    def _():
+        walk(index_ref, stores, sems, vdev, chunk, last, step)
+        out_ref[pl.ds(vdev - chunk, chunk), :] = buf1[...].astype(BF16)
+
+    @pl.when(pl.program_id(0) == last)
+    def _():
+        out_ref[...] = local_ref[...].astype(BF16)
 
 
 def middle_kernel(levels, list_ref, pre_ref, rows_ref, *refs):
@@ -226,8 +246,8 @@
 
     lax.fori_loop(0, levels * slots // 64, patch, 0)
 
-    for step in range(vdev // LANES):
-        part = pl.ds(step * LANES, LANES)
+    def point(step, _):
+        part = pl.ds(pl.multiple_of(step * 4 * LANES, 4 * LANES), 4 * LANES)
         pre = pre_ref[part, :]
         sig = 1.0 / (1.0 + jnp.exp(-pre))
         value = (pre * sig).astype(BF16).astype(F32)
@@ -236,6 +256,9 @@
         grad = rows[part, :] * (sig * (1.0 + pre * (1.0 - sig)))
         grad_ref[part, :] = grad.astype(BF16)
         turned_ref[:, part] = grad.T.astype(BF16)
+        return 0
+
+    lax.fori_loop(0, vdev // (4 * LANES), point, 0)
     act[pl.ds(vdev, SUB), :] = jnp.zeros((SUB, LANES), F32)
     copy_rows(levels * slots, 64, lambda r: list_ref[0, r], act, out)
     for level in range(levels):
@@ -253,8 +276,10 @@
 def unpack_kernel(full_ref, weights_ref, down_ref):
     kvol, chans, _ = weights_ref.shape
     noct, c2, _ = down_ref.shape
+    centre = kvol // 2
     for k in range(kvol):
-        weights_ref[k] = full_ref[pl.ds(k * chans, chans), :][:, :chans]
+        spot = kvol - 1 if k == centre else k - int(k > centre)
+        weights_ref[k] = full_ref[pl.ds(spot * chans, chans), :][:, :chans]
     first = kvol * chans
     rest = LANES - chans
     for o in range(noct - 1):
@@ -279,8 +304,7 @@
     ndev = grad_ref.shape[1]
     for level in range(levels):
         rows[pl.ds(level * slots, slots), :] = received[level][...].astype(F32)
-    for pool in pools:
-        pool[...] = jnp.zeros_like(pool)
+    clear(pools)
     add_rows(act_ref.shape[0], 64, lambda r: self_ref[0, r], act_ref, pools)
     add_rows(levels * slots, 64, lambda r: keys_ref[0, r], rows, pools)
     coarse = jnp.zeros(coarse_ref.shape, F32)
@@ -326,8 +350,7 @@
 
     @pl.when(k == 0)
     def _():
-        for table in tables:
-            table[...] = jnp.zeros_like(table)
+        clear(tables)
         ready(0, 0, buf0)
 
     def step(base, parity, store, entry):
@@ -336,12 +359,13 @@
         ahead = pl.multiple_of(jnp.where(over, 0, base + chunk), chunk)
         ready(ahead, jnp.minimum(jnp.where(over, k + 1, k), last), bufs[1 - parity])
         for start in range(0, chunk, lanes):
-            spots = [store[0, entry + start + j] for j in range(lanes)]
-            sums = [tables[j][pl.ds(spots[j], 1), :] + buf[pl.ds(start + j, 1), :] for j in range(lanes)]
-            for j in range(lanes):
+            now = min(lanes, chunk - start)
+            spots = [store[0, entry + start + j] for j in range(now)]
+            sums = [tables[j][pl.ds(spots[j], 1), :] + buf[pl.ds(start + j, 1), :] for j in range(now)]
+            for j in range(now):
                 tables[j][pl.ds(spots[j], 1), :] = sums[j]
 
-    walk(index_ref, stores, sems, vdev, chunk, step)
+    walk(index_ref, stores, sems, vdev, chunk, last + 1, step)
 
     @pl.when(k == last)
     def _():
@@ -351,7 +375,13 @@
                 result = result + table[part, :]
             return result
 
-        local_ref[...] = total(pl.ds(0, vdev))
+        def close(step, _):
+            part = pl.ds(pl.multiple_of(step * chunk, chunk), chunk)
+            centre = jnp.dot(grad_ref[part, :], weight_ref[last + 1], preferred_element_type=F32)
+            local_ref[part, :] = total(part) + centre
+            return 0
+
+        lax.fori_loop(0, vdev // chunk, close, 0)
         for level in range(levels):
             backs[level][...] = total(pl.ds(vdev + level * halo, halo)).astype(BF16)
 
@@ -364,15 +394,18 @@
     chans, vdev = out_ref.shape
     for level in range(levels):
         rows[pl.ds(level * halo, halo), :] = incoming[level][...].astype(F32)
-    for table in tables:
-        table[...] = jnp.zeros_like(table)
+    clear(tables)
     add_rows(levels * halo, 64, lambda r: rows_ref[0, r], rows, tables)
-    for c in range(vdev // LANES):
-        part = pl.ds(c * LANES, LANES)
+
+    def close(step, _):
+        part = pl.ds(pl.multiple_of(step * 2 * LANES, 2 * LANES), 2 * LANES)
         total = local_ref[part, :]
         for table in tables:
             total = total + table[part, :]
         out_ref[:, part] = total.T[:chans]
+        return 0
+
+    lax.fori_loop(0, vdev // (2 * LANES), close, 0)
 
 
 def shape(dims, dtype):
@@ -396,9 +429,11 @@
     lane_pad = LANES - chans
     outgoing = send_rows.reshape(1, levels * halo)
     table_rows = vdev + levels * halo + SUB
-    index = kmap.reshape(kvol, 1, vdev)
-
-    w_backward = jnp.pad(w_sub, ((0, 0), (0, lane_pad), (0, lane_pad)))
+    middle_k = kvol // 2
+    index = jnp.concatenate([kmap[:middle_k], kmap[middle_k + 1 :]], axis=0).reshape(kvol - 1, 1, vdev)
+
+    w_ordered = jnp.concatenate([w_sub[:middle_k], w_sub[middle_k + 1 :], w_sub[middle_k : middle_k + 1]], axis=0)
+    w_backward = jnp.pad(w_ordered, ((0, 0), (0, lane_pad), (0, lane_pad)))
     w_forward = w_backward.transpose(0, 2, 1).reshape(kvol * LANES, LANES)
     down_pad = jnp.pad(w_down, ((0, 0), (0, 0), (0, lane_pad)))
 
@@ -531,7 +566,7 @@
     accumulators = 8
     scattered = pl.pallas_call(
         functools.partial(scatter_kernel, levels, halo, stages),
-        grid=(kvol,),
+        grid=(kvol - 1,),
         in_specs=[
             pl.BlockSpec(memory_space=pl.ANY),
             vmem_full((vdev, LANES)),
@@ -549,23 +584,25 @@
     )(index, grad_pre, w_backward)
     incoming = [from_partner(scattered[1 + level], level, bits_member) for level in range(levels)]
 
+    grad_w, grad_down = pl.pallas_call(
+        unpack_kernel,
+        in_specs=[vmem_full((devices * share, LANES))],
+        out_specs=[vmem_full((kvol, chans, chans)), vmem_full((noct, c2, chans))],
+        out_shape=[shape((kvol, chans, chans), F32), shape((noct, c2, chans), F32)],
+        compiler_params=params(),
+        name="unpack",
+    )(full)
+    *incoming, grad_w, grad_down = lax.optimization_barrier((*incoming, grad_w, grad_down))
+
     grad_feats = pl.pallas_call(
         functools.partial(finish_kernel, levels),
         in_specs=[smem_full((1, levels * halo)), vmem_full((vdev, LANES))] + [vmem_full((halo, LANES))] * levels,
         out_specs=vmem_full((chans, vdev)),
         out_shape=shape((chans, vdev), F32),
-        scratch_shapes=[pltpu.VMEM((levels * halo, LANES), F32)] + [pltpu.VMEM((vdev, LANES), F32)] * 4,
+        scratch_shapes=[pltpu.VMEM((levels * halo, LANES), F32)] + [pltpu.VMEM((vdev, LANES), F32)] * 8,
         compiler_params=params(),
         name="finish",
     )(outgoing, scattered[0], *incoming)
-    grad_w, grad_down = pl.pallas_call(
-        unpack_kernel,
-        in_specs=[vmem_full((devices * share, LANES))],
-        out_specs=[vmem_full((kvol, chans, chans)), vmem_full((noct, c2, chans))],
-        out_shape=[shape((kvol, chans, chans), F32), shape((noct, c2, chans), F32)],
-        compiler_params=params(),
-        name="unpack",
-    )(full)
     return coarse_out, grad_feats, grad_w, grad_down
 
 

time: 323 us -> 320 us (level)
  transfers between devices with their start and end apart: 29 -> 29, of which waited for: 4 -> 2; matrix products, arithmetic and copies ran while one was open for 6% -> 7% of each run, Pallas kernels for 57% -> 56%
where the time goes in v4:
time: 320 us
  Pallas kernels  212 us (66%)
  starting transfers between devices  39.4 us (12%)
  blocking collectives  23.1 us (7%)
  between operations  14.6 us (5%)
  matrix products  14 us (4%)
  local copies, waits for them, and re-layouts  8.48 us (3%)
  other arithmetic  4.02 us (1%)
  waiting for transfers between devices  3.84 us (1%)
    pallas_call x1, Pallas kernels, shards(): pl.pallas_call(functools.partial(scatter_kernel, levels, halo, stages), g...  88.3 us
    pallas_call x1, Pallas kernels, shards(): pl.pallas_call(functools.partial(gather_kernel, levels, halo), grid=(kvol...  65.3 us
    ppermute x28, starting transfers between devices, from_partner(): return lax.ppermute(value, axis, pairs)  39.4 us
    all_to_all x1, blocking collectives, shards(): lax.all_to_all(packed.reshape(devices, share, LANES), both, split_axis=0,...  23.1 us
    pallas_call x1, Pallas kernels, shards(): pl.pallas_call(weights_kernel, grid=(kvol // group,), in_specs=[vmem_full...  14.5 us
    dot_general x1, matrix products, shards(): pre = jnp.dot(gathered, w_forward, preferred_element_type=F32)  14 us
    pallas_call x1, Pallas kernels, shards(): pl.pallas_call(functools.partial(pool_kernel, levels, chans), in_specs=[s...  9.33 us
    pallas_call x1, Pallas kernels, shards(): pl.pallas_call(functools.partial(middle_kernel, levels), in_specs=[smem_f...  7.68 us
  transfers between devices with their start and end apart: 29, of which 2 were waited for; matrix products, arithmetic and copies ran while one was open for 7% of the time, Pallas kernels for 56%

profile of v4, /device:TPU:0, one launch (start us, length us, event | category | flops | bytes accessed | tf_op | source)
XLA Modules:
  0.0 319.5 jit_solution(5066991391170296511)
XLA Ops:
  7.2 6.1 %prepare.1 = (bf16[272,128]{1,0:T(8,128)(2,1)}, bf16[272,128]{1,0:T(8,128)(2,1)}, bf16[272,128]{1,0:T(8,128)(2,1)}, bf16[272,128]{1,0:T(8,128)(2,1)}, bf16[272,1...) custom-call(s32[1]{0:T(128)} %bitcast.me_ref, ...), custom_call_target="tpu_custom_call" | custom-call | tf_op jit(solution)/shard_map/prepare/pallas_call | solution.py:440
  13.3 1.6 collective-permute-start
  14.9 2.7 collective-permute-start.1
  17.7 1.9 collective-permute-start.2
  19.6 3.6 %collective-permute-start.3 = (bf16[272,128]{1,0:T(8,128)(2,1)}, bf16[272,128]{1,0:T(8,128)(2,1)S(1)}, u32[]{:S(2)}, u32[]{:S(2)}) collective-permute-start(bf16[272,128]{1,0:T(8,128)(2,1)} %get-tuple-element.71), channel_id=1, source_target_pairs={{0,8},{1,9},{2,10},{3,11},{4,12},{5,13},{6,14},{7,15},{8,0},{9,1},... | collective-permute-start | bytes 208904 | tf_op jit(solution)/shard_map/ppermute | solution.py:23
  23.9 1.1 fusion.11
  25.9 1.6 collective-permute-start.5
  27.5 3.0 collective-permute-start.6
  30.5 1.2 fusion.8.weight_ref
  32.5 1.2 reshape.65.index_ref
  33.8 1.3 copy.14
  35.9 7.3 %parents.1 = (f32[4104,128]{1,0:T(8,128)}, f32[4096,128]{1,0:T(8,128)}) custom-call(s32[1,4096]{1,0:T(1,128)} %get-tuple-element.75.self_ref, bf16[512,192]{1,0:T(8,128)(2,1)} %bitcast.29, bf16[8,192,128]{2,1,0:T(8,128)(2,1)} %pad.9.weight_ref), custom_call_target="tpu_custom_call" | custom-call | tf_op jit(solution)/shard_map/parents/pallas_call | solution.py:457
  44.0 3.1 answer.1
  47.3 1.7 collective-permute-start.8
  49.9 65.3 %gather.1.taken_ref = bf16[4096,3456]{1,0:T(8,128)(2,1)} custom-call(s32[26,1,4096]{2,1,0:T(1,128)} %reshape.65.index_ref, f32[4096,128]{1,0:T(8,128)} %get-tuple-element.87.local_ref, bf16[272,128]{1,0:T(8,128)(2,1)} %copy-done.4, bf16[272,128]{1,0:T(8,128)(2,1)} %copy-done.5, bf16[272,128]{1,0:T(8,128)(2,1)} %copy-done.6, bf16[272,128]{1,0:T(8,128)(2,1)} %copy-done.7, ...), custom_call_target="tpu_custom_call" | custom-call | bytes 300000000 | tf_op jit(solution)/shard_map/gather/pallas_call | solution.py:484
  116.0 2.1 collective-permute-start.13
  118.1 14.0 %fusion.13.pre_ref = f32[4096,128]{1,0:T(8,128)} fusion(bf16[4096,3456]{1,0:T(8,128)(2,1)} %gather.1.taken_ref, bf16[3456,128]{1,0:T(8,128)(2,1)S(1)} %bitcast.30), kind=kOutput, calls=%fused_computation.27 | convolution fusion | flops 3623878656 | bytes 31293440 | tf_op jit(solution)/shard_map/dot_general | solution.py:502
  132.8 7.7 %middle.1 = (bf16[4096,128]{1,0:T(8,128)(2,1)}, bf16[128,4096]{1,0:T(8,128)(2,1)}, f32[4096,128]{1,0:T(8,128)}, bf16[128,128]{1,0:T(8,128)(2,1)}, bf16[128,128]{...) custom-call(s32[1,896]{1,0:T(1,128)} %get-tuple-element.85.list_ref,, ...), custom_call_target="tpu_custom_call" | custom-call | tf_op jit(solution)/shard_map/middle/pallas_call | solution.py:504
  141.1 2.7 collective-permute-start.15
  143.8 1.4 collective-permute-start.16
  145.2 4.1 %collective-permute-start.17 = (bf16[128,128]{1,0:T(8,128)(2,1)}, bf16[128,128]{1,0:T(8,128)(2,1)S(1)}, u32[]{:S(2)}, u32[]{:S(2)}) collective-permute-start(bf16[128,128]{1,0:T(8,128)(2,1)} %get-tuple-element.102), channel_id=1, source_target_pairs={{0,8},{1,9},{2,10},{3,11},{4,12},{5,13},{6,14},{7,15},{8,0},{9,1},... | collective-permute-start | bytes 98312 | tf_op jit(solution)/shard_map/ppermute | solution.py:23
  149.7 4.1 %collective-permute-start.20 = (bf16[128,128]{1,0:T(8,128)(2,1)}, bf16[128,128]{1,0:T(8,128)(2,1)S(1)}, u32[]{:S(2)}, u32[]{:S(2)}) collective-permute-start(bf16[128,128]{1,0:T(8,128)(2,1)} %get-tuple-element.105), channel_id=1, source_target_pairs={{0,64},{16,80},{32,96},{48,112},{64,0},{80,16},{96,32},{112,48},{1... | collective-permute-start | bytes 98312 | tf_op jit(solution)/shard_map/ppermute | solution.py:23
  153.9 14.5 %weights.1 = bf16[2592,128]{1,0:T(8,128)(2,1)} custom-call(bf16[128,4096]{1,0:T(8,128)(2,1)} %get-tuple-element.107.turned_ref, bf16[4096,3456]{1,0:T(8,128)(2,1)} %gather.1.taken_ref), custom_call_target="tpu_custom_call" | custom-call | bytes 40000000 | tf_op jit(solution)/shard_map/weights/pallas_call | solution.py:526
  169.1 9.3 %pool.1 = (bf16[192,512]{1,0:T(8,128)(2,1)}, bf16[1504,128]{1,0:T(8,128)(2,1)}) custom-call(s32[1,896]{1,0:T(1,128)} %fusion.10.keys_ref, s32[1,4096]{1,0:T(1,128)} %get-tuple-element.75.self_ref, f32[4096,128]{1,0:T(8,128)} %get-tuple-element.98.act_ref, bf16[192,512]{1,0:T(8,128)(2,1)} %grad_ref.1, bf16[8,192,128]{2,1,0:T(8,128)(2,1)} %pad.9.weight_ref, ...), custom_call_target="tpu_custom_call" | custom-call | tf_op jit(solution)/shard_map/pool/pallas_call | solution.py:537
  179.5 23.1 %all_to_all.5 = bf16[128,32,128]{2,1,0:T(8,128)(2,1)S(1)} all-to-all(bf16[128,32,128]{2,1,0:T(8,128)(2,1)S(1)} %bitcast.28), channel_id=1, replica_groups=mesh['group'=8,'member'=16] {'group','member'}, dimensions={0} | all-to-all | bytes 2097152 | tf_op jit(solution)/shard_map/all_to_all | solution.py:559
  203.4 88.3 %scatter.1 = (f32[4096,128]{1,0:T(8,128)}, bf16[256,128]{1,0:T(8,128)(2,1)}, bf16[256,128]{1,0:T(8,128)(2,1)}, bf16[256,128]{1,0:T(8,128)(2,1)}, bf16[256,128]{1...) custom-call(s32[26,1,4096]{2,1,0:T(1,128)} %reshape.65.index_ref, ...), custom_call_target="tpu_custom_call" | custom-call | bytes 400000000 | tf_op jit(solution)/shard_map/scatter/pallas_call | solution.py:567
  292.6 2.0 collective-permute-start.22
  295.3 1.7 collective-permute-start.24
  297.1 1.5 collective-permute-done.22.refs_1_
  299.2 3.0 unpack.1
  302.3 2.3 collective-permute-done.27.refs_6_
  305.2 7.5 %finish.1 = f32[96,4096]{1,0:T(8,128)} custom-call(s32[1,1792]{1,0:T(1,128)} %bitcast.32, f32[4096,128]{1,0:T(8,128)} %get-tuple-element.112.local_ref, bf16[256,128]{1,0:T(8,128)(2,1)} %copy-done.11, bf16[256,128]{1,0:T(8,128)(2,1)} %copy-done.12, bf16[256,128]{1,0:T(8,128)(2,1)} %copy-done.13, bf16[256,128]{1,0:T(8,128)(2,1)} %copy-done.14, ...), custom_call_target="tpu_custom_call" | custom-call | tf_op jit(solution)/shard_map/finish/pallas_call | solution.py:597
  (132 shorter events, 12.9 us)
Async XLA Ops:
  7.2 292.1 %all-gather.2.cloned.1.call-start = ((), (), s32[]{:S(2)}) async-start(), calls=%async_computation.1 | async-start | bytes 2113536 | tf_op jit(solution)/shard_map/all_gather | solution.py:564
  13.3 12.2 %collective-permute-start = (bf16[272,128]{1,0:T(8,128)(2,1)}, bf16[272,128]{1,0:T(8,128)(2,1)S(1)}, u32[]{:S(2)}, u32[]{:S(2)}) collective-permute-start(bf16[272,128]{1,0:T(8,128)(2,1)} %get-tuple-element.68), channel_id=1, source_target_pairs={{0,1},{1,0},{2,3},{3,2},{4,5},{5,4},{6,7},{7,6},{8,9},{9,8},{10,11... | collective-permute-start | bytes 208904 | tf_op jit(solution)/shard_map/ppermute | solution.py:23
  14.9 12.6 %collective-permute-start.1 = (bf16[272,128]{1,0:T(8,128)(2,1)}, bf16[272,128]{1,0:T(8,128)(2,1)S(1)}, u32[]{:S(2)}, u32[]{:S(2)}) collective-permute-start(bf16[272,128]{1,0:T(8,128)(2,1)} %get-tuple-element.69), channel_id=1, source_target_pairs={{0,2},{1,3},{2,0},{3,1},{4,6},{5,7},{6,4},{7,5},{8,10},{9,11},{10,... | collective-permute-start | bytes 208904 | tf_op jit(solution)/shard_map/ppermute | solution.py:23
  17.7 25.6 %collective-permute-start.2 = (bf16[272,128]{1,0:T(8,128)(2,1)}, bf16[272,128]{1,0:T(8,128)(2,1)S(1)}, u32[]{:S(2)}, u32[]{:S(2)}) collective-permute-start(bf16[272,128]{1,0:T(8,128)(2,1)} %get-tuple-element.70), channel_id=1, source_target_pairs={{0,4},{1,5},{2,6},{3,7},{4,0},{5,1},{6,2},{7,3},{8,12},{9,13},{10,... | collective-permute-start | bytes 208904 | tf_op jit(solution)/shard_map/ppermute | solution.py:23
  19.6 23.7 %collective-permute-start.3 = (bf16[272,128]{1,0:T(8,128)(2,1)}, bf16[272,128]{1,0:T(8,128)(2,1)S(1)}, u32[]{:S(2)}, u32[]{:S(2)}) collective-permute-start(bf16[272,128]{1,0:T(8,128)(2,1)} %get-tuple-element.71), channel_id=1, source_target_pairs={{0,8},{1,9},{2,10},{3,11},{4,12},{5,13},{6,14},{7,15},{8,0},{9,1},... | collective-permute-start | bytes 208904 | tf_op jit(solution)/shard_map/ppermute | solution.py:23
  23.2 20.1 %collective-permute-start.4 = (bf16[272,128]{1,0:T(8,128)(2,1)}, bf16[272,128]{1,0:T(8,128)(2,1)S(1)}, u32[]{:S(2)}, u32[]{:S(2)}) collective-permute-start(bf16[272,128]{1,0:T(8,128)(2,1)} %get-tuple-element.72), channel_id=1, source_target_pairs={{0,16},{16,0},{32,48},{48,32},{64,80},{80,64},{96,112},{112,96},{1... | collective-permute-start | bytes 208904 | tf_op jit(solution)/shard_map/ppermute | solution.py:23
  25.9 17.4 %collective-permute-start.5 = (bf16[272,128]{1,0:T(8,128)(2,1)S(1)}, bf16[272,128]{1,0:T(8,128)(2,1)S(1)}, u32[]{:S(2)}, u32[]{:S(2)}) collective-permute-start(bf16[272,128]{1,0:T(8,128)(2,1)S(1)} %copy-done.33), channel_id=1, source_target_pairs={{0,32},{16,48},{32,0},{48,16},{64,96},{80,112},{96,64},{112,80},{1... | collective-permute-start | bytes 208904 | tf_op jit(solution)/shard_map/ppermute | solution.py:23
  27.5 15.8 %collective-permute-start.6 = (bf16[272,128]{1,0:T(8,128)(2,1)S(1)}, bf16[272,128]{1,0:T(8,128)(2,1)S(1)}, u32[]{:S(2)}, u32[]{:S(2)}) collective-permute-start(bf16[272,128]{1,0:T(8,128)(2,1)S(1)} %copy-done.32), channel_id=1, source_target_pairs={{0,64},{16,80},{32,96},{48,112},{64,0},{80,16},{96,32},{112,48},{1... | collective-permute-start | bytes 208904 | tf_op jit(solution)/shard_map/ppermute | solution.py:23
  47.1 68.1 %collective-permute-start.7 = (bf16[128,128]{1,0:T(8,128)(2,1)}, bf16[128,128]{1,0:T(8,128)(2,1)S(1)}, u32[]{:S(2)}, u32[]{:S(2)}) collective-permute-start(bf16[128,128]{1,0:T(8,128)(2,1)} %get-tuple-element.91), channel_id=1, source_target_pairs={{0,1},{1,0},{2,3},{3,2},{4,5},{5,4},{6,7},{7,6},{8,9},{9,8},{10,11... | collective-permute-start | bytes 98312 | tf_op jit(solution)/shard_map/ppermute | solution.py:23
  47.3 68.7 %collective-permute-start.8 = (bf16[128,128]{1,0:T(8,128)(2,1)}, bf16[128,128]{1,0:T(8,128)(2,1)S(1)}, u32[]{:S(2)}, u32[]{:S(2)}) collective-permute-start(bf16[128,128]{1,0:T(8,128)(2,1)} %get-tuple-element.92), channel_id=1, source_target_pairs={{0,2},{1,3},{2,0},{3,1},{4,6},{5,7},{6,4},{7,5},{8,10},{9,11},{10,... | collective-permute-start | bytes 98312 | tf_op jit(solution)/shard_map/ppermute | solution.py:23
  49.1 83.0 %collective-permute-start.9 = (bf16[128,128]{1,0:T(8,128)(2,1)}, bf16[128,128]{1,0:T(8,128)(2,1)S(1)}, u32[]{:S(2)}, u32[]{:S(2)}) collective-permute-start(bf16[128,128]{1,0:T(8,128)(2,1)} %get-tuple-element.93), channel_id=1, source_target_pairs={{0,4},{1,5},{2,6},{3,7},{4,0},{5,1},{6,2},{7,3},{8,12},{9,13},{10,... | collective-permute-start | bytes 98312 | tf_op jit(solution)/shard_map/ppermute | solution.py:23
  49.1 83.1 %collective-permute-start.10 = (bf16[128,128]{1,0:T(8,128)(2,1)}, bf16[128,128]{1,0:T(8,128)(2,1)S(1)}, u32[]{:S(2)}, u32[]{:S(2)}) collective-permute-start(bf16[128,128]{1,0:T(8,128)(2,1)} %get-tuple-element.94), channel_id=1, source_target_pairs={{0,8},{1,9},{2,10},{3,11},{4,12},{5,13},{6,14},{7,15},{8,0},{9,1},... | collective-permute-start | bytes 98312 | tf_op jit(solution)/shard_map/ppermute | solution.py:23
  49.9 82.3 %collective-permute-start.11 = (bf16[128,128]{1,0:T(8,128)(2,1)}, bf16[128,128]{1,0:T(8,128)(2,1)S(1)}, u32[]{:S(2)}, u32[]{:S(2)}) collective-permute-start(bf16[128,128]{1,0:T(8,128)(2,1)} %get-tuple-element.95), channel_id=1, source_target_pairs={{0,16},{16,0},{32,48},{48,32},{64,80},{80,64},{96,112},{112,96},{1... | collective-permute-start | bytes 98312 | tf_op jit(solution)/shard_map/ppermute | solution.py:23
  49.9 65.4 %copy-start.35 = (bf16[128,128]{1,0:T(8,128)(2,1)S(1)}, bf16[128,128]{1,0:T(8,128)(2,1)}, u32[]{:S(2)}) copy-start(bf16[128,128]{1,0:T(8,128)(2,1)} %get-tuple-element.96) | copy-start | bytes 98308
  49.9 66.1 %copy-start.34 = (bf16[128,128]{1,0:T(8,128)(2,1)S(1)}, bf16[128,128]{1,0:T(8,128)(2,1)}, u32[]{:S(2)}) copy-start(bf16[128,128]{1,0:T(8,128)(2,1)} %get-tuple-element.97) | copy-start | bytes 98308
  115.3 16.9 %collective-permute-start.12 = (bf16[128,128]{1,0:T(8,128)(2,1)S(1)}, bf16[128,128]{1,0:T(8,128)(2,1)S(1)}, u32[]{:S(2)}, u32[]{:S(2)}) collective-permute-start(bf16[128,128]{1,0:T(8,128)(2,1)S(1)} %copy-done.35), channel_id=1, source_target_pairs={{0,32},{16,48},{32,0},{48,16},{64,96},{80,112},{96,64},{112,80},{1... | collective-permute-start | bytes 98312 | tf_op jit(solution)/shard_map/ppermute | solution.py:23
  116.0 16.2 %collective-permute-start.13 = (bf16[128,128]{1,0:T(8,128)(2,1)S(1)}, bf16[128,128]{1,0:T(8,128)(2,1)S(1)}, u32[]{:S(2)}, u32[]{:S(2)}) collective-permute-start(bf16[128,128]{1,0:T(8,128)(2,1)S(1)} %copy-done.34), channel_id=1, source_target_pairs={{0,64},{16,80},{32,96},{48,112},{64,0},{80,16},{96,32},{112,48},{1... | collective-permute-start | bytes 98312 | tf_op jit(solution)/shard_map/ppermute | solution.py:23
  140.5 8.8 %collective-permute-start.14 = (bf16[128,128]{1,0:T(8,128)(2,1)}, bf16[128,128]{1,0:T(8,128)(2,1)S(1)}, u32[]{:S(2)}, u32[]{:S(2)}) collective-permute-start(bf16[128,128]{1,0:T(8,128)(2,1)} %get-tuple-element.99), channel_id=1, source_target_pairs={{0,1},{1,0},{2,3},{3,2},{4,5},{5,4},{6,7},{7,6},{8,9},{9,8},{10,11... | collective-permute-start | bytes 98312 | tf_op jit(solution)/shard_map/ppermute | solution.py:23
  141.1 8.6 %collective-permute-start.15 = (bf16[128,128]{1,0:T(8,128)(2,1)}, bf16[128,128]{1,0:T(8,128)(2,1)S(1)}, u32[]{:S(2)}, u32[]{:S(2)}) collective-permute-start(bf16[128,128]{1,0:T(8,128)(2,1)} %get-tuple-element.100), channel_id=1, source_target_pairs={{0,2},{1,3},{2,0},{3,1},{4,6},{5,7},{6,4},{7,5},{8,10},{9,11},{10,... | collective-permute-start | bytes 98312 | tf_op jit(solution)/shard_map/ppermute | solution.py:23
  143.8 24.6 %collective-permute-start.16 = (bf16[128,128]{1,0:T(8,128)(2,1)}, bf16[128,128]{1,0:T(8,128)(2,1)S(1)}, u32[]{:S(2)}, u32[]{:S(2)}) collective-permute-start(bf16[128,128]{1,0:T(8,128)(2,1)} %get-tuple-element.101), channel_id=1, source_target_pairs={{0,4},{1,5},{2,6},{3,7},{4,0},{5,1},{6,2},{7,3},{8,12},{9,13},{10,... | collective-permute-start | bytes 98312 | tf_op jit(solution)/shard_map/ppermute | solution.py:23
  145.2 23.2 %collective-permute-start.17 = (bf16[128,128]{1,0:T(8,128)(2,1)}, bf16[128,128]{1,0:T(8,128)(2,1)S(1)}, u32[]{:S(2)}, u32[]{:S(2)}) collective-permute-start(bf16[128,128]{1,0:T(8,128)(2,1)} %get-tuple-element.102), channel_id=1, source_target_pairs={{0,8},{1,9},{2,10},{3,11},{4,12},{5,13},{6,14},{7,15},{8,0},{9,1},... | collective-permute-start | bytes 98312 | tf_op jit(solution)/shard_map/ppermute | solution.py:23
  149.3 19.2 %collective-permute-start.18 = (bf16[128,128]{1,0:T(8,128)(2,1)}, bf16[128,128]{1,0:T(8,128)(2,1)S(1)}, u32[]{:S(2)}, u32[]{:S(2)}) collective-permute-start(bf16[128,128]{1,0:T(8,128)(2,1)} %get-tuple-element.103), channel_id=1, source_target_pairs={{0,16},{16,0},{32,48},{48,32},{64,80},{80,64},{96,112},{112,96},{1... | collective-permute-start | bytes 98312 | tf_op jit(solution)/shard_map/ppermute | solution.py:23
  149.3 19.1 %copy-start.25 = (bf16[128,128]{1,0:T(8,128)(2,1)}, bf16[128,128]{1,0:T(8,128)(2,1)S(1)}, u32[]{:S(2)}) copy-start(bf16[128,128]{1,0:T(8,128)(2,1)S(1)} %collective-permute-done.14.refs_0_) | copy-start | bytes 98308
  149.3 19.2 %collective-permute-start.19 = (bf16[128,128]{1,0:T(8,128)(2,1)}, bf16[128,128]{1,0:T(8,128)(2,1)S(1)}, u32[]{:S(2)}, u32[]{:S(2)}) collective-permute-start(bf16[128,128]{1,0:T(8,128)(2,1)} %get-tuple-element.104), channel_id=1, source_target_pairs={{0,32},{16,48},{32,0},{48,16},{64,96},{80,112},{96,64},{112,80},{1... | collective-permute-start | bytes 98312 | tf_op jit(solution)/shard_map/ppermute | solution.py:23
  149.7 18.7 %collective-permute-start.20 = (bf16[128,128]{1,0:T(8,128)(2,1)}, bf16[128,128]{1,0:T(8,128)(2,1)S(1)}, u32[]{:S(2)}, u32[]{:S(2)}) collective-permute-start(bf16[128,128]{1,0:T(8,128)(2,1)} %get-tuple-element.105), channel_id=1, source_target_pairs={{0,64},{16,80},{32,96},{48,112},{64,0},{80,16},{96,32},{112,48},{1... | collective-permute-start | bytes 98312 | tf_op jit(solution)/shard_map/ppermute | solution.py:23
  291.7 5.3 %collective-permute-start.21 = (bf16[256,128]{1,0:T(8,128)(2,1)}, bf16[256,128]{1,0:T(8,128)(2,1)S(1)}, u32[]{:S(2)}, u32[]{:S(2)}) collective-permute-start(bf16[256,128]{1,0:T(8,128)(2,1)} %get-tuple-element.113), channel_id=1, source_target_pairs={{0,1},{1,0},{2,3},{3,2},{4,5},{5,4},{6,7},{7,6},{8,9},{9,8},{10,11... | collective-permute-start | bytes 196616 | tf_op jit(solution)/shard_map/ppermute | solution.py:23
  292.6 6.0 %collective-permute-start.22 = (bf16[256,128]{1,0:T(8,128)(2,1)}, bf16[256,128]{1,0:T(8,128)(2,1)S(1)}, u32[]{:S(2)}, u32[]{:S(2)}) collective-permute-start(bf16[256,128]{1,0:T(8,128)(2,1)} %get-tuple-element.114), channel_id=1, source_target_pairs={{0,2},{1,3},{2,0},{3,1},{4,6},{5,7},{6,4},{7,5},{8,10},{9,11},{10,... | collective-permute-start | bytes 196616 | tf_op jit(solution)/shard_map/ppermute | solution.py:23
  294.6 7.6 %collective-permute-start.23 = (bf16[256,128]{1,0:T(8,128)(2,1)}, bf16[256,128]{1,0:T(8,128)(2,1)S(1)}, u32[]{:S(2)}, u32[]{:S(2)}) collective-permute-start(bf16[256,128]{1,0:T(8,128)(2,1)} %get-tuple-element.115), channel_id=1, source_target_pairs={{0,4},{1,5},{2,6},{3,7},{4,0},{5,1},{6,2},{7,3},{8,12},{9,13},{10,... | collective-permute-start | bytes 196616 | tf_op jit(solution)/shard_map/ppermute | solution.py:23
  295.3 7.0 %collective-permute-start.24 = (bf16[256,128]{1,0:T(8,128)(2,1)}, bf16[256,128]{1,0:T(8,128)(2,1)S(1)}, u32[]{:S(2)}, u32[]{:S(2)}) collective-permute-start(bf16[256,128]{1,0:T(8,128)(2,1)} %get-tuple-element.116), channel_id=1, source_target_pairs={{0,8},{1,9},{2,10},{3,11},{4,12},{5,13},{6,14},{7,15},{8,0},{9,1},... | collective-permute-start | bytes 196616 | tf_op jit(solution)/shard_map/ppermute | solution.py:23
  297.0 5.3 %collective-permute-start.25 = (bf16[256,128]{1,0:T(8,128)(2,1)}, bf16[256,128]{1,0:T(8,128)(2,1)S(1)}, u32[]{:S(2)}, u32[]{:S(2)}) collective-permute-start(bf16[256,128]{1,0:T(8,128)(2,1)} %get-tuple-element.117), channel_id=1, source_target_pairs={{0,16},{16,0},{32,48},{48,32},{64,80},{80,64},{96,112},{112,96},{1... | collective-permute-start | bytes 196616 | tf_op jit(solution)/shard_map/ppermute | solution.py:23
  297.0 5.3 %collective-permute-start.26 = (bf16[256,128]{1,0:T(8,128)(2,1)}, bf16[256,128]{1,0:T(8,128)(2,1)S(1)}, u32[]{:S(2)}, u32[]{:S(2)}) collective-permute-start(bf16[256,128]{1,0:T(8,128)(2,1)} %get-tuple-element.118), channel_id=1, source_target_pairs={{0,32},{16,48},{32,0},{48,16},{64,96},{80,112},{96,64},{112,80},{1... | collective-permute-start | bytes 196616 | tf_op jit(solution)/shard_map/ppermute | solution.py:23
  298.6 6.0 %collective-permute-start.27 = (bf16[256,128]{1,0:T(8,128)(2,1)}, bf16[256,128]{1,0:T(8,128)(2,1)S(1)}, u32[]{:S(2)}, u32[]{:S(2)}) collective-permute-start(bf16[256,128]{1,0:T(8,128)(2,1)} %get-tuple-element.119), channel_id=1, source_target_pairs={{0,64},{16,80},{32,96},{48,112},{64,0},{80,16},{96,32},{112,48},{1... | collective-permute-start | bytes 196616 | tf_op jit(solution)/shard_map/ppermute | solution.py:23
  (33 other events, 189.0 us)
Sparse Core Ops, SparseCore 0:
  203.6 60.7 all-gather.1

commit v5 on v4

--- a/solution.py
+++ b/solution.py
@@ -227,28 +227,37 @@
         out_ref[...] = local_ref[...].astype(BF16)
 
 
-def middle_kernel(levels, list_ref, pre_ref, rows_ref, *refs):
+def middle_kernel(levels, list_ref, taken_ref, weight_ref, rows_ref, *refs):
     returned = refs[:levels]
     grad_ref, turned_ref, act_ref = refs[levels : levels + 3]
     sends = refs[levels + 3 : 2 * levels + 3]
-    rows, back, act, out = refs[2 * levels + 3 :]
-    vdev = pre_ref.shape[0]
+    rows, back, act, out, pre_buf = refs[2 * levels + 3 :]
+    vdev = rows_ref.shape[0]
     slots = returned[0].shape[0]
-    rows[pl.ds(0, vdev), :] = rows_ref[...]
-    for level in range(levels):
-        back[pl.ds(level * slots, slots), :] = returned[level][...].astype(F32)
-
-    def patch(step, _):
-        base = pl.multiple_of(step * 64, 64)
-        for j in range(64):
-            rows[pl.ds(list_ref[0, base + j], 1), :] = back[pl.ds(base + j, 1), :]
-        return 0
-
-    lax.fori_loop(0, levels * slots // 64, patch, 0)
+    block = taken_ref.shape[0]
+    piece = 2 * LANES
+    turn = pl.program_id(0)
+
+    @pl.when(turn == 0)
+    def _():
+        rows[pl.ds(0, vdev), :] = rows_ref[...]
+        for level in range(levels):
+            back[pl.ds(level * slots, slots), :] = returned[level][...].astype(F32)
+
+        def patch(step, _):
+            base = pl.multiple_of(step * 64, 64)
+            for j in range(64):
+                rows[pl.ds(list_ref[0, base + j], 1), :] = back[pl.ds(base + j, 1), :]
+            return 0
+
+        lax.fori_loop(0, levels * slots // 64, patch, 0)
+        act[pl.ds(vdev, SUB), :] = jnp.zeros((SUB, LANES), F32)
+
+    pre_buf[...] = jnp.dot(taken_ref[...], weight_ref[...], preferred_element_type=F32)
 
     def point(step, _):
-        part = pl.ds(pl.multiple_of(step * 4 * LANES, 4 * LANES), 4 * LANES)
-        pre = pre_ref[part, :]
+        part = pl.ds(pl.multiple_of(turn * block + step * piece, piece), piece)
+        pre = pre_buf[pl.ds(pl.multiple_of(step * piece, piece), piece), :]
         sig = 1.0 / (1.0 + jnp.exp(-pre))
         value = (pre * sig).astype(BF16).astype(F32)
         act[part, :] = value
@@ -258,11 +267,13 @@
         turned_ref[:, part] = grad.T.astype(BF16)
         return 0
 
-    lax.fori_loop(0, vdev // (4 * LANES), point, 0)
-    act[pl.ds(vdev, SUB), :] = jnp.zeros((SUB, LANES), F32)
-    copy_rows(levels * slots, 64, lambda r: list_ref[0, r], act, out)
-    for level in range(levels):
-        sends[level][...] = out[pl.ds(level * slots, slots), :].astype(BF16)
+    lax.fori_loop(0, block // piece, point, 0)
+
+    @pl.when(turn == pl.num_programs(0) - 1)
+    def _():
+        copy_rows(levels * slots, 64, lambda r: list_ref[0, r], act, out)
+        for level in range(levels):
+            sends[level][...] = out[pl.ds(level * slots, slots), :].astype(BF16)
 
 
 def weights_kernel(turned_ref, taken_ref, out_ref):
@@ -499,12 +510,17 @@
         cost_estimate=pl.CostEstimate(flops=0, bytes_accessed=300_000_000, transcendentals=0),
         name="gather",
     )(index, table, *received)
-    pre = jnp.dot(gathered, w_forward, preferred_element_type=F32)
-
+
+    block = vdev // 4
     middle = pl.pallas_call(
         functools.partial(middle_kernel, levels),
-        in_specs=[smem_full((1, levels * slots))]
-        + [vmem_full((vdev, LANES))] * 2
+        grid=(vdev // block,),
+        in_specs=[
+            smem_full((1, levels * slots)),
+            pl.BlockSpec((block, kvol * LANES), lambda i: (i, 0)),
+            vmem_full((kvol * LANES, LANES)),
+            vmem_full((vdev, LANES)),
+        ]
         + [vmem_full((slots, LANES))] * levels,
         out_specs=[vmem_full((vdev, LANES)), vmem_full((LANES, vdev)), vmem_full((vdev, LANES))]
         + [vmem_full((slots, LANES))] * levels,
@@ -515,10 +531,12 @@
             pltpu.VMEM((levels * slots, LANES), F32),
             pltpu.VMEM((vdev + SUB, LANES), F32),
             pltpu.VMEM((levels * slots, LANES), F32),
+            pltpu.VMEM((block, LANES), F32),
         ],
         compiler_params=params(),
+        cost_estimate=pl.CostEstimate(flops=0, bytes_accessed=40_000_000, transcendentals=0),
         name="middle",
-    )(send_list, pre, rows, *returned)
+    )(send_list, gathered, w_forward, rows, *returned)
     grad_pre, grad_turned, act = middle[:3]
     came = [from_partner(middle[3 + level], level, bits_member) for level in range(levels)]
 
@@ -599,7 +617,7 @@
         in_specs=[smem_full((1, levels * halo)), vmem_full((vdev, LANES))] + [vmem_full((halo, LANES))] * levels,
         out_specs=vmem_full((chans, vdev)),
         out_shape=shape((chans, vdev), F32),
-        scratch_shapes=[pltpu.VMEM((levels * halo, LANES), F32)] + [pltpu.VMEM((vdev, LANES), F32)] * 8,
+        scratch_shapes=[pltpu.VMEM((levels * halo, LANES), F32)] + [pltpu.VMEM((vdev, LANES), F32)] * 4,
         compiler_params=params(),
         name="finish",
     )(outgoing, scattered[0], *incoming)

time: 320 us -> 317 us (level)
  matrix products: 14 us -> 0 us
  Pallas kernels: 212 us -> 223 us
    dot_general x1 -> x0, matrix products: 14 us -> none  [shards(): pre = jnp.dot(gathered, w_forward, preferred_element_type=F32)]
    pallas_call x1, Pallas kernels: 7.68 us -> 18.6 us  [shards(): pl.pallas_call(functools.partial(middle_kernel, levels), grid=(vdev // bl...]
  transfers between devices with their start and end apart: 29 -> 29, of which waited for: 2 -> 4; matrix products, arithmetic and copies ran while one was open for 7% -> 3% of each run, Pallas kernels for 56% -> 56%
where the time goes in v5:
time: 317 us; the launch traced here: 316 us
  Pallas kernels  223 us (70%)
  starting transfers between devices  36.4 us (11%)
  blocking collectives  23.1 us (7%)
  between operations  14.6 us (5%)
  local copies, waits for them, and re-layouts  8.79 us (3%)
  waiting for transfers between devices  6.45 us (2%)
  other arithmetic  4.03 us (1%)
    pallas_call x1, Pallas kernels, shards(): pl.pallas_call(functools.partial(scatter_kernel, levels, halo, stages), g...  88.3 us
    pallas_call x1, Pallas kernels, shards(): pl.pallas_call(functools.partial(gather_kernel, levels, halo), grid=(kvol...  65.3 us
    ppermute x28, starting transfers between devices, from_partner(): return lax.ppermute(value, axis, pairs)  36.4 us
    all_to_all x1, blocking collectives, shards(): lax.all_to_all(packed.reshape(devices, share, LANES), both, split_axis=0,...  23.1 us
    pallas_call x1, Pallas kernels, shards(): pl.pallas_call(functools.partial(middle_kernel, levels), grid=(vdev // bl...  18.6 us
    pallas_call x1, Pallas kernels, shards(): pl.pallas_call(weights_kernel, grid=(kvol // group,), in_specs=[vmem_full...  14.5 us
    pallas_call x1, Pallas kernels, shards(): pl.pallas_call(functools.partial(pool_kernel, levels, chans), in_specs=[s...  9.34 us
    pallas_call x1, Pallas kernels, shards(): pl.pallas_call(functools.partial(finish_kernel, levels), in_specs=[smem_f...  7.41 us
  transfers between devices with their start and end apart: 29, of which 4 were waited for; matrix products, arithmetic and copies ran while one was open for 3% of the time, Pallas kernels for 56%

profile of v5, /device:TPU:0, one launch (start us, length us, event | category | flops | bytes accessed | tf_op | source)
XLA Modules:
  0.0 316.3 jit_solution(11997089340776742530)
XLA Ops:
  7.2 6.1 %prepare.1 = (bf16[272,128]{1,0:T(8,128)(2,1)}, bf16[272,128]{1,0:T(8,128)(2,1)}, bf16[272,128]{1,0:T(8,128)(2,1)}, bf16[272,128]{1,0:T(8,128)(2,1)}, bf16[272,1...) custom-call(s32[1]{0:T(128)} %bitcast.me_ref, ...), custom_call_target="tpu_custom_call" | custom-call | tf_op jit(solution)/shard_map/prepare/pallas_call | solution.py:451
  13.3 1.6 collective-permute-start
  14.9 2.7 collective-permute-start.1
  17.7 1.9 collective-permute-start.2
  19.6 3.6 %collective-permute-start.3 = (bf16[272,128]{1,0:T(8,128)(2,1)}, bf16[272,128]{1,0:T(8,128)(2,1)S(1)}, u32[]{:S(2)}, u32[]{:S(2)}) collective-permute-start(bf16[272,128]{1,0:T(8,128)(2,1)} %get-tuple-element.71), channel_id=1, source_target_pairs={{0,8},{1,9},{2,10},{3,11},{4,12},{5,13},{6,14},{7,15},{8,0},{9,1},... | collective-permute-start | bytes 208904 | tf_op jit(solution)/shard_map/ppermute | solution.py:23
  23.9 1.1 fusion.11
  25.9 1.6 collective-permute-start.5
  27.5 3.0 collective-permute-start.6
  30.5 1.2 fusion.8.weight_ref
  32.5 1.2 reshape.65.index_ref
  33.7 1.6 copy.14
  36.2 7.3 %parents.1 = (f32[4104,128]{1,0:T(8,128)}, f32[4096,128]{1,0:T(8,128)}) custom-call(s32[1,4096]{1,0:T(1,128)} %get-tuple-element.75.self_ref, bf16[512,192]{1,0:T(8,128)(2,1)} %bitcast.28, bf16[8,192,128]{2,1,0:T(8,128)(2,1)} %pad.9.weight_ref), custom_call_target="tpu_custom_call" | custom-call | tf_op jit(solution)/shard_map/parents/pallas_call | solution.py:468
  44.3 3.1 answer.1
  47.6 1.7 collective-permute-start.8
  50.1 1.4 collective-permute-done.7.refs_0_
  51.7 1.6 collective-permute-done.8.refs_1_
  53.9 65.3 %gather.1.taken_ref = bf16[4096,3456]{1,0:T(8,128)(2,1)} custom-call(s32[26,1,4096]{2,1,0:T(1,128)} %reshape.65.index_ref, f32[4096,128]{1,0:T(8,128)} %get-tuple-element.87.local_ref, bf16[272,128]{1,0:T(8,128)(2,1)} %copy-done.4, bf16[272,128]{1,0:T(8,128)(2,1)} %copy-done.5, bf16[272,128]{1,0:T(8,128)(2,1)} %copy-done.6, bf16[272,128]{1,0:T(8,128)(2,1)} %copy-done.7, ...), custom_call_target="tpu_custom_call" | custom-call | bytes 300000000 | tf_op jit(solution)/shard_map/gather/pallas_call | solution.py:495
  119.9 18.6 %middle.1 = (bf16[4096,128]{1,0:T(8,128)(2,1)}, bf16[128,4096]{1,0:T(8,128)(2,1)}, f32[4096,128]{1,0:T(8,128)}, bf16[128,128]{1,0:T(8,128)(2,1)}, bf16[128,128]{...) custom-call(s32[1,896]{1,0:T(1,128)} %get-tuple-element.85.list_ref,, ...), custom_call_target="tpu_custom_call" | custom-call | bytes 40000000 | tf_op jit(solution)/shard_map/middle/pallas_call | solution.py:515
  138.5 1.9 collective-permute-start.14
  142.1 4.1 %collective-permute-start.17 = (bf16[128,128]{1,0:T(8,128)(2,1)}, bf16[128,128]{1,0:T(8,128)(2,1)S(1)}, u32[]{:S(2)}, u32[]{:S(2)}) collective-permute-start(bf16[128,128]{1,0:T(8,128)(2,1)} %get-tuple-element.102), channel_id=1, source_target_pairs={{0,8},{1,9},{2,10},{3,11},{4,12},{5,13},{6,14},{7,15},{8,0},{9,1},... | collective-permute-start | bytes 98312 | tf_op jit(solution)/shard_map/ppermute | solution.py:23
  146.7 4.1 %collective-permute-start.20 = (bf16[128,128]{1,0:T(8,128)(2,1)}, bf16[128,128]{1,0:T(8,128)(2,1)S(1)}, u32[]{:S(2)}, u32[]{:S(2)}) collective-permute-start(bf16[128,128]{1,0:T(8,128)(2,1)} %get-tuple-element.105), channel_id=1, source_target_pairs={{0,64},{16,80},{32,96},{48,112},{64,0},{80,16},{96,32},{112,48},{1... | collective-permute-start | bytes 98312 | tf_op jit(solution)/shard_map/ppermute | solution.py:23
  150.8 14.5 %weights.1 = bf16[2592,128]{1,0:T(8,128)(2,1)} custom-call(bf16[128,4096]{1,0:T(8,128)(2,1)} %get-tuple-element.107.turned_ref, bf16[4096,3456]{1,0:T(8,128)(2,1)} %gather.1.taken_ref), custom_call_target="tpu_custom_call" | custom-call | bytes 40000000 | tf_op jit(solution)/shard_map/weights/pallas_call | solution.py:544
  166.0 9.3 %pool.1 = (bf16[192,512]{1,0:T(8,128)(2,1)}, bf16[1504,128]{1,0:T(8,128)(2,1)}) custom-call(s32[1,896]{1,0:T(1,128)} %fusion.10.keys_ref, s32[1,4096]{1,0:T(1,128)} %get-tuple-element.75.self_ref, f32[4096,128]{1,0:T(8,128)} %get-tuple-element.98.act_ref, bf16[192,512]{1,0:T(8,128)(2,1)} %grad_ref.1, bf16[8,192,128]{2,1,0:T(8,128)(2,1)} %pad.9.weight_ref, ...), custom_call_target="tpu_custom_call" | custom-call | tf_op jit(solution)/shard_map/pool/pallas_call | solution.py:555
  175.4 1.1 pad_maximum_fusion
  176.4 23.1 %all_to_all.5 = bf16[128,32,128]{2,1,0:T(8,128)(2,1)S(1)} all-to-all(bf16[128,32,128]{2,1,0:T(8,128)(2,1)S(1)} %bitcast.26), channel_id=1, replica_groups=mesh['group'=8,'member'=16] {'group','member'}, dimensions={0} | all-to-all | bytes 2097152 | tf_op jit(solution)/shard_map/all_to_all | solution.py:577
  200.4 88.3 %scatter.1 = (f32[4096,128]{1,0:T(8,128)}, bf16[256,128]{1,0:T(8,128)(2,1)}, bf16[256,128]{1,0:T(8,128)(2,1)}, bf16[256,128]{1,0:T(8,128)(2,1)}, bf16[256,128]{1...) custom-call(s32[26,1,4096]{2,1,0:T(1,128)} %reshape.65.index_ref, ...), custom_call_target="tpu_custom_call" | custom-call | bytes 400000000 | tf_op jit(solution)/shard_map/scatter/pallas_call | solution.py:585
  289.4 2.2 collective-permute-start.22
  292.1 1.8 collective-permute-start.24
  294.1 1.3 collective-permute-done.22.refs_1_
  296.2 3.0 unpack.1
  299.3 2.1 collective-permute-done.27.refs_6_
  302.0 7.4 %finish.1 = f32[96,4096]{1,0:T(8,128)} custom-call(s32[1,1792]{1,0:T(1,128)} %bitcast.30, f32[4096,128]{1,0:T(8,128)} %get-tuple-element.112.local_ref, bf16[256,128]{1,0:T(8,128)(2,1)} %copy-done.11, bf16[256,128]{1,0:T(8,128)(2,1)} %copy-done.12, bf16[256,128]{1,0:T(8,128)(2,1)} %copy-done.13, bf16[256,128]{1,0:T(8,128)(2,1)} %copy-done.14, ...), custom_call_target="tpu_custom_call" | custom-call | tf_op jit(solution)/shard_map/finish/pallas_call | solution.py:615
  (127 shorter events, 12.9 us)
Async XLA Ops:
  7.2 289.1 %all-gather.2.cloned.1.call-start = ((), (), s32[]{:S(2)}) async-start(), calls=%async_computation.1 | async-start | bytes 2113536 | tf_op jit(solution)/shard_map/all_gather | solution.py:582
  13.3 12.2 %collective-permute-start = (bf16[272,128]{1,0:T(8,128)(2,1)}, bf16[272,128]{1,0:T(8,128)(2,1)S(1)}, u32[]{:S(2)}, u32[]{:S(2)}) collective-permute-start(bf16[272,128]{1,0:T(8,128)(2,1)} %get-tuple-element.68), channel_id=1, source_target_pairs={{0,1},{1,0},{2,3},{3,2},{4,5},{5,4},{6,7},{7,6},{8,9},{9,8},{10,11... | collective-permute-start | bytes 208904 | tf_op jit(solution)/shard_map/ppermute | solution.py:23
  14.9 12.6 %collective-permute-start.1 = (bf16[272,128]{1,0:T(8,128)(2,1)}, bf16[272,128]{1,0:T(8,128)(2,1)S(1)}, u32[]{:S(2)}, u32[]{:S(2)}) collective-permute-start(bf16[272,128]{1,0:T(8,128)(2,1)} %get-tuple-element.69), channel_id=1, source_target_pairs={{0,2},{1,3},{2,0},{3,1},{4,6},{5,7},{6,4},{7,5},{8,10},{9,11},{10,... | collective-permute-start | bytes 208904 | tf_op jit(solution)/shard_map/ppermute | solution.py:23
  17.7 25.9 %collective-permute-start.2 = (bf16[272,128]{1,0:T(8,128)(2,1)}, bf16[272,128]{1,0:T(8,128)(2,1)S(1)}, u32[]{:S(2)}, u32[]{:S(2)}) collective-permute-start(bf16[272,128]{1,0:T(8,128)(2,1)} %get-tuple-element.70), channel_id=1, source_target_pairs={{0,4},{1,5},{2,6},{3,7},{4,0},{5,1},{6,2},{7,3},{8,12},{9,13},{10,... | collective-permute-start | bytes 208904 | tf_op jit(solution)/shard_map/ppermute | solution.py:23
  19.6 24.0 %collective-permute-start.3 = (bf16[272,128]{1,0:T(8,128)(2,1)}, bf16[272,128]{1,0:T(8,128)(2,1)S(1)}, u32[]{:S(2)}, u32[]{:S(2)}) collective-permute-start(bf16[272,128]{1,0:T(8,128)(2,1)} %get-tuple-element.71), channel_id=1, source_target_pairs={{0,8},{1,9},{2,10},{3,11},{4,12},{5,13},{6,14},{7,15},{8,0},{9,1},... | collective-permute-start | bytes 208904 | tf_op jit(solution)/shard_map/ppermute | solution.py:23
  23.2 20.4 %collective-permute-start.4 = (bf16[272,128]{1,0:T(8,128)(2,1)}, bf16[272,128]{1,0:T(8,128)(2,1)S(1)}, u32[]{:S(2)}, u32[]{:S(2)}) collective-permute-start(bf16[272,128]{1,0:T(8,128)(2,1)} %get-tuple-element.72), channel_id=1, source_target_pairs={{0,16},{16,0},{32,48},{48,32},{64,80},{80,64},{96,112},{112,96},{1... | collective-permute-start | bytes 208904 | tf_op jit(solution)/shard_map/ppermute | solution.py:23
  25.9 17.7 %collective-permute-start.5 = (bf16[272,128]{1,0:T(8,128)(2,1)S(1)}, bf16[272,128]{1,0:T(8,128)(2,1)S(1)}, u32[]{:S(2)}, u32[]{:S(2)}) collective-permute-start(bf16[272,128]{1,0:T(8,128)(2,1)S(1)} %copy-done.33), channel_id=1, source_target_pairs={{0,32},{16,48},{32,0},{48,16},{64,96},{80,112},{96,64},{112,80},{1... | collective-permute-start | bytes 208904 | tf_op jit(solution)/shard_map/ppermute | solution.py:23
  27.5 16.1 %collective-permute-start.6 = (bf16[272,128]{1,0:T(8,128)(2,1)S(1)}, bf16[272,128]{1,0:T(8,128)(2,1)S(1)}, u32[]{:S(2)}, u32[]{:S(2)}) collective-permute-start(bf16[272,128]{1,0:T(8,128)(2,1)S(1)} %copy-done.32), channel_id=1, source_target_pairs={{0,64},{16,80},{32,96},{48,112},{64,0},{80,16},{96,32},{112,48},{1... | collective-permute-start | bytes 208904 | tf_op jit(solution)/shard_map/ppermute | solution.py:23
  47.4 4.1 %collective-permute-start.7 = (bf16[128,128]{1,0:T(8,128)(2,1)}, bf16[128,128]{1,0:T(8,128)(2,1)S(1)}, u32[]{:S(2)}, u32[]{:S(2)}) collective-permute-start(bf16[128,128]{1,0:T(8,128)(2,1)} %get-tuple-element.91), channel_id=1, source_target_pairs={{0,1},{1,0},{2,3},{3,2},{4,5},{5,4},{6,7},{7,6},{8,9},{9,8},{10,11... | collective-permute-start | bytes 98312 | tf_op jit(solution)/shard_map/ppermute | solution.py:23
  47.6 5.6 %collective-permute-start.8 = (bf16[128,128]{1,0:T(8,128)(2,1)}, bf16[128,128]{1,0:T(8,128)(2,1)S(1)}, u32[]{:S(2)}, u32[]{:S(2)}) collective-permute-start(bf16[128,128]{1,0:T(8,128)(2,1)} %get-tuple-element.92), channel_id=1, source_target_pairs={{0,2},{1,3},{2,0},{3,1},{4,6},{5,7},{6,4},{7,5},{8,10},{9,11},{10,... | collective-permute-start | bytes 98312 | tf_op jit(solution)/shard_map/ppermute | solution.py:23
  49.3 69.9 %collective-permute-start.9 = (bf16[128,128]{1,0:T(8,128)(2,1)}, bf16[128,128]{1,0:T(8,128)(2,1)S(1)}, u32[]{:S(2)}, u32[]{:S(2)}) collective-permute-start(bf16[128,128]{1,0:T(8,128)(2,1)} %get-tuple-element.93), channel_id=1, source_target_pairs={{0,4},{1,5},{2,6},{3,7},{4,0},{5,1},{6,2},{7,3},{8,12},{9,13},{10,... | collective-permute-start | bytes 98312 | tf_op jit(solution)/shard_map/ppermute | solution.py:23
  49.3 69.9 %collective-permute-start.10 = (bf16[128,128]{1,0:T(8,128)(2,1)}, bf16[128,128]{1,0:T(8,128)(2,1)S(1)}, u32[]{:S(2)}, u32[]{:S(2)}) collective-permute-start(bf16[128,128]{1,0:T(8,128)(2,1)} %get-tuple-element.94), channel_id=1, source_target_pairs={{0,8},{1,9},{2,10},{3,11},{4,12},{5,13},{6,14},{7,15},{8,0},{9,1},... | collective-permute-start | bytes 98312 | tf_op jit(solution)/shard_map/ppermute | solution.py:23
  50.1 69.1 %collective-permute-start.11 = (bf16[128,128]{1,0:T(8,128)(2,1)}, bf16[128,128]{1,0:T(8,128)(2,1)S(1)}, u32[]{:S(2)}, u32[]{:S(2)}) collective-permute-start(bf16[128,128]{1,0:T(8,128)(2,1)} %get-tuple-element.95), channel_id=1, source_target_pairs={{0,16},{16,0},{32,48},{48,32},{64,80},{80,64},{96,112},{112,96},{1... | collective-permute-start | bytes 98312 | tf_op jit(solution)/shard_map/ppermute | solution.py:23
  51.5 67.7 %copy-start.25 = (bf16[128,128]{1,0:T(8,128)(2,1)}, bf16[128,128]{1,0:T(8,128)(2,1)S(1)}, u32[]{:S(2)}) copy-start(bf16[128,128]{1,0:T(8,128)(2,1)S(1)} %collective-permute-done.7.refs_0_) | copy-start | bytes 98308
  51.5 67.8 %collective-permute-start.12 = (bf16[128,128]{1,0:T(8,128)(2,1)}, bf16[128,128]{1,0:T(8,128)(2,1)S(1)}, u32[]{:S(2)}, u32[]{:S(2)}) collective-permute-start(bf16[128,128]{1,0:T(8,128)(2,1)} %get-tuple-element.96), channel_id=1, source_target_pairs={{0,32},{16,48},{32,0},{48,16},{64,96},{80,112},{96,64},{112,80},{1... | collective-permute-start | bytes 98312 | tf_op jit(solution)/shard_map/ppermute | solution.py:23
  53.2 65.9 %copy-start.26 = (bf16[128,128]{1,0:T(8,128)(2,1)}, bf16[128,128]{1,0:T(8,128)(2,1)S(1)}, u32[]{:S(2)}) copy-start(bf16[128,128]{1,0:T(8,128)(2,1)S(1)} %collective-permute-done.8.refs_1_) | copy-start | bytes 98308
  53.3 66.0 %collective-permute-start.13 = (bf16[128,128]{1,0:T(8,128)(2,1)}, bf16[128,128]{1,0:T(8,128)(2,1)S(1)}, u32[]{:S(2)}, u32[]{:S(2)}) collective-permute-start(bf16[128,128]{1,0:T(8,128)(2,1)} %get-tuple-element.97), channel_id=1, source_target_pairs={{0,64},{16,80},{32,96},{48,112},{64,0},{80,16},{96,32},{112,48},{1... | collective-permute-start | bytes 98312 | tf_op jit(solution)/shard_map/ppermute | solution.py:23
  138.5 7.7 %collective-permute-start.14 = (bf16[128,128]{1,0:T(8,128)(2,1)}, bf16[128,128]{1,0:T(8,128)(2,1)S(1)}, u32[]{:S(2)}, u32[]{:S(2)}) collective-permute-start(bf16[128,128]{1,0:T(8,128)(2,1)} %get-tuple-element.99), channel_id=1, source_target_pairs={{0,1},{1,0},{2,3},{3,2},{4,5},{5,4},{6,7},{7,6},{8,9},{9,8},{10,11... | collective-permute-start | bytes 98312 | tf_op jit(solution)/shard_map/ppermute | solution.py:23
  140.4 6.3 %collective-permute-start.15 = (bf16[128,128]{1,0:T(8,128)(2,1)}, bf16[128,128]{1,0:T(8,128)(2,1)S(1)}, u32[]{:S(2)}, u32[]{:S(2)}) collective-permute-start(bf16[128,128]{1,0:T(8,128)(2,1)} %get-tuple-element.100), channel_id=1, source_target_pairs={{0,2},{1,3},{2,0},{3,1},{4,6},{5,7},{6,4},{7,5},{8,10},{9,11},{10,... | collective-permute-start | bytes 98312 | tf_op jit(solution)/shard_map/ppermute | solution.py:23
  141.4 24.0 %collective-permute-start.16 = (bf16[128,128]{1,0:T(8,128)(2,1)}, bf16[128,128]{1,0:T(8,128)(2,1)S(1)}, u32[]{:S(2)}, u32[]{:S(2)}) collective-permute-start(bf16[128,128]{1,0:T(8,128)(2,1)} %get-tuple-element.101), channel_id=1, source_target_pairs={{0,4},{1,5},{2,6},{3,7},{4,0},{5,1},{6,2},{7,3},{8,12},{9,13},{10,... | collective-permute-start | bytes 98312 | tf_op jit(solution)/shard_map/ppermute | solution.py:23
  142.1 23.3 %collective-permute-start.17 = (bf16[128,128]{1,0:T(8,128)(2,1)}, bf16[128,128]{1,0:T(8,128)(2,1)S(1)}, u32[]{:S(2)}, u32[]{:S(2)}) collective-permute-start(bf16[128,128]{1,0:T(8,128)(2,1)} %get-tuple-element.102), channel_id=1, source_target_pairs={{0,8},{1,9},{2,10},{3,11},{4,12},{5,13},{6,14},{7,15},{8,0},{9,1},... | collective-permute-start | bytes 98312 | tf_op jit(solution)/shard_map/ppermute | solution.py:23
  146.2 19.2 %collective-permute-start.18 = (bf16[128,128]{1,0:T(8,128)(2,1)}, bf16[128,128]{1,0:T(8,128)(2,1)S(1)}, u32[]{:S(2)}, u32[]{:S(2)}) collective-permute-start(bf16[128,128]{1,0:T(8,128)(2,1)} %get-tuple-element.103), channel_id=1, source_target_pairs={{0,16},{16,0},{32,48},{48,32},{64,80},{80,64},{96,112},{112,96},{1... | collective-permute-start | bytes 98312 | tf_op jit(solution)/shard_map/ppermute | solution.py:23
  146.2 19.1 %copy-start.18 = (bf16[128,128]{1,0:T(8,128)(2,1)}, bf16[128,128]{1,0:T(8,128)(2,1)S(1)}, u32[]{:S(2)}) copy-start(bf16[128,128]{1,0:T(8,128)(2,1)S(1)} %collective-permute-done.14.refs_0_) | copy-start | bytes 98308
  146.2 19.2 %collective-permute-start.19 = (bf16[128,128]{1,0:T(8,128)(2,1)}, bf16[128,128]{1,0:T(8,128)(2,1)S(1)}, u32[]{:S(2)}, u32[]{:S(2)}) collective-permute-start(bf16[128,128]{1,0:T(8,128)(2,1)} %get-tuple-element.104), channel_id=1, source_target_pairs={{0,32},{16,48},{32,0},{48,16},{64,96},{80,112},{96,64},{112,80},{1... | collective-permute-start | bytes 98312 | tf_op jit(solution)/shard_map/ppermute | solution.py:23
  146.7 18.7 %collective-permute-start.20 = (bf16[128,128]{1,0:T(8,128)(2,1)}, bf16[128,128]{1,0:T(8,128)(2,1)S(1)}, u32[]{:S(2)}, u32[]{:S(2)}) collective-permute-start(bf16[128,128]{1,0:T(8,128)(2,1)} %get-tuple-element.105), channel_id=1, source_target_pairs={{0,64},{16,80},{32,96},{48,112},{64,0},{80,16},{96,32},{112,48},{1... | collective-permute-start | bytes 98312 | tf_op jit(solution)/shard_map/ppermute | solution.py:23
  288.7 5.3 %collective-permute-start.21 = (bf16[256,128]{1,0:T(8,128)(2,1)}, bf16[256,128]{1,0:T(8,128)(2,1)S(1)}, u32[]{:S(2)}, u32[]{:S(2)}) collective-permute-start(bf16[256,128]{1,0:T(8,128)(2,1)} %get-tuple-element.113), channel_id=1, source_target_pairs={{0,1},{1,0},{2,3},{3,2},{4,5},{5,4},{6,7},{7,6},{8,9},{9,8},{10,11... | collective-permute-start | bytes 196616 | tf_op jit(solution)/shard_map/ppermute | solution.py:23
  289.4 6.0 %collective-permute-start.22 = (bf16[256,128]{1,0:T(8,128)(2,1)}, bf16[256,128]{1,0:T(8,128)(2,1)S(1)}, u32[]{:S(2)}, u32[]{:S(2)}) collective-permute-start(bf16[256,128]{1,0:T(8,128)(2,1)} %get-tuple-element.114), channel_id=1, source_target_pairs={{0,2},{1,3},{2,0},{3,1},{4,6},{5,7},{6,4},{7,5},{8,10},{9,11},{10,... | collective-permute-start | bytes 196616 | tf_op jit(solution)/shard_map/ppermute | solution.py:23
  291.6 7.6 %collective-permute-start.23 = (bf16[256,128]{1,0:T(8,128)(2,1)}, bf16[256,128]{1,0:T(8,128)(2,1)S(1)}, u32[]{:S(2)}, u32[]{:S(2)}) collective-permute-start(bf16[256,128]{1,0:T(8,128)(2,1)} %get-tuple-element.115), channel_id=1, source_target_pairs={{0,4},{1,5},{2,6},{3,7},{4,0},{5,1},{6,2},{7,3},{8,12},{9,13},{10,... | collective-permute-start | bytes 196616 | tf_op jit(solution)/shard_map/ppermute | solution.py:23
  292.1 7.1 %collective-permute-start.24 = (bf16[256,128]{1,0:T(8,128)(2,1)}, bf16[256,128]{1,0:T(8,128)(2,1)S(1)}, u32[]{:S(2)}, u32[]{:S(2)}) collective-permute-start(bf16[256,128]{1,0:T(8,128)(2,1)} %get-tuple-element.116), channel_id=1, source_target_pairs={{0,8},{1,9},{2,10},{3,11},{4,12},{5,13},{6,14},{7,15},{8,0},{9,1},... | collective-permute-start | bytes 196616 | tf_op jit(solution)/shard_map/ppermute | solution.py:23
  294.0 5.3 %collective-permute-start.25 = (bf16[256,128]{1,0:T(8,128)(2,1)}, bf16[256,128]{1,0:T(8,128)(2,1)S(1)}, u32[]{:S(2)}, u32[]{:S(2)}) collective-permute-start(bf16[256,128]{1,0:T(8,128)(2,1)} %get-tuple-element.117), channel_id=1, source_target_pairs={{0,16},{16,0},{32,48},{48,32},{64,80},{80,64},{96,112},{112,96},{1... | collective-permute-start | bytes 196616 | tf_op jit(solution)/shard_map/ppermute | solution.py:23
  294.0 5.3 %collective-permute-start.26 = (bf16[256,128]{1,0:T(8,128)(2,1)}, bf16[256,128]{1,0:T(8,128)(2,1)S(1)}, u32[]{:S(2)}, u32[]{:S(2)}) collective-permute-start(bf16[256,128]{1,0:T(8,128)(2,1)} %get-tuple-element.118), channel_id=1, source_target_pairs={{0,32},{16,48},{32,0},{48,16},{64,96},{80,112},{96,64},{112,80},{1... | collective-permute-start | bytes 196616 | tf_op jit(solution)/shard_map/ppermute | solution.py:23
  295.4 6.0 %collective-permute-start.27 = (bf16[256,128]{1,0:T(8,128)(2,1)}, bf16[256,128]{1,0:T(8,128)(2,1)S(1)}, u32[]{:S(2)}, u32[]{:S(2)}) collective-permute-start(bf16[256,128]{1,0:T(8,128)(2,1)} %get-tuple-element.119), channel_id=1, source_target_pairs={{0,64},{16,80},{32,96},{48,112},{64,0},{80,16},{96,32},{112,48},{1... | collective-permute-start | bytes 196616 | tf_op jit(solution)/shard_map/ppermute | solution.py:23
  (31 other events, 174.9 us)
Sparse Core Ops, SparseCore 0:
  200.5 60.7 all-gather.1

commit v6 on v5

--- a/solution.py
+++ b/solution.py
@@ -287,10 +287,8 @@
 def unpack_kernel(full_ref, weights_ref, down_ref):
     kvol, chans, _ = weights_ref.shape
     noct, c2, _ = down_ref.shape
-    centre = kvol // 2
     for k in range(kvol):
-        spot = kvol - 1 if k == centre else k - int(k > centre)
-        weights_ref[k] = full_ref[pl.ds(spot * chans, chans), :][:, :chans]
+        weights_ref[k] = full_ref[pl.ds(k * chans, chans), :][:, :chans]
     first = kvol * chans
     rest = LANES - chans
     for o in range(noct - 1):
@@ -355,14 +353,15 @@
     lanes = len(tables)
     k = pl.program_id(0)
     last = pl.num_programs(0) - 1
+    middle_k = weight_ref.shape[0] // 2
 
     def ready(base, offset, buf):
-        buf[...] = jnp.dot(grad_ref[pl.ds(base, chunk), :], weight_ref[offset], preferred_element_type=F32)
+        buf[...] = jnp.dot(grad_ref[pl.ds(base, chunk), :], weight_ref[offset + (offset >= middle_k).astype(I32)], preferred_element_type=F32)
 
     @pl.when(k == 0)
     def _():
         clear(tables)
-        ready(0, 0, buf0)
+        ready(0, jnp.int32(0), buf0)
 
     def step(base, parity, store, entry):
         buf = bufs[parity]
@@ -388,7 +387,7 @@
 
         def close(step, _):
             part = pl.ds(pl.multiple_of(step * chunk, chunk), chunk)
-            centre = jnp.dot(grad_ref[part, :], weight_ref[last + 1], preferred_element_type=F32)
+            centre = jnp.dot(grad_ref[part, :], weight_ref[middle_k], preferred_element_type=F32)
             local_ref[part, :] = total(part) + centre
             return 0
 
@@ -443,8 +442,7 @@
     middle_k = kvol // 2
     index = jnp.concatenate([kmap[:middle_k], kmap[middle_k + 1 :]], axis=0).reshape(kvol - 1, 1, vdev)
 
-    w_ordered = jnp.concatenate([w_sub[:middle_k], w_sub[middle_k + 1 :], w_sub[middle_k : middle_k + 1]], axis=0)
-    w_backward = jnp.pad(w_ordered, ((0, 0), (0, lane_pad), (0, lane_pad)))
+    w_backward = jnp.pad(w_sub, ((0, 0), (0, lane_pad), (0, lane_pad)))
     w_forward = w_backward.transpose(0, 2, 1).reshape(kvol * LANES, LANES)
     down_pad = jnp.pad(w_down, ((0, 0), (0, 0), (0, lane_pad)))
 
@@ -500,7 +498,9 @@
             vmem_full((vdev, LANES)),
         ]
         + [vmem_full((halo + 2 * SUB, LANES))] * levels,
-        out_specs=pl.BlockSpec((vdev, LANES), lambda k: (0, k)),
+        out_specs=pl.BlockSpec(
+            (vdev, LANES), lambda k: (0, jnp.where(k == kvol - 1, middle_k, k + (k >= middle_k).astype(I32)))
+        ),
         out_shape=shape((vdev, kvol * LANES), BF16),
         scratch_shapes=[pltpu.VMEM((table_rows, LANES), F32)]
         + [pltpu.VMEM((chunk, LANES), F32)] * 2

time: 317 us -> 316 us (level)
  transfers between devices with their start and end apart: 29 -> 29, of which waited for: 4 -> 3; matrix products, arithmetic and copies ran while one was open for 3% -> 2% of each run, Pallas kernels for 56% -> 57%
where the time goes in v6:
time: 316 us
  Pallas kernels  224 us (71%)
  starting transfers between devices  38.2 us (12%)
  blocking collectives  23.1 us (7%)
  between operations  14.5 us (5%)
  local copies, waits for them, and re-layouts  8.96 us (3%)
  waiting for transfers between devices  4.71 us (1%)
    pallas_call x1, Pallas kernels, shards(): pl.pallas_call(functools.partial(scatter_kernel, levels, halo, stages), g...  88.8 us
    pallas_call x1, Pallas kernels, shards(): pl.pallas_call(functools.partial(gather_kernel, levels, halo), grid=(kvol...  65.4 us
    ppermute x28, starting transfers between devices, from_partner(): return lax.ppermute(value, axis, pairs)  38.2 us
    all_to_all x1, blocking collectives, shards(): lax.all_to_all(packed.reshape(devices, share, LANES), both, split_axis=0,...  23.1 us
    pallas_call x1, Pallas kernels, shards(): pl.pallas_call(functools.partial(middle_kernel, levels), grid=(vdev // bl...  18.6 us
    pallas_call x1, Pallas kernels, shards(): pl.pallas_call(weights_kernel, grid=(kvol // group,), in_specs=[vmem_full...  14.5 us
    pallas_call x1, Pallas kernels, shards(): pl.pallas_call(functools.partial(pool_kernel, levels, chans), in_specs=[s...  9.33 us
    pallas_call x1, Pallas kernels, shards(): pl.pallas_call(functools.partial(finish_kernel, levels), in_specs=[smem_f...  7.41 us
  transfers between devices with their start and end apart: 29, of which 3 were waited for; matrix products, arithmetic and copies ran while one was open for 2% of the time, Pallas kernels for 57%

profile of v6, /device:TPU:0, one launch (start us, length us, event | category | flops | bytes accessed | tf_op | source)
XLA Modules:
  0.0 315.7 jit_solution(13401542503616721202)
XLA Ops:
  7.2 6.1 %prepare.1 = (bf16[272,128]{1,0:T(8,128)(2,1)}, bf16[272,128]{1,0:T(8,128)(2,1)}, bf16[272,128]{1,0:T(8,128)(2,1)}, bf16[272,128]{1,0:T(8,128)(2,1)}, bf16[272,1...) custom-call(s32[1]{0:T(128)} %bitcast.me_ref, ...), custom_call_target="tpu_custom_call" | custom-call | tf_op jit(solution)/shard_map/prepare/pallas_call | solution.py:449
  13.3 1.7 collective-permute-start
  15.0 2.7 collective-permute-start.1
  17.7 1.9 collective-permute-start.2
  19.6 3.6 %collective-permute-start.3 = (bf16[272,128]{1,0:T(8,128)(2,1)}, bf16[272,128]{1,0:T(8,128)(2,1)S(1)}, u32[]{:S(2)}, u32[]{:S(2)}) collective-permute-start(bf16[272,128]{1,0:T(8,128)(2,1)} %get-tuple-element.71), channel_id=1, source_target_pairs={{0,8},{1,9},{2,10},{3,11},{4,12},{5,13},{6,14},{7,15},{8,0},{9,1},... | collective-permute-start | bytes 208904 | tf_op jit(solution)/shard_map/ppermute | solution.py:23
  23.2 1.2 fusion.3
  24.5 1.7 collective-permute-start.5
  26.1 3.0 collective-permute-start.6
  29.1 1.3 fusion.2
  31.3 1.2 reshape.65.index_ref
  32.5 1.6 copy.14
  35.0 7.3 %parents.1 = (f32[4104,128]{1,0:T(8,128)}, f32[4096,128]{1,0:T(8,128)}) custom-call(s32[1,4096]{1,0:T(1,128)} %get-tuple-element.75.self_ref, bf16[512,192]{1,0:T(8,128)(2,1)} %bitcast.28, bf16[8,192,128]{2,1,0:T(8,128)(2,1)} %pad.9.weight_ref), custom_call_target="tpu_custom_call" | custom-call | tf_op jit(solution)/shard_map/parents/pallas_call | solution.py:466
  43.1 3.1 answer.1
  46.4 1.7 collective-permute-start.8
  48.1 2.2 collective-permute-start.10
  52.9 65.4 %gather.1.taken_ref = bf16[4096,3456]{1,0:T(8,128)(2,1)} custom-call(s32[26,1,4096]{2,1,0:T(1,128)} %reshape.65.index_ref, f32[4096,128]{1,0:T(8,128)} %get-tuple-element.87.local_ref, bf16[272,128]{1,0:T(8,128)(2,1)} %copy-done.4, bf16[272,128]{1,0:T(8,128)(2,1)} %copy-done.5, bf16[272,128]{1,0:T(8,128)(2,1)} %copy-done.6, bf16[272,128]{1,0:T(8,128)(2,1)} %copy-done.7, ...), custom_call_target="tpu_custom_call" | custom-call | bytes 300000000 | tf_op jit(solution)/shard_map/gather/pallas_call | solution.py:493
  119.1 18.6 %middle.1 = (bf16[4096,128]{1,0:T(8,128)(2,1)}, bf16[128,4096]{1,0:T(8,128)(2,1)}, f32[4096,128]{1,0:T(8,128)}, bf16[128,128]{1,0:T(8,128)(2,1)}, bf16[128,128]{...) custom-call(s32[1,896]{1,0:T(1,128)} %get-tuple-element.85.list_ref,, ...), custom_call_target="tpu_custom_call" | custom-call | bytes 40000000 | tf_op jit(solution)/shard_map/middle/pallas_call | solution.py:515
  137.7 1.6 collective-permute-start.14
  139.3 1.4 collective-permute-start.15
  141.0 4.1 %collective-permute-start.17 = (bf16[128,128]{1,0:T(8,128)(2,1)}, bf16[128,128]{1,0:T(8,128)(2,1)S(1)}, u32[]{:S(2)}, u32[]{:S(2)}) collective-permute-start(bf16[128,128]{1,0:T(8,128)(2,1)} %get-tuple-element.102), channel_id=1, source_target_pairs={{0,8},{1,9},{2,10},{3,11},{4,12},{5,13},{6,14},{7,15},{8,0},{9,1},... | collective-permute-start | bytes 98312 | tf_op jit(solution)/shard_map/ppermute | solution.py:23
  145.6 4.1 %collective-permute-start.20 = (bf16[128,128]{1,0:T(8,128)(2,1)}, bf16[128,128]{1,0:T(8,128)(2,1)S(1)}, u32[]{:S(2)}, u32[]{:S(2)}) collective-permute-start(bf16[128,128]{1,0:T(8,128)(2,1)} %get-tuple-element.105), channel_id=1, source_target_pairs={{0,64},{16,80},{32,96},{48,112},{64,0},{80,16},{96,32},{112,48},{1... | collective-permute-start | bytes 98312 | tf_op jit(solution)/shard_map/ppermute | solution.py:23
  149.7 14.5 %weights.1 = bf16[2592,128]{1,0:T(8,128)(2,1)} custom-call(bf16[128,4096]{1,0:T(8,128)(2,1)} %get-tuple-element.107.turned_ref, bf16[4096,3456]{1,0:T(8,128)(2,1)} %gather.1.taken_ref), custom_call_target="tpu_custom_call" | custom-call | bytes 40000000 | tf_op jit(solution)/shard_map/weights/pallas_call | solution.py:544
  164.9 9.3 %pool.1 = (bf16[192,512]{1,0:T(8,128)(2,1)}, bf16[1504,128]{1,0:T(8,128)(2,1)}) custom-call(s32[1,896]{1,0:T(1,128)} %fusion.1.keys_ref, s32[1,4096]{1,0:T(1,128)} %get-tuple-element.75.self_ref, f32[4096,128]{1,0:T(8,128)} %get-tuple-element.98.act_ref, bf16[192,512]{1,0:T(8,128)(2,1)} %grad_ref.1, bf16[8,192,128]{2,1,0:T(8,128)(2,1)} %pad.9.weight_ref, ...), custom_call_target="tpu_custom_call" | custom-call | tf_op jit(solution)/shard_map/pool/pallas_call | solution.py:555
  174.3 1.1 pad_maximum_fusion
  175.3 23.1 %all_to_all.5 = bf16[128,32,128]{2,1,0:T(8,128)(2,1)S(1)} all-to-all(bf16[128,32,128]{2,1,0:T(8,128)(2,1)S(1)} %bitcast.26), channel_id=1, replica_groups=mesh['group'=8,'member'=16] {'group','member'}, dimensions={0} | all-to-all | bytes 2097152 | tf_op jit(solution)/shard_map/all_to_all | solution.py:577
  199.3 88.8 %scatter.1 = (f32[4096,128]{1,0:T(8,128)}, bf16[256,128]{1,0:T(8,128)(2,1)}, bf16[256,128]{1,0:T(8,128)(2,1)}, bf16[256,128]{1,0:T(8,128)(2,1)}, bf16[256,128]{1...) custom-call(s32[26,1,4096]{2,1,0:T(1,128)} %reshape.65.index_ref, ...), custom_call_target="tpu_custom_call" | custom-call | bytes 400000000 | tf_op jit(solution)/shard_map/scatter/pallas_call | solution.py:585
  288.9 1.9 collective-permute-start.22
  291.4 1.8 collective-permute-start.24
  293.3 1.5 collective-permute-done.22.refs_1_
  295.6 3.0 unpack.1
  298.6 2.2 collective-permute-done.27.refs_6_
  301.4 7.4 %finish.1 = f32[96,4096]{1,0:T(8,128)} custom-call(s32[1,1792]{1,0:T(1,128)} %bitcast.30, f32[4096,128]{1,0:T(8,128)} %get-tuple-element.112.local_ref, bf16[256,128]{1,0:T(8,128)(2,1)} %copy-done.11, bf16[256,128]{1,0:T(8,128)(2,1)} %copy-done.12, bf16[256,128]{1,0:T(8,128)(2,1)} %copy-done.13, bf16[256,128]{1,0:T(8,128)(2,1)} %copy-done.14, ...), custom_call_target="tpu_custom_call" | custom-call | tf_op jit(solution)/shard_map/finish/pallas_call | solution.py:615
  (124 shorter events, 11.1 us)
Async XLA Ops:
  7.2 21.9 %copy-start.2 = (bf16[27,96,96]{2,1,0:T(8,128)(2,1)S(1)}, bf16[27,96,96]{2,1,0:T(8,128)(2,1)}, u32[]{:S(2)}) copy-start(bf16[27,96,96]{2,1,0:T(8,128)(2,1)} %param.12) | copy-start | bytes 1492996
  7.2 288.4 %all-gather.2.cloned.1.call-start = ((), (), s32[]{:S(2)}) async-start(), calls=%async_computation.1 | async-start | bytes 2113536 | tf_op jit(solution)/shard_map/all_gather | solution.py:582
  13.3 11.1 %collective-permute-start = (bf16[272,128]{1,0:T(8,128)(2,1)}, bf16[272,128]{1,0:T(8,128)(2,1)S(1)}, u32[]{:S(2)}, u32[]{:S(2)}) collective-permute-start(bf16[272,128]{1,0:T(8,128)(2,1)} %get-tuple-element.68), channel_id=1, source_target_pairs={{0,1},{1,0},{2,3},{3,2},{4,5},{5,4},{6,7},{7,6},{8,9},{9,8},{10,11... | collective-permute-start | bytes 208904 | tf_op jit(solution)/shard_map/ppermute | solution.py:23
  15.0 11.1 %collective-permute-start.1 = (bf16[272,128]{1,0:T(8,128)(2,1)}, bf16[272,128]{1,0:T(8,128)(2,1)S(1)}, u32[]{:S(2)}, u32[]{:S(2)}) collective-permute-start(bf16[272,128]{1,0:T(8,128)(2,1)} %get-tuple-element.69), channel_id=1, source_target_pairs={{0,2},{1,3},{2,0},{3,1},{4,6},{5,7},{6,4},{7,5},{8,10},{9,11},{10,... | collective-permute-start | bytes 208904 | tf_op jit(solution)/shard_map/ppermute | solution.py:23
  17.7 24.6 %collective-permute-start.2 = (bf16[272,128]{1,0:T(8,128)(2,1)}, bf16[272,128]{1,0:T(8,128)(2,1)S(1)}, u32[]{:S(2)}, u32[]{:S(2)}) collective-permute-start(bf16[272,128]{1,0:T(8,128)(2,1)} %get-tuple-element.70), channel_id=1, source_target_pairs={{0,4},{1,5},{2,6},{3,7},{4,0},{5,1},{6,2},{7,3},{8,12},{9,13},{10,... | collective-permute-start | bytes 208904 | tf_op jit(solution)/shard_map/ppermute | solution.py:23
  19.6 22.7 %collective-permute-start.3 = (bf16[272,128]{1,0:T(8,128)(2,1)}, bf16[272,128]{1,0:T(8,128)(2,1)S(1)}, u32[]{:S(2)}, u32[]{:S(2)}) collective-permute-start(bf16[272,128]{1,0:T(8,128)(2,1)} %get-tuple-element.71), channel_id=1, source_target_pairs={{0,8},{1,9},{2,10},{3,11},{4,12},{5,13},{6,14},{7,15},{8,0},{9,1},... | collective-permute-start | bytes 208904 | tf_op jit(solution)/shard_map/ppermute | solution.py:23
  23.2 19.1 %collective-permute-start.4 = (bf16[272,128]{1,0:T(8,128)(2,1)}, bf16[272,128]{1,0:T(8,128)(2,1)S(1)}, u32[]{:S(2)}, u32[]{:S(2)}) collective-permute-start(bf16[272,128]{1,0:T(8,128)(2,1)} %get-tuple-element.72), channel_id=1, source_target_pairs={{0,16},{16,0},{32,48},{48,32},{64,80},{80,64},{96,112},{112,96},{1... | collective-permute-start | bytes 208904 | tf_op jit(solution)/shard_map/ppermute | solution.py:23
  24.5 17.9 %collective-permute-start.5 = (bf16[272,128]{1,0:T(8,128)(2,1)S(1)}, bf16[272,128]{1,0:T(8,128)(2,1)S(1)}, u32[]{:S(2)}, u32[]{:S(2)}) collective-permute-start(bf16[272,128]{1,0:T(8,128)(2,1)S(1)} %copy-done.33), channel_id=1, source_target_pairs={{0,32},{16,48},{32,0},{48,16},{64,96},{80,112},{96,64},{112,80},{1... | collective-permute-start | bytes 208904 | tf_op jit(solution)/shard_map/ppermute | solution.py:23
  26.1 16.2 %collective-permute-start.6 = (bf16[272,128]{1,0:T(8,128)(2,1)S(1)}, bf16[272,128]{1,0:T(8,128)(2,1)S(1)}, u32[]{:S(2)}, u32[]{:S(2)}) collective-permute-start(bf16[272,128]{1,0:T(8,128)(2,1)S(1)} %copy-done.32), channel_id=1, source_target_pairs={{0,64},{16,80},{32,96},{48,112},{64,0},{80,16},{96,32},{112,48},{1... | collective-permute-start | bytes 208904 | tf_op jit(solution)/shard_map/ppermute | solution.py:23
  46.1 4.2 %collective-permute-start.7 = (bf16[128,128]{1,0:T(8,128)(2,1)}, bf16[128,128]{1,0:T(8,128)(2,1)S(1)}, u32[]{:S(2)}, u32[]{:S(2)}) collective-permute-start(bf16[128,128]{1,0:T(8,128)(2,1)} %get-tuple-element.91), channel_id=1, source_target_pairs={{0,1},{1,0},{2,3},{3,2},{4,5},{5,4},{6,7},{7,6},{8,9},{9,8},{10,11... | collective-permute-start | bytes 98312 | tf_op jit(solution)/shard_map/ppermute | solution.py:23
  46.4 5.6 %collective-permute-start.8 = (bf16[128,128]{1,0:T(8,128)(2,1)}, bf16[128,128]{1,0:T(8,128)(2,1)S(1)}, u32[]{:S(2)}, u32[]{:S(2)}) collective-permute-start(bf16[128,128]{1,0:T(8,128)(2,1)} %get-tuple-element.92), channel_id=1, source_target_pairs={{0,2},{1,3},{2,0},{3,1},{4,6},{5,7},{6,4},{7,5},{8,10},{9,11},{10,... | collective-permute-start | bytes 98312 | tf_op jit(solution)/shard_map/ppermute | solution.py:23
  48.1 70.3 %collective-permute-start.9 = (bf16[128,128]{1,0:T(8,128)(2,1)}, bf16[128,128]{1,0:T(8,128)(2,1)S(1)}, u32[]{:S(2)}, u32[]{:S(2)}) collective-permute-start(bf16[128,128]{1,0:T(8,128)(2,1)} %get-tuple-element.93), channel_id=1, source_target_pairs={{0,4},{1,5},{2,6},{3,7},{4,0},{5,1},{6,2},{7,3},{8,12},{9,13},{10,... | collective-permute-start | bytes 98312 | tf_op jit(solution)/shard_map/ppermute | solution.py:23
  48.1 70.4 %collective-permute-start.10 = (bf16[128,128]{1,0:T(8,128)(2,1)}, bf16[128,128]{1,0:T(8,128)(2,1)S(1)}, u32[]{:S(2)}, u32[]{:S(2)}) collective-permute-start(bf16[128,128]{1,0:T(8,128)(2,1)} %get-tuple-element.94), channel_id=1, source_target_pairs={{0,8},{1,9},{2,10},{3,11},{4,12},{5,13},{6,14},{7,15},{8,0},{9,1},... | collective-permute-start | bytes 98312 | tf_op jit(solution)/shard_map/ppermute | solution.py:23
  50.3 68.2 %collective-permute-start.11 = (bf16[128,128]{1,0:T(8,128)(2,1)}, bf16[128,128]{1,0:T(8,128)(2,1)S(1)}, u32[]{:S(2)}, u32[]{:S(2)}) collective-permute-start(bf16[128,128]{1,0:T(8,128)(2,1)} %get-tuple-element.95), channel_id=1, source_target_pairs={{0,16},{16,0},{32,48},{48,32},{64,80},{80,64},{96,112},{112,96},{1... | collective-permute-start | bytes 98312 | tf_op jit(solution)/shard_map/ppermute | solution.py:23
  50.3 68.1 %copy-start.25 = (bf16[128,128]{1,0:T(8,128)(2,1)}, bf16[128,128]{1,0:T(8,128)(2,1)S(1)}, u32[]{:S(2)}) copy-start(bf16[128,128]{1,0:T(8,128)(2,1)S(1)} %collective-permute-done.7.refs_0_) | copy-start | bytes 98308
  50.3 68.2 %collective-permute-start.12 = (bf16[128,128]{1,0:T(8,128)(2,1)}, bf16[128,128]{1,0:T(8,128)(2,1)S(1)}, u32[]{:S(2)}, u32[]{:S(2)}) collective-permute-start(bf16[128,128]{1,0:T(8,128)(2,1)} %get-tuple-element.96), channel_id=1, source_target_pairs={{0,32},{16,48},{32,0},{48,16},{64,96},{80,112},{96,64},{112,80},{1... | collective-permute-start | bytes 98312 | tf_op jit(solution)/shard_map/ppermute | solution.py:23
  52.0 66.4 %copy-start.26 = (bf16[128,128]{1,0:T(8,128)(2,1)}, bf16[128,128]{1,0:T(8,128)(2,1)S(1)}, u32[]{:S(2)}) copy-start(bf16[128,128]{1,0:T(8,128)(2,1)S(1)} %collective-permute-done.8.refs_1_) | copy-start | bytes 98308
  52.0 66.5 %collective-permute-start.13 = (bf16[128,128]{1,0:T(8,128)(2,1)}, bf16[128,128]{1,0:T(8,128)(2,1)S(1)}, u32[]{:S(2)}, u32[]{:S(2)}) collective-permute-start(bf16[128,128]{1,0:T(8,128)(2,1)} %get-tuple-element.97), channel_id=1, source_target_pairs={{0,64},{16,80},{32,96},{48,112},{64,0},{80,16},{96,32},{112,48},{1... | collective-permute-start | bytes 98312 | tf_op jit(solution)/shard_map/ppermute | solution.py:23
  137.7 7.4 %collective-permute-start.14 = (bf16[128,128]{1,0:T(8,128)(2,1)}, bf16[128,128]{1,0:T(8,128)(2,1)S(1)}, u32[]{:S(2)}, u32[]{:S(2)}) collective-permute-start(bf16[128,128]{1,0:T(8,128)(2,1)} %get-tuple-element.99), channel_id=1, source_target_pairs={{0,1},{1,0},{2,3},{3,2},{4,5},{5,4},{6,7},{7,6},{8,9},{9,8},{10,11... | collective-permute-start | bytes 98312 | tf_op jit(solution)/shard_map/ppermute | solution.py:23
  139.3 6.3 %collective-permute-start.15 = (bf16[128,128]{1,0:T(8,128)(2,1)}, bf16[128,128]{1,0:T(8,128)(2,1)S(1)}, u32[]{:S(2)}, u32[]{:S(2)}) collective-permute-start(bf16[128,128]{1,0:T(8,128)(2,1)} %get-tuple-element.100), channel_id=1, source_target_pairs={{0,2},{1,3},{2,0},{3,1},{4,6},{5,7},{6,4},{7,5},{8,10},{9,11},{10,... | collective-permute-start | bytes 98312 | tf_op jit(solution)/shard_map/ppermute | solution.py:23
  140.7 23.5 %collective-permute-start.16 = (bf16[128,128]{1,0:T(8,128)(2,1)}, bf16[128,128]{1,0:T(8,128)(2,1)S(1)}, u32[]{:S(2)}, u32[]{:S(2)}) collective-permute-start(bf16[128,128]{1,0:T(8,128)(2,1)} %get-tuple-element.101), channel_id=1, source_target_pairs={{0,4},{1,5},{2,6},{3,7},{4,0},{5,1},{6,2},{7,3},{8,12},{9,13},{10,... | collective-permute-start | bytes 98312 | tf_op jit(solution)/shard_map/ppermute | solution.py:23
  141.0 23.3 %collective-permute-start.17 = (bf16[128,128]{1,0:T(8,128)(2,1)}, bf16[128,128]{1,0:T(8,128)(2,1)S(1)}, u32[]{:S(2)}, u32[]{:S(2)}) collective-permute-start(bf16[128,128]{1,0:T(8,128)(2,1)} %get-tuple-element.102), channel_id=1, source_target_pairs={{0,8},{1,9},{2,10},{3,11},{4,12},{5,13},{6,14},{7,15},{8,0},{9,1},... | collective-permute-start | bytes 98312 | tf_op jit(solution)/shard_map/ppermute | solution.py:23
  145.1 19.1 %collective-permute-start.18 = (bf16[128,128]{1,0:T(8,128)(2,1)}, bf16[128,128]{1,0:T(8,128)(2,1)S(1)}, u32[]{:S(2)}, u32[]{:S(2)}) collective-permute-start(bf16[128,128]{1,0:T(8,128)(2,1)} %get-tuple-element.103), channel_id=1, source_target_pairs={{0,16},{16,0},{32,48},{48,32},{64,80},{80,64},{96,112},{112,96},{1... | collective-permute-start | bytes 98312 | tf_op jit(solution)/shard_map/ppermute | solution.py:23
  145.1 19.2 %collective-permute-start.19 = (bf16[128,128]{1,0:T(8,128)(2,1)}, bf16[128,128]{1,0:T(8,128)(2,1)S(1)}, u32[]{:S(2)}, u32[]{:S(2)}) collective-permute-start(bf16[128,128]{1,0:T(8,128)(2,1)} %get-tuple-element.104), channel_id=1, source_target_pairs={{0,32},{16,48},{32,0},{48,16},{64,96},{80,112},{96,64},{112,80},{1... | collective-permute-start | bytes 98312 | tf_op jit(solution)/shard_map/ppermute | solution.py:23
  145.6 18.7 %collective-permute-start.20 = (bf16[128,128]{1,0:T(8,128)(2,1)}, bf16[128,128]{1,0:T(8,128)(2,1)S(1)}, u32[]{:S(2)}, u32[]{:S(2)}) collective-permute-start(bf16[128,128]{1,0:T(8,128)(2,1)} %get-tuple-element.105), channel_id=1, source_target_pairs={{0,64},{16,80},{32,96},{48,112},{64,0},{80,16},{96,32},{112,48},{1... | collective-permute-start | bytes 98312 | tf_op jit(solution)/shard_map/ppermute | solution.py:23
  288.1 5.1 %collective-permute-start.21 = (bf16[256,128]{1,0:T(8,128)(2,1)}, bf16[256,128]{1,0:T(8,128)(2,1)S(1)}, u32[]{:S(2)}, u32[]{:S(2)}) collective-permute-start(bf16[256,128]{1,0:T(8,128)(2,1)} %get-tuple-element.113), channel_id=1, source_target_pairs={{0,1},{1,0},{2,3},{3,2},{4,5},{5,4},{6,7},{7,6},{8,9},{9,8},{10,11... | collective-permute-start | bytes 196616 | tf_op jit(solution)/shard_map/ppermute | solution.py:23
  288.9 6.0 %collective-permute-start.22 = (bf16[256,128]{1,0:T(8,128)(2,1)}, bf16[256,128]{1,0:T(8,128)(2,1)S(1)}, u32[]{:S(2)}, u32[]{:S(2)}) collective-permute-start(bf16[256,128]{1,0:T(8,128)(2,1)} %get-tuple-element.114), channel_id=1, source_target_pairs={{0,2},{1,3},{2,0},{3,1},{4,6},{5,7},{6,4},{7,5},{8,10},{9,11},{10,... | collective-permute-start | bytes 196616 | tf_op jit(solution)/shard_map/ppermute | solution.py:23
  290.7 7.9 %collective-permute-start.23 = (bf16[256,128]{1,0:T(8,128)(2,1)}, bf16[256,128]{1,0:T(8,128)(2,1)S(1)}, u32[]{:S(2)}, u32[]{:S(2)}) collective-permute-start(bf16[256,128]{1,0:T(8,128)(2,1)} %get-tuple-element.115), channel_id=1, source_target_pairs={{0,4},{1,5},{2,6},{3,7},{4,0},{5,1},{6,2},{7,3},{8,12},{9,13},{10,... | collective-permute-start | bytes 196616 | tf_op jit(solution)/shard_map/ppermute | solution.py:23
  291.4 7.2 %collective-permute-start.24 = (bf16[256,128]{1,0:T(8,128)(2,1)}, bf16[256,128]{1,0:T(8,128)(2,1)S(1)}, u32[]{:S(2)}, u32[]{:S(2)}) collective-permute-start(bf16[256,128]{1,0:T(8,128)(2,1)} %get-tuple-element.116), channel_id=1, source_target_pairs={{0,8},{1,9},{2,10},{3,11},{4,12},{5,13},{6,14},{7,15},{8,0},{9,1},... | collective-permute-start | bytes 196616 | tf_op jit(solution)/shard_map/ppermute | solution.py:23
  293.2 5.4 %collective-permute-start.25 = (bf16[256,128]{1,0:T(8,128)(2,1)}, bf16[256,128]{1,0:T(8,128)(2,1)S(1)}, u32[]{:S(2)}, u32[]{:S(2)}) collective-permute-start(bf16[256,128]{1,0:T(8,128)(2,1)} %get-tuple-element.117), channel_id=1, source_target_pairs={{0,16},{16,0},{32,48},{48,32},{64,80},{80,64},{96,112},{112,96},{1... | collective-permute-start | bytes 196616 | tf_op jit(solution)/shard_map/ppermute | solution.py:23
  293.2 5.4 %collective-permute-start.26 = (bf16[256,128]{1,0:T(8,128)(2,1)}, bf16[256,128]{1,0:T(8,128)(2,1)S(1)}, u32[]{:S(2)}, u32[]{:S(2)}) collective-permute-start(bf16[256,128]{1,0:T(8,128)(2,1)} %get-tuple-element.118), channel_id=1, source_target_pairs={{0,32},{16,48},{32,0},{48,16},{64,96},{80,112},{96,64},{112,80},{1... | collective-permute-start | bytes 196616 | tf_op jit(solution)/shard_map/ppermute | solution.py:23
  294.9 6.0 %collective-permute-start.27 = (bf16[256,128]{1,0:T(8,128)(2,1)}, bf16[256,128]{1,0:T(8,128)(2,1)S(1)}, u32[]{:S(2)}, u32[]{:S(2)}) collective-permute-start(bf16[256,128]{1,0:T(8,128)(2,1)} %get-tuple-element.119), channel_id=1, source_target_pairs={{0,64},{16,80},{32,96},{48,112},{64,0},{80,16},{96,32},{112,48},{1... | collective-permute-start | bytes 196616 | tf_op jit(solution)/shard_map/ppermute | solution.py:23
  (31 other events, 199.2 us)
Sparse Core Ops, SparseCore 0:
  199.4 60.7 all-gather.1
